TPU v7x, 32 devices: a whole 2x2x4 slice. The times are simulated.
32 devices in a mesh: dp: 8 (over y, x, core), tensor: 4 (over z).
Axes of the slice: x: 2, y: 2, z: 4, core: 2. Of those that a mesh axis runs over, the one named last changes fastest.
Arguments:
- char_inputs: bfloat16 [131072, 256], P(('dp', 'tensor')), may hold values from -6 to 6
- char_counts: int32 [8192], P(('dp', 'tensor')), may hold values from 1 to 16
- doc_ids: int32 [8, 1024], P('dp'), may hold values from 0 to 3, never falling along the last dimension, each value on 1 to 512 neighbouring positions
- cotangent: bfloat16 [8192, 512], P('dp'), may hold values from -6 to 6
- char_norm_one: float32 [256], replicated, may hold values from 0.5 to 1.5
- char_query: bfloat16 [256, 256], replicated, may hold values from -0.375 to 0.375
- char_key: bfloat16 [256, 256], replicated, may hold values from -0.375 to 0.375
- char_value: bfloat16 [256, 256], replicated, may hold values from -0.375 to 0.375
- char_out: bfloat16 [256, 256], replicated, may hold values from -0.75 to 0.75
- char_norm_two: float32 [256], replicated, may hold values from 0.5 to 1.5
- char_up: bfloat16 [256, 1024], replicated, may hold values from -0.375 to 0.375
- char_down: bfloat16 [1024, 256], replicated, may hold values from -0.1875 to 0.1875
- char_proj: bfloat16 [256, 512], replicated, may hold values from -1.5 to 1.5
- word_norm_one: float32 [512], replicated, may hold values from 0.5 to 1.5
- word_query: bfloat16 [512, 512], P(None, 'tensor'), may hold values from -0.25 to 0.25
- word_key: bfloat16 [512, 512], P(None, 'tensor'), may hold values from -0.25 to 0.25
- word_value: bfloat16 [512, 512], P(None, 'tensor'), may hold values from -0.25 to 0.25
- word_out_proj: bfloat16 [512, 512], P('tensor'), may hold values from -1 to 1
- word_norm_two: float32 [512], replicated, may hold values from 0.5 to 1.5
- word_up: bfloat16 [512, 2048], P(None, 'tensor'), may hold values from -0.25 to 0.25
- word_down: bfloat16 [2048, 512], P('tensor'), may hold values from -0.125 to 0.125
Outputs:
- word_output: bfloat16 [8192, 512], P(('dp', 'tensor'))
- char_input_gradient: float32 [131072, 256], P(('dp', 'tensor'))
- char_norm_one_gradient: float32 [256], replicated
- char_query_gradient: float32 [256, 256], replicated
- char_key_gradient: float32 [256, 256], replicated
- char_value_gradient: float32 [256, 256], replicated
- char_out_gradient: float32 [256, 256], replicated
- char_norm_two_gradient: float32 [256], replicated
- char_up_gradient: float32 [256, 1024], replicated
- char_down_gradient: float32 [1024, 256], replicated
- char_proj_gradient: float32 [256, 512], replicated
- word_norm_one_gradient: float32 [512], replicated
- word_query_gradient: float32 [512, 512], P(None, 'tensor')
- word_key_gradient: float32 [512, 512], P(None, 'tensor')
- word_value_gradient: float32 [512, 512], P(None, 'tensor')
- word_out_proj_gradient: float32 [512, 512], P('tensor')
- word_norm_two_gradient: float32 [512], replicated
- word_up_gradient: float32 [512, 2048], P(None, 'tensor')
- word_down_gradient: float32 [2048, 512], P('tensor')
Inputs may be any that keep to these rules, and one draw needn't show every extreme that they name: Slots of a word from char_counts on are padding. `doc_ids`: ids never fall along a sequence; each document covers 1 to 512 consecutive words, one exactly that many.
All inputs are finite; a program needn't handle non-finite values.
Results may differ from a plain program's by a relative error of at most 0.018.
Values may be sent and summed in bfloat16 or wider, within the bound.
A program may use at most 192 MiB of HBM per device.

v0:
```python
import jax
import jax.numpy as jnp
from jax import lax
from jax.sharding import PartitionSpec as P

HD = 64
CHEADS = 4
CHD = 64


EPSILON = 1e-05
NEG_LARGE = -1e30


def layer_norm(values, gain_vector):
    centre = values - jnp.mean(values, axis=-1, keepdims=True)
    spread = jnp.mean(centre * centre, axis=-1, keepdims=True)
    return centre * lax.rsqrt(spread + EPSILON) * gain_vector


def gelu_tanh(values):
    return jax.nn.gelu(values, approximate=True)


def matmul(left, right):
    return jnp.dot(left, right, preferred_element_type=jnp.float32)


def contract_rows(left, right):
    return lax.dot_general(
        left, right, (((0,), (0,)), ((), ())), preferred_element_type=jnp.float32
    )


def contract_cols(left, right):
    return lax.dot_general(
        left, right, (((1,), (1,)), ((), ())), preferred_element_type=jnp.float32
    )


def block_mask(seq_docs, first_row, block_rows):
    length = seq_docs.shape[0]
    block_docs = lax.dynamic_slice_in_dim(seq_docs, first_row, block_rows, 0)
    row_ids = first_row + jnp.arange(block_rows)
    key_ids = jnp.arange(length)
    return (block_docs[:, None] == seq_docs[None, :]) & (key_ids[None, :] <= row_ids[:, None])


def attention_forward(queries, key_rows, value_rows, doc_ids, block_rows):
    length = queries.shape[1]
    score_scale = queries.shape[3] ** (-0.5)
    block_count = length // block_rows

    def sequence_pass(members):
        seq_q, seq_k, seq_v, seq_docs = members

        def block_pass(block_index):
            first_row = block_index * block_rows
            block_q = lax.dynamic_slice_in_dim(seq_q, first_row, block_rows, 0)
            allowed = block_mask(seq_docs, first_row, block_rows)
            scores = (
                jnp.einsum("qhd,khd->hqk", block_q, seq_k, preferred_element_type=jnp.float32)
                * score_scale
            )
            scores = jnp.where(allowed[None], scores, NEG_LARGE)
            row_max = jnp.max(scores, axis=-1, keepdims=True)
            exponent = jnp.exp(scores - row_max)
            row_total = jnp.sum(exponent, axis=-1, keepdims=True)
            weights_low = (exponent / row_total).astype(jnp.bfloat16)
            mixed_rows = jnp.einsum(
                "hqk,khd->qhd", weights_low, seq_v, preferred_element_type=jnp.float32
            ).astype(jnp.bfloat16)
            return (mixed_rows, (row_max + jnp.log(row_total))[..., 0])

        mixed_rows, log_totals = lax.map(block_pass, jnp.arange(block_count))
        return (mixed_rows.reshape(seq_q.shape), log_totals)

    return lax.map(sequence_pass, (queries, key_rows, value_rows, doc_ids))


def attention_backward(queries, key_rows, value_rows, doc_ids, log_totals, grad_mixed, block_rows):
    length = queries.shape[1]
    score_scale = queries.shape[3] ** (-0.5)
    block_count = length // block_rows

    def sequence_pass(members):
        seq_q, seq_k, seq_v, seq_docs, seq_logs, seq_grad = members

        def block_pass(carried, block_index):
            key_acc, value_acc = carried
            first_row = block_index * block_rows
            block_q = lax.dynamic_slice_in_dim(seq_q, first_row, block_rows, 0)
            block_grad = lax.dynamic_slice_in_dim(seq_grad, first_row, block_rows, 0)
            allowed = block_mask(seq_docs, first_row, block_rows)
            scores = (
                jnp.einsum("qhd,khd->hqk", block_q, seq_k, preferred_element_type=jnp.float32)
                * score_scale
            )
            scores = jnp.where(allowed[None], scores, NEG_LARGE)
            weights_full = jnp.exp(scores - seq_logs[block_index][..., None])
            weights_low = weights_full.astype(jnp.bfloat16)
            value_acc = value_acc + jnp.einsum(
                "hqk,qhd->khd", weights_low, block_grad, preferred_element_type=jnp.float32
            )
            grad_weights = jnp.einsum(
                "qhd,khd->hqk", block_grad, seq_v, preferred_element_type=jnp.float32
            )
            inner_sum = jnp.sum(weights_full * grad_weights, axis=-1, keepdims=True)
            grad_scores = (weights_full * (grad_weights - inner_sum)).astype(jnp.bfloat16)
            grad_block_q = (
                jnp.einsum("hqk,khd->qhd", grad_scores, seq_k, preferred_element_type=jnp.float32)
                * score_scale
            ).astype(jnp.bfloat16)
            key_acc = (
                key_acc
                + jnp.einsum(
                    "hqk,qhd->khd", grad_scores, block_q, preferred_element_type=jnp.float32
                )
                * score_scale
            )
            return ((key_acc, value_acc), grad_block_q)

        zero_rows = jnp.zeros(seq_k.shape, jnp.float32)
        (key_acc, value_acc), grad_q = lax.scan(
            block_pass, (zero_rows, zero_rows), jnp.arange(block_count)
        )
        return (
            grad_q.reshape(seq_q.shape),
            key_acc.astype(jnp.bfloat16),
            value_acc.astype(jnp.bfloat16),
        )

    return lax.map(sequence_pass, (queries, key_rows, value_rows, doc_ids, log_totals, grad_mixed))


def per_device(
    char_inputs,
    char_counts,
    doc_ids,
    cotangent,
    char_norm_one,
    char_query,
    char_key,
    char_value,
    char_out,
    char_norm_two,
    char_up,
    char_down,
    char_proj,
    word_norm_one,
    word_query,
    word_key,
    word_value,
    word_out_proj,
    word_norm_two,
    word_up,
    word_down,
):
    word_count = char_counts.shape[0]
    slot_count = char_inputs.shape[0] // word_count
    char_width = char_inputs.shape[1]
    shape_four = (word_count, slot_count, CHEADS, CHD)
    char_scale = CHD ** (-0.5)
    tensor_rank = lax.axis_index("tensor")
    base_rows = char_inputs.astype(jnp.float32)
    char_normed, pull_char_one = jax.vjp(layer_norm, base_rows, char_norm_one)
    char_normed = char_normed.astype(jnp.bfloat16)
    char_q = matmul(char_normed, char_query).astype(jnp.bfloat16).reshape(shape_four)
    char_k = matmul(char_normed, char_key).astype(jnp.bfloat16).reshape(shape_four)
    char_v = matmul(char_normed, char_value).astype(jnp.bfloat16).reshape(shape_four)
    char_scores = (
        jnp.einsum("wqhd,wkhd->whqk", char_q, char_k, preferred_element_type=jnp.float32)
        * char_scale
    )
    slot_valid = jnp.arange(slot_count)[None, :] < char_counts[:, None]
    char_scores = jnp.where(slot_valid[:, None, None, :], char_scores, NEG_LARGE)
    char_probs = jax.nn.softmax(char_scores, axis=-1)
    char_probs_low = char_probs.astype(jnp.bfloat16)
    char_mixed = jnp.einsum(
        "whqk,wkhd->wqhd", char_probs_low, char_v, preferred_element_type=jnp.float32
    )
    char_mixed = char_mixed.astype(jnp.bfloat16).reshape(word_count * slot_count, char_width)
    char_first = base_rows + matmul(char_mixed, char_out)
    char_normed_two, pull_char_two = jax.vjp(layer_norm, char_first, char_norm_two)
    char_normed_two = char_normed_two.astype(jnp.bfloat16)
    char_hidden, pull_char_gelu = jax.vjp(gelu_tanh, matmul(char_normed_two, char_up))
    char_hidden = char_hidden.astype(jnp.bfloat16)
    char_second = char_first + matmul(char_hidden, char_down)
    slot_weights = slot_valid.astype(jnp.float32) / char_counts.astype(jnp.float32)[:, None]
    pooled = jnp.sum(
        char_second.reshape(word_count, slot_count, char_width) * slot_weights[:, :, None], axis=1
    )
    pooled = pooled.astype(jnp.bfloat16)
    word_vectors = matmul(pooled, char_proj).astype(jnp.bfloat16)
    input_whole = lax.all_gather(word_vectors, "tensor", axis=0, tiled=True).astype(jnp.float32)
    normed_whole, pull_first = jax.vjp(layer_norm, input_whole, word_norm_one)
    normed = normed_whole.astype(jnp.bfloat16)
    sequences = doc_ids.shape[0]
    seq_len = doc_ids.shape[1]
    token_count = sequences * seq_len
    head_count = word_query.shape[1] // HD
    shape_heads = (sequences, seq_len, head_count, HD)
    block_rows = min(512, seq_len)
    queries = matmul(normed, word_query).astype(jnp.bfloat16).reshape(shape_heads)
    key_rows = matmul(normed, word_key).astype(jnp.bfloat16).reshape(shape_heads)
    value_rows = matmul(normed, word_value).astype(jnp.bfloat16).reshape(shape_heads)
    mixed_heads, log_totals = attention_forward(queries, key_rows, value_rows, doc_ids, block_rows)
    mixed_flat = mixed_heads.reshape(token_count, head_count * HD)
    attention_part = matmul(mixed_flat, word_out_proj)
    middle = input_whole + lax.psum(attention_part.astype(jnp.bfloat16), "tensor").astype(
        jnp.float32
    )
    normed_mid, pull_mid = jax.vjp(layer_norm, middle, word_norm_two)
    normed_mid = normed_mid.astype(jnp.bfloat16)
    hidden, pull_gelu = jax.vjp(gelu_tanh, matmul(normed_mid, word_up))
    hidden = hidden.astype(jnp.bfloat16)
    feedforward_part = matmul(hidden, word_down)
    full_output = middle + lax.psum(feedforward_part.astype(jnp.bfloat16), "tensor").astype(
        jnp.float32
    )
    word_output = lax.dynamic_slice_in_dim(full_output, tensor_rank * word_count, word_count, 0)
    word_output = word_output.astype(jnp.bfloat16)
    grad_down = contract_rows(hidden, cotangent)
    grad_pre = pull_gelu(contract_cols(cotangent, word_down))[0].astype(jnp.bfloat16)
    grad_up = contract_rows(normed_mid, grad_pre)
    mid_part = contract_cols(grad_pre, word_up)
    cotangent_full = cotangent.astype(jnp.float32)
    back_mid, grad_gain_two = pull_mid(
        lax.psum(mid_part.astype(jnp.bfloat16), "tensor").astype(jnp.float32)
    )
    grad_middle = cotangent_full + back_mid
    grad_middle_low = grad_middle.astype(jnp.bfloat16)
    grad_out_proj = contract_rows(mixed_flat, grad_middle_low)
    grad_mixed = (
        contract_cols(grad_middle_low, word_out_proj).astype(jnp.bfloat16).reshape(shape_heads)
    )
    grad_q, grad_k, grad_v = attention_backward(
        queries, key_rows, value_rows, doc_ids, log_totals, grad_mixed, block_rows
    )
    flat_shape = (token_count, head_count * HD)
    grad_q = grad_q.reshape(flat_shape)
    grad_k = grad_k.reshape(flat_shape)
    grad_v = grad_v.reshape(flat_shape)
    grad_query = contract_rows(normed, grad_q)
    grad_key = contract_rows(normed, grad_k)
    grad_value = contract_rows(normed, grad_v)
    first_part = (
        contract_cols(grad_q, word_query)
        + contract_cols(grad_k, word_key)
        + contract_cols(grad_v, word_value)
    )
    back_first, grad_gain_one = pull_first(
        lax.psum(first_part.astype(jnp.bfloat16), "tensor").astype(jnp.float32)
    )
    grad_input = lax.dynamic_slice_in_dim(
        grad_middle + back_first, tensor_rank * word_count, word_count, 0
    )
    gain_share = (tensor_rank == 0).astype(jnp.float32)
    grad_vectors = grad_input.astype(jnp.bfloat16)
    grad_proj = contract_rows(pooled, grad_vectors)
    grad_pooled = contract_cols(grad_vectors, char_proj)
    grad_second = (grad_pooled[:, None, :] * slot_weights[:, :, None]).reshape(
        word_count * slot_count, char_width
    )
    second_low = grad_second.astype(jnp.bfloat16)
    grad_char_down = contract_rows(char_hidden, second_low)
    grad_char_pre = pull_char_gelu(contract_cols(second_low, char_down))[0].astype(jnp.bfloat16)
    grad_char_up = contract_rows(char_normed_two, grad_char_pre)
    back_char_two, grad_char_gain_two = pull_char_two(contract_cols(grad_char_pre, char_up))
    grad_first = grad_second + back_char_two
    first_low = grad_first.astype(jnp.bfloat16)
    grad_char_out = contract_rows(char_mixed, first_low)
    grad_char_mixed = contract_cols(first_low, char_out).astype(jnp.bfloat16).reshape(shape_four)
    grad_char_probs = jnp.einsum(
        "wqhd,wkhd->whqk", grad_char_mixed, char_v, preferred_element_type=jnp.float32
    )
    char_inner = jnp.sum(char_probs * grad_char_probs, axis=-1, keepdims=True)
    grad_char_scores = (char_probs * (grad_char_probs - char_inner)).astype(jnp.bfloat16)
    flat_chars = (word_count * slot_count, char_width)
    grad_cv = jnp.einsum(
        "whqk,wqhd->wkhd", char_probs_low, grad_char_mixed, preferred_element_type=jnp.float32
    )
    grad_cv = grad_cv.astype(jnp.bfloat16).reshape(flat_chars)
    grad_cq = jnp.einsum(
        "whqk,wkhd->wqhd", grad_char_scores, char_k, preferred_element_type=jnp.float32
    )
    grad_cq = (grad_cq * char_scale).astype(jnp.bfloat16).reshape(flat_chars)
    grad_ck = jnp.einsum(
        "whqk,wqhd->wkhd", grad_char_scores, char_q, preferred_element_type=jnp.float32
    )
    grad_ck = (grad_ck * char_scale).astype(jnp.bfloat16).reshape(flat_chars)
    grad_char_query = contract_rows(char_normed, grad_cq)
    grad_char_key = contract_rows(char_normed, grad_ck)
    grad_char_value = contract_rows(char_normed, grad_cv)
    back_char_one, grad_char_gain_one = pull_char_one(
        contract_cols(grad_cq, char_query)
        + contract_cols(grad_ck, char_key)
        + contract_cols(grad_cv, char_value)
    )
    char_input_gradient = grad_first + back_char_one
    word_sums = lax.psum(
        (grad_query, grad_key, grad_value, grad_out_proj, grad_up, grad_down), "dp"
    )
    char_sums = lax.psum(
        (
            grad_char_gain_one,
            grad_char_query,
            grad_char_key,
            grad_char_value,
            grad_char_out,
            grad_char_gain_two,
            grad_char_up,
            grad_char_down,
            grad_proj,
            grad_gain_one * gain_share,
            grad_gain_two * gain_share,
        ),
        ("dp", "tensor"),
    )
    return (
        word_output,
        char_input_gradient,
        char_sums[0],
        char_sums[1],
        char_sums[2],
        char_sums[3],
        char_sums[4],
        char_sums[5],
        char_sums[6],
        char_sums[7],
        char_sums[8],
        char_sums[9],
        word_sums[0],
        word_sums[1],
        word_sums[2],
        word_sums[3],
        char_sums[10],
        word_sums[4],
        word_sums[5],
    )


def solution(mesh):
    in_specs = (
        P(("dp", "tensor"), None),
        P(("dp", "tensor")),
        P("dp", None),
        P("dp", None),
        P(),
        P(),
        P(),
        P(),
        P(),
        P(),
        P(),
        P(),
        P(),
        P(),
        P(None, "tensor"),
        P(None, "tensor"),
        P(None, "tensor"),
        P("tensor", None),
        P(),
        P(None, "tensor"),
        P("tensor", None),
    )
    out_specs = (
        P(("dp", "tensor"), None),
        P(("dp", "tensor"), None),
        P(),
        P(),
        P(),
        P(),
        P(),
        P(),
        P(),
        P(),
        P(),
        P(),
        P(None, "tensor"),
        P(None, "tensor"),
        P(None, "tensor"),
        P("tensor", None),
        P(),
        P(None, "tensor"),
        P("tensor", None),
    )
    return jax.shard_map(
        per_device, mesh=mesh, in_specs=in_specs, out_specs=out_specs, check_vma=False
    )
```

profile of v0, /device:TPU:0, one launch (start us, length us, event | category | flops | bytes accessed | tf_op | source)
XLA Modules:
  0.0 727.4 jit_solution(17585414568510393199)
XLA Ops:
  20.2 7.1 reshape.407
  30.9 7.1 reshape.406
  41.6 7.1 reshape.405
  48.7 5.8 fusion.75
  54.5 28.7 %fusion.134 = (f32[256,4,16]{2,1,0:T(4,128)S(1)}, f32[256,4,16,16]{2,3,1,0:T(8,128)S(1)}) fusion(f32[256,4,16,16]{2,3,1,0:T(8,128)S(1)} %fusion.75, pred[256,16]{1,0:T(8,128)(4,1)S(1)} %iota_compare_fusion.2), kind=kOutput, calls=%fused_computation.213 | output fusion | flops 1572879 | bytes 2166784 | tf_op jit(solution)/shard_map/sub | solution.py:177
  94.9 7.0 reshape.408
  106.4 9.7 %multiply_convert_fusion.1 = (bf16[4096,1024]{1,0:T(8,128)(2,1)S(1)}, f32[4096,1024]{1,0:T(8,128)}) fusion(bf16[256,1024]{1,0:T(8,128)(2,1)S(1)} %copy-done, f32[4096,256]{1,0:T(8,128)S(1)} %get-tuple-element.291, f32[256]{0:T(256)S(1)} %copy-done.97, f32[4096]{0:T(1024)S(1)} %fusion.121, f32[4096]{0:T(1024)S(1)} %broadcast_multiply_fusion), kind=kOutput, calls=%fused_computation.59 | convolution fusion | flops 2189426688 | bytes 29918208 | tf_op jit(solution)/shard_map/dot_general | solution.py:26
  120.4 30.8 %all-gather.2.cloned.1.call-done = bf16[1024,512]{1,0:T(8,128)(2,1)} async-done(((bf16[256,512]{1,0:T(8,128)(2,1)}), bf16[1024,512]{1,0:T(8,128)(2,1)}) %all-gather.2.cloned.1.call-update) | async-done | bytes 1048592 | tf_op jit(solution)/shard_map/all_gather | solution.py:195
  159.0 16.5 %while.47 = (s32[]{:T(128)}, bf16[2,512,2,64]{1,3,2,0:T(8,128)(2,1)S(1)}, f32[2,2,512]{2,1,0:T(2,128)}, s32[2]{0:T(128)S(1)}, s32[1024]{0:T(1024)S(1)}, /*index=...) while((s32[]{:T(128)}, ...), condition=%wide.region_12.13_spmd, body=%wide.region_9.12_spmd.sunk | while | flops 282656256 | bytes 15513803 | solution.py:75
  182.4 47.9 %all-reduce.10.cloned.1.call-done = bf16[1024,512]{1,0:T(8,128)(2,1)} async-done(((bf16[1024,512]{1,0:T(8,128)(2,1)}), bf16[1024,512]{1,0:T(8,128)(2,1)}) %all-reduce.10.cloned.1.call-update) | async-done | bytes 1048592 | tf_op jit(solution)/shard_map/psum | solution.py:210
  243.6 47.8 %all-reduce.12.cloned.1.call-done = bf16[1024,512]{1,0:T(8,128)(2,1)} async-done(((bf16[1024,512]{1,0:T(8,128)(2,1)}), bf16[1024,512]{1,0:T(8,128)(2,1)}) %all-reduce.12.cloned.1.call-update) | async-done | bytes 1048592 | tf_op jit(solution)/shard_map/psum | solution.py:229
  302.9 28.6 %while.48 = (s32[]{:T(128)}, f32[1024,2,64]{0,2,1:T(8,128)S(1)}, f32[1024,2,64]{0,2,1:T(8,128)}, bf16[2,512,2,64]{1,3,2,0:T(8,128)(2,1)}, s32[2]{0:T(128)S(1)}, ...) while((s32[]{:T(128)}, f32[1024,2,64]{0,2,1:T(8,128)S(1)}, ...), condition=%wide.region_22.23_spmd.clone, body=%wide.region_20.22_spmd.clone.sunk | while | flops 689176064 | bytes 44476844 | solution.py:124
  348.0 75.0 %all-reduce.18.cloned.1.call-done = (bf16[1024,512]{1,0:T(8,128)(2,1)}, bf16[1024,512]{1,0:T(8,128)(2,1)}) async-done(((bf16[1024,512]{1,0:T(8,128)(2,1)}, bf16[1024,512]{1,0:T(8,128)(2,1)}), (bf16[1024,512]{1,0:T(8,128)(2,1)}, bf16[1024,512]{1,0:T(8,128)(2,1)})) %all-reduce.18.cloned.1.call-update) | async-done | bytes 2097168 | tf_op jit(solution)/shard_map/psum | solution.py:218
  431.7 15.4 %fusion.47 = bf16[4096,1024]{1,0:T(8,128)(2,1)S(1)} fusion(f32[4096,1024]{1,0:T(8,128)} %get-tuple-element.293, bf16[4096,256]{1,0:T(8,128)(2,1)S(1)} %fusion.62, bf16[1024,256]{1,0:T(8,128)(2,1)S(1)} %copy-done.54), kind=kOutput, calls=%fused_computation.58 | convolution fusion | flops 2231369728 | bytes 27787264 | tf_op jit(solution)/shard_map/dot_general | solution.py:36
  462.4 9.0 %convert_bitcast_fusion = bf16[256,16,4,64]{3,1,2,0:T(8,128)(2,1)} fusion(bf16[256,16,4,64]{3,2,1,0:T(4,128)(2,1)} %reshape.414, f32[256,4,16,16]{2,3,1,0:T(8,128)} %copy-done.21, f32[256,4,16]{2,1,0:T(4,128)S(1)} %copy-done.56), kind=kOutput, calls=%fused_computation.96 | convolution fusion | flops 35127296 | bytes 5308416 | tf_op jit(solution)/shard_map/whqk,wqhd->wkhd/dot_general | solution.py:280
  471.4 12.3 %multiply_reduce_fusion.1 = (f32[256,4,16]{2,1,0:T(4,128)S(1)}, f32[256,4,16,16]{2,3,1,0:T(8,128)}) fusion(f32[256,4,16,16]{2,3,1,0:T(8,128)} %copy-done.21, f32[256,4,16]{2,1,0:T(4,128)S(1)} %copy-done.56, bf16[256,16,4,64]{3,2,1,0:T(4,128)(2,1)} %reshape.405, bf16[256,16,4,64]{3,2,1,0:T(4,128)(2,1)} %reshape.414), kind=kOutput, calls=%fused_computation.63 | convolution fusion | flops 34324480 | bytes 6422528 | tf_op jit(solution)/shard_map/wqhd,wkhd->whqk/dot_general | solution.py:274
  483.7 7.6 %multiply_convert_fusion.4 = bf16[256,4,16,16]{2,3,1,0:T(8,128)(2,1)S(1)} fusion(f32[256,4,16,16]{2,3,1,0:T(8,128)} %get-tuple-element.298, f32[256,4,16]{2,1,0:T(4,128)S(1)} %get-tuple-element.297, f32[256,4,16,16]{2,3,1,0:T(8,128)} %copy-done.21, f32[256,4,16]{2,1,0:T(4,128)S(1)} %copy-done.56), kind=kLoop, calls=%fused_computation.62 | loop fusion | flops 1048576 | bytes 2752512 | tf_op jit(solution)/shard_map/convert_element_type | solution.py:278
  502.1 7.1 reshape.415
  520.0 7.0 reshape.417
  534.3 7.2 reshape.416
  553.9 7.5 %fusion.130 = f32[256,1024]{1,0:T(8,128)} fusion(bf16[4096,1024]{1,0:T(8,128)(2,1)} %copy-done.101, f32[4096,256]{1,0:T(8,128)S(1)} %copy-done.8, f32[256]{0:T(256)S(1)} %copy-done.98, f32[4096]{0:T(1024)S(1)} %copy-done.83, f32[4096]{0:T(1024)S(1)} %copy-done.75), kind=kOutput, calls=%fused_computation.209 | convolution fusion | flops 2151677952 | bytes 13665280 | tf_op jit(solution)/shard_map/dot_general | solution.py:30
  570.3 5.9 add_add_fusion.2
  576.2 40.0 %all-reduce = (f32[256]{0:T(256)}, f32[256]{0:T(256)}, f32[512]{0:T(512)}, f32[512]{0:T(512)}) all-reduce(f32[256]{0:T(256)S(1)} %get-tuple-element.215, f32[256]{0:T(256)S(1)} %get-tuple-element.213, f32[512]{0:T(512)S(1)} %get-tuple-element.302, f32[512]{0:T(512)S(1)} %get-tuple-element.301), channel_id=1, replica_groups=mesh['dp'=8,'tensor'=4] {'dp','tensor'}, use_global_device_ids=true, to_apply=%region_32.33 | all-reduce | flops 1536 | bytes 12288 | tf_op jit(solution)/shard_map/psum | solution.py:304
  618.0 86.2 %all-reduce.14.cloned.1.call-done = (f32[256,256]{1,0:T(8,128)}, f32[256,256]{1,0:T(8,128)}, f32[256,256]{1,0:T(8,128)}, f32[256,256]{1,0:T(8,128)}, f32[256,102...) async-done(((f32[256,256]{1,0:T(8,128)}, f32[256,256]{1,0:T(8,128)}, f32[256,256]{1,0:T(8,128)}, f32[256,256]{1,0:T(8,128)}, f32[256,1024]{1,0:T(8,128)}, ...) | async-done | bytes 3670032 | tf_op jit(solution)/shard_map/psum | solution.py:304
  (385 shorter events, 225.5 us)
Async XLA Ops:
  7.2 99.2 %copy-start = (bf16[256,1024]{1,0:T(8,128)(2,1)S(1)}, bf16[256,1024]{1,0:T(8,128)(2,1)}, u32[]{:S(2)}) copy-start(bf16[256,1024]{1,0:T(8,128)(2,1)} %param.35) | copy-start | bytes 1572868
  7.2 144.0 %all-gather.2.cloned.1.call-start = ((), (), s32[]{:S(2)}) async-start(), calls=%async_computation | async-start | bytes 1310720 | tf_op jit(solution)/shard_map/all_gather | solution.py:195
  14.5 101.6 %copy-start.34 = (f32[256,16]{1,0:T(8,128)}, f32[256,16]{1,0:T(8,128)S(1)}, u32[]{:S(2)}) copy-start(f32[256,16]{1,0:T(8,128)S(1)} %convert_divide_fusion) | copy-start | bytes 49156
  116.1 38.3 %copy-start.90 = (f32[512]{0:T(512)S(1)}, f32[512]{0:T(512)}, u32[]{:S(2)}) copy-start(f32[512]{0:T(512)} %param.38) | copy-start | bytes 6148
  119.4 36.7 %copy-start.66 = (bf16[512,128]{1,0:T(8,128)(2,1)S(1)}, bf16[512,128]{1,0:T(8,128)(2,1)}, u32[]{:S(2)}) copy-start(bf16[512,128]{1,0:T(8,128)(2,1)} %param.41) | copy-start | bytes 393220
  119.4 37.9 %copy-start.63 = (bf16[512,128]{1,0:T(8,128)(2,1)S(1)}, bf16[512,128]{1,0:T(8,128)(2,1)}, u32[]{:S(2)}) copy-start(bf16[512,128]{1,0:T(8,128)(2,1)} %param.40) | copy-start | bytes 393220
  119.4 38.4 %copy-start.64 = (bf16[512,128]{1,0:T(8,128)(2,1)S(1)}, bf16[512,128]{1,0:T(8,128)(2,1)}, u32[]{:S(2)}) copy-start(bf16[512,128]{1,0:T(8,128)(2,1)} %param.39) | copy-start | bytes 393220
  120.3 109.9 %all-reduce.10.cloned.1.call-start = ((), (), s32[]{:S(2)}) async-start(), calls=%async_computation.1 | async-start | bytes 2097152 | tf_op jit(solution)/shard_map/psum | solution.py:210
  120.4 38.6 %copy-start.44 = (s32[1,1024]{1,0:T(1,128)S(1)}, s32[1,1024]{1,0:T(1,128)}, u32[]{:S(2)}) copy-start(s32[1,1024]{1,0:T(1,128)} %param.27) | copy-start | bytes 12292
  175.5 54.8 %copy-start.1 = (bf16[1024,512]{1,0:T(8,128)(2,1)S(1)}, bf16[1024,512]{1,0:T(8,128)(2,1)}, u32[]{:S(2)}) copy-start(bf16[1024,512]{1,0:T(8,128)(2,1)} %all-gather.2.cloned.1.call-done) | copy-start | bytes 3145732
  178.8 54.9 %copy-start.88 = (f32[512]{0:T(512)S(1)}, f32[512]{0:T(512)}, u32[]{:S(2)}) copy-start(f32[512]{0:T(512)} %param.43) | copy-start | bytes 6148
  178.9 112.5 %all-reduce.12.cloned.1.call-start = ((), (), s32[]{:S(2)}) async-start(), calls=%async_computation.2 | async-start | bytes 2097152 | tf_op jit(solution)/shard_map/psum | solution.py:229
  240.1 182.9 %all-reduce.18.cloned.1.call-start = ((), (), s32[]{:S(2)}) async-start(), calls=%async_computation.5 | async-start | bytes 4194304 | tf_op jit(solution)/shard_map/psum | solution.py:218
  337.4 280.6 %all-reduce.16.cloned.1.call-start = ((), (), s32[]{:S(2)}) async-start(), calls=%async_computation.4 | async-start | bytes 6291456 | tf_op jit(solution)/shard_map/psum | solution.py:301
  344.1 78.9 %copy-start.81 = (f32[1024]{0:T(1024)S(1)}, f32[1024]{0:T(1024)}, u32[]{:S(2)}) copy-start(f32[1024]{0:T(1024)} %copy-done.80) | copy-start | bytes 12292
  344.1 78.9 %copy-start.85 = (f32[1024]{0:T(1024)S(1)}, f32[1024]{0:T(1024)}, u32[]{:S(2)}) copy-start(f32[1024]{0:T(1024)} %copy-done.84) | copy-start | bytes 12292
  344.1 78.9 %copy-start.91 = (f32[512]{0:T(512)S(1)}, f32[512]{0:T(512)}, u32[]{:S(2)}) copy-start(f32[512]{0:T(512)} %param.38) | copy-start | bytes 6148
  346.5 79.6 %copy-start.87 = (f32[1024]{0:T(1024)S(1)}, f32[1024]{0:T(1024)}, u32[]{:S(2)}) copy-start(f32[1024]{0:T(1024)} %copy-done.86) | copy-start | bytes 12292
  347.5 82.1 %copy-start.37 = (bf16[256,512]{1,0:T(8,128)(2,1)S(1)}, bf16[256,512]{1,0:T(8,128)(2,1)}, u32[]{:S(2)}) copy-start(bf16[256,512]{1,0:T(8,128)(2,1)} %param.37) | copy-start | bytes 786436
  347.6 356.7 %all-reduce.14.cloned.1.call-start = ((), (), s32[]{:S(2)}) async-start(), calls=%async_computation.3 | async-start | bytes 7340032 | tf_op jit(solution)/shard_map/psum | solution.py:304
  431.6 15.5 %copy-start.23 = (bf16[4096,256]{1,0:T(8,128)(2,1)}, bf16[4096,256]{1,0:T(8,128)(2,1)S(1)}, u32[]{:S(2)}) copy-start(bf16[4096,256]{1,0:T(8,128)(2,1)S(1)} %fusion.62) | copy-start | bytes 6291460
  431.7 15.5 %copy-start.7 = (f32[4096,256]{1,0:T(8,128)S(1)}, f32[4096,256]{1,0:T(8,128)}, u32[]{:S(2)}) copy-start(f32[4096,256]{1,0:T(8,128)} %copy-done.6) | copy-start | bytes 12582916
  618.0 97.3 %copy-start.71 = (f32[512,128]{1,0:T(8,128)S(1)}, f32[512,128]{1,0:T(8,128)}, u32[]{:S(2)}) copy-start(f32[512,128]{1,0:T(8,128)} %get-tuple-element.523) | copy-start | bytes 786436
  618.0 98.1 %copy-start.70 = (f32[512,128]{1,0:T(8,128)S(1)}, f32[512,128]{1,0:T(8,128)}, u32[]{:S(2)}) copy-start(f32[512,128]{1,0:T(8,128)} %get-tuple-element.524) | copy-start | bytes 786436
  (92 other events, 477.1 us)
Sparse Core Ops, SparseCore 0:
  120.5 30.7 all-gather.1
  179.0 51.2 all-reduce.9
  240.2 51.1 all-reduce.11
  337.5 85.4 all-reduce.17
  428.0 69.0 all-reduce.15
  561.5 142.6 all-reduce.13
where the time goes:
time: 738 us; the launch traced here: 727 us
  waiting for transfers between devices  288 us (39%)
  matrix products  176 us (24%)
  local copies, waits for them, and re-layouts  106 us (14%)
  other arithmetic  94.4 us (13%)
  blocking collectives  40 us (5%)
  between operations  15.8 us (2%)
    psum x1, waiting for transfers between devices, per_device(): lax.psum((grad_char_gain_one, grad_char_query, grad_char_key, grad_char_v...  86.2 us
    psum x1, waiting for transfers between devices, per_device(): lax.psum(feedforward_part.astype(jnp.bfloat16), 'tensor')  75 us
    psum x1, waiting for transfers between devices, per_device(): lax.psum(attention_part.astype(jnp.bfloat16), 'tensor').astype(jnp.float32)  47.9 us
    psum x1, waiting for transfers between devices, per_device(): lax.psum(mid_part.astype(jnp.bfloat16), 'tensor').astype(jnp.float32)  47.8 us
    dot_general x13, matrix products, contract_cols(): lax.dot_general(left, right, (((1,), (1,)), ((), ())), preferred_element_...  43 us
    psum x1, blocking collectives, per_device(): lax.psum((grad_char_gain_one, grad_char_query, grad_char_key, grad_char_v...  40 us
    dot_general x13, matrix products, matmul(): return jnp.dot(left, right, preferred_element_type=jnp.float32)  37.2 us
    dot_general x13, matrix products, contract_rows(): lax.dot_general(left, right, (((0,), (0,)), ((), ())), preferred_element_...  32.8 us
  transfers between devices with their start and end apart: 6, of which 5 were waited for; matrix products, arithmetic and copies ran while one was open for 23% of the time, Pallas kernels for 0%

commit v1 on v0

--- a/solution.py
+++ b/solution.py
@@ -1,15 +1,328 @@
+import functools
+
 import jax
 import jax.numpy as jnp
 from jax import lax
+from jax.experimental import pallas as pl
+from jax.experimental.pallas import tpu as pltpu
+
 from jax.sharding import PartitionSpec as P
 
-HD = 64
+BF = jnp.bfloat16
+F32 = jnp.float32
+EPSILON = 1e-05
+NEG_LARGE = -1e30
 CHEADS = 4
 CHD = 64
-
-
-EPSILON = 1e-05
-NEG_LARGE = -1e30
+TILE = 128
+CSTEP = 512
+GELU_C = 0.7978845608028654
+GELU_A = 0.044715
+
+
+def nn(left, right):
+    return lax.dot_general(left, right, (((1,), (0,)), ((), ())), preferred_element_type=F32)
+
+
+def nt(left, right):
+    return lax.dot_general(left, right, (((1,), (1,)), ((), ())), preferred_element_type=F32)
+
+
+def tn(left, right):
+    return lax.dot_general(left, right, (((0,), (0,)), ((), ())), preferred_element_type=F32)
+
+
+def norm_parts(values):
+    centre = values - jnp.mean(values, axis=-1, keepdims=True)
+    spread = jnp.mean(centre * centre, axis=-1, keepdims=True)
+    rate = lax.rsqrt(spread + EPSILON)
+    return centre * rate, rate
+
+
+def norm_back(upstream, gain, unit, rate):
+    scaled = upstream * gain
+    first = jnp.mean(scaled, axis=-1, keepdims=True)
+    second = jnp.mean(scaled * unit, axis=-1, keepdims=True)
+    return rate * (scaled - first - unit * second)
+
+
+def gelu_parts(values):
+    square = values * values
+    inner = values * (GELU_C + (GELU_C * GELU_A) * square)
+    half = 0.5 + 0.5 * jnp.tanh(inner)
+    active = values * half
+    slope = half + (active * (1.0 - half)) * (2.0 * GELU_C + (6.0 * GELU_C * GELU_A) * square)
+    return active, slope
+
+
+def split_heads(pair):
+    low_half = lax.broadcasted_iota(jnp.int32, pair.shape, 1) < CHD
+    zero = jnp.zeros_like(pair)
+    return jnp.concatenate([jnp.where(low_half, pair, zero), jnp.where(low_half, zero, pair)], axis=0)
+
+
+def word_of_lane(shape, slots):
+    lane = lax.broadcasted_iota(jnp.int32, shape, 1)
+    return jnp.bitwise_and(lane, TILE - 1) // slots
+
+
+def compact(scores, slots):
+    words = word_of_lane((slots, scores.shape[1]), slots)
+    result = scores[0:slots]
+    for word in range(1, TILE // slots):
+        result = jnp.where(words == word, scores[word * slots:(word + 1) * slots], result)
+    return result
+
+
+def expand(packed, slots):
+    words = word_of_lane(packed.shape, slots)
+    zero = jnp.zeros_like(packed)
+    return jnp.concatenate(
+        [jnp.where(words == word, packed, zero) for word in range(TILE // slots)], axis=0
+    )
+
+
+def stack_lanes(pair):
+    return jnp.concatenate([pair[:, :TILE], pair[:, TILE:]], axis=0)
+
+
+def pool_matrix(rows, slots, counts_col):
+    words = rows // slots
+    row = lax.broadcasted_iota(jnp.int32, (rows, words), 0)
+    word = lax.broadcasted_iota(jnp.int32, (rows, words), 1)
+    mine = (row // slots == word) & (jnp.bitwise_and(row, slots - 1) < counts_col)
+    return jnp.where(mine, 1.0 / counts_col.astype(F32), 0.0)
+
+
+def char_forward_kernel(slots, x_ref, cnt_lane_ref, cnt_col_ref, gain1_ref, wqkv_ref, wout_ref,
+                        gain2_ref, wup_ref, wdown_ref, wproj_ref,
+                        vec_ref, pooled_ref, qkv_ref, probs_ref, mixed_ref, first_ref,
+                        slope_ref, act_pool_ref):
+    rows = x_ref.shape[0]
+    width = x_ref.shape[1]
+    base = x_ref[...].astype(F32)
+    unit, _ = norm_parts(base)
+    normed = (unit * gain1_ref[...]).astype(BF)
+    qkv_ref[...] = nn(normed, wqkv_ref[...]).astype(BF)
+    for tile in range(rows // TILE):
+        at = pl.ds(tile * TILE, TILE)
+        valid = (lax.broadcasted_iota(jnp.int32, (slots, TILE), 0)
+                 < cnt_lane_ref[:, tile * TILE:(tile + 1) * TILE])
+        for pair in range(CHEADS // 2):
+            c0 = pair * TILE
+            queries = split_heads(qkv_ref[at, c0:c0 + TILE])
+            keys = qkv_ref[at, width + c0:width + c0 + TILE]
+            values = split_heads(qkv_ref[at, 2 * width + c0:2 * width + c0 + TILE])
+            scores = compact(nt(keys, queries), slots)
+            parts = []
+            for head in range(2):
+                own = jnp.where(valid, scores[:, head * TILE:(head + 1) * TILE], NEG_LARGE)
+                top = jnp.max(own, axis=0, keepdims=True)
+                weight = jnp.exp((own - top) * (CHD ** -0.5))
+                parts.append(weight / jnp.sum(weight, axis=0, keepdims=True))
+            probs = jnp.concatenate(parts, axis=1).astype(BF)
+            probs_ref[tile, pair] = probs
+            mixed_ref[at, c0:c0 + TILE] = tn(stack_lanes(expand(probs, slots)), values).astype(BF)
+    first = base + nn(mixed_ref[...], wout_ref[...])
+    first_ref[...] = first
+    unit2, _ = norm_parts(first)
+    normed2 = (unit2 * gain2_ref[...]).astype(BF)
+    counts_col = cnt_col_ref[...]
+    slot = jnp.bitwise_and(lax.broadcasted_iota(jnp.int32, (rows, 1), 0), slots - 1)
+    valid_col = slot < counts_col
+    pool = pool_matrix(rows, slots, counts_col).astype(BF)
+    chunk = 256
+    for part in range(wup_ref.shape[1] // chunk):
+        cols = slice(part * chunk, (part + 1) * chunk)
+        active, slope = gelu_parts(nn(normed2, wup_ref[:, cols]))
+        slope_ref[:, cols] = jnp.where(valid_col, slope, 0.0).astype(BF)
+        act_pool_ref[:, cols] = tn(pool, active.astype(BF)).astype(BF)
+    pooled = tn(pool, first.astype(BF)) + nn(act_pool_ref[...], wdown_ref[...])
+    pooled = pooled.astype(BF)
+    pooled_ref[...] = pooled
+    vec_ref[...] = nn(pooled, wproj_ref[...]).astype(BF)
+
+
+def char_forward(x, counts, gain1, wqkv, wout, gain2, wup, wdown, wproj):
+    rows, width = x.shape
+    words = counts.shape[0]
+    slots = rows // words
+    hidden = wup.shape[1]
+    wide = wproj.shape[1]
+    step = min(CSTEP, rows)
+    step_words = step // slots
+    spread = jnp.repeat(counts, slots)
+    row_block = lambda cols: pl.BlockSpec((step, cols), lambda i: (i, 0))
+    word_block = lambda cols: pl.BlockSpec((step_words, cols), lambda i: (i, 0))
+    whole = lambda shape: pl.BlockSpec(shape, lambda i: (0, 0))
+    tiles = step // TILE
+    return pl.pallas_call(
+        functools.partial(char_forward_kernel, slots),
+        grid=(rows // step,),
+        in_specs=[
+            row_block(width),
+            pl.BlockSpec((1, step), lambda i: (0, i)),
+            row_block(1),
+            whole((1, width)),
+            whole((width, 3 * width)),
+            whole((width, width)),
+            whole((1, width)),
+            whole((width, hidden)),
+            whole((hidden, width)),
+            whole((width, wide)),
+        ],
+        out_specs=[
+            word_block(wide),
+            word_block(width),
+            row_block(3 * width),
+            pl.BlockSpec((tiles, CHEADS // 2, slots, 2 * TILE), lambda i: (i, 0, 0, 0)),
+            row_block(width),
+            row_block(width),
+            row_block(hidden),
+            word_block(hidden),
+        ],
+        out_shape=[
+            jax.ShapeDtypeStruct((words, wide), BF),
+            jax.ShapeDtypeStruct((words, width), BF),
+            jax.ShapeDtypeStruct((rows, 3 * width), BF),
+            jax.ShapeDtypeStruct((rows // TILE, CHEADS // 2, slots, 2 * TILE), BF),
+            jax.ShapeDtypeStruct((rows, width), BF),
+            jax.ShapeDtypeStruct((rows, width), F32),
+            jax.ShapeDtypeStruct((rows, hidden), BF),
+            jax.ShapeDtypeStruct((words, hidden), BF),
+        ],
+        compiler_params=pltpu.CompilerParams(vmem_limit_bytes=60 << 20),
+        name="char_forward",
+    )(x, spread[None, :], spread[:, None], gain1[None, :], wqkv, wout, gain2[None, :], wup, wdown, wproj)
+
+
+def char_backward_kernel(slots, x_ref, cnt_col_ref, inv_ref, gain1_ref, wqkv_ref, wout_ref, gain2_ref,
+                         wup_ref, wdown_ref, gpl_ref, act_pool_ref, qkv_ref, probs_ref,
+                         mixed_ref, first_ref, slope_ref,
+                         dx_ref, dgain_ref, dqkv_ref, dout_ref, dup_ref, ddown_ref,
+                         down_ref, gq_ref, gmix_ref, gup_ref, spread_ref):
+    step = pl.program_id(0)
+    rows, width = x_ref.shape
+    words = rows // slots
+
+    @pl.when(step == 0)
+    def _():
+        dgain_ref[...] = jnp.zeros_like(dgain_ref)
+        dqkv_ref[...] = jnp.zeros_like(dqkv_ref)
+        dout_ref[...] = jnp.zeros_like(dout_ref)
+        dup_ref[...] = jnp.zeros_like(dup_ref)
+        low = gpl_ref[...].astype(BF)
+        ddown_ref[...] = tn(act_pool_ref[...], low)
+        scaled = gpl_ref[...] * inv_ref[...]
+        down_ref[:, width:] = nt(scaled.astype(BF), wdown_ref[...])
+        down_ref[:, :width] = scaled
+
+    for word in range(words):
+        line = down_ref[pl.ds(step * words + word, 1), :width]
+        spread_ref[word * slots:(word + 1) * slots, :] = jnp.broadcast_to(line, (slots, width))
+        line = down_ref[pl.ds(step * words + word, 1), width:]
+        at = slice(word * slots, (word + 1) * slots)
+        gup_ref[at, :] = (jnp.broadcast_to(line, (slots, line.shape[1])) * slope_ref[at, :].astype(F32)).astype(BF)
+
+    slot = jnp.bitwise_and(lax.broadcasted_iota(jnp.int32, (rows, 1), 0), slots - 1)
+    valid_col = slot < cnt_col_ref[...]
+    first = first_ref[...]
+    unit2, rate2 = norm_parts(first)
+    dup_ref[...] += tn((unit2 * gain2_ref[...]).astype(BF), gup_ref[...])
+    upstream = nt(gup_ref[...], wup_ref[...])
+    dgain_ref[1:2, :] += jnp.sum(upstream * unit2, axis=0, keepdims=True)
+    grad_first = jnp.where(valid_col, spread_ref[...], 0.0) + norm_back(upstream, gain2_ref[...], unit2, rate2)
+    spread_ref[...] = grad_first
+    low = grad_first.astype(BF)
+    dout_ref[...] += tn(mixed_ref[...], low)
+    gmix_ref[...] = nt(low, wout_ref[...]).astype(BF)
+    for tile in range(rows // TILE):
+        at = pl.ds(tile * TILE, TILE)
+        for pair in range(CHEADS // 2):
+            c0 = pair * TILE
+            queries = split_heads(qkv_ref[at, c0:c0 + TILE])
+            keys = split_heads(qkv_ref[at, width + c0:width + c0 + TILE])
+            values = qkv_ref[at, 2 * width + c0:2 * width + c0 + TILE]
+            grads = split_heads(gmix_ref[at, c0:c0 + TILE])
+            probs_low = probs_ref[tile, pair]
+            probs = probs_low.astype(F32)
+            grad_probs = compact(nt(values, grads), slots)
+            inner = jnp.sum(probs * grad_probs, axis=0, keepdims=True)
+            grad_scores = (probs * (grad_probs - inner) * (CHD ** -0.5)).astype(BF)
+            wide_scores = expand(grad_scores, slots)
+            wide_probs = expand(probs_low, slots)
+            gq_ref[at, c0:c0 + TILE] = tn(stack_lanes(wide_scores), keys).astype(BF)
+            gq_ref[at, width + c0:width + c0 + TILE] = nn(wide_scores, queries).astype(BF)
+            gq_ref[at, 2 * width + c0:2 * width + c0 + TILE] = nn(wide_probs, grads).astype(BF)
+    unit1, rate1 = norm_parts(x_ref[...].astype(F32))
+    dqkv_ref[...] += tn((unit1 * gain1_ref[...]).astype(BF), gq_ref[...])
+    upstream1 = nt(gq_ref[...], wqkv_ref[...])
+    dgain_ref[0:1, :] += jnp.sum(upstream1 * unit1, axis=0, keepdims=True)
+    dx_ref[...] = spread_ref[...] + norm_back(upstream1, gain1_ref[...], unit1, rate1)
+
+
+def char_backward(x, counts, gain1, wqkv, wout, gain2, wup, wdown, grad_pooled, saved):
+    qkv, probs, mixed, first, slope, act_pool = saved
+    rows, width = x.shape
+    words = counts.shape[0]
+    slots = rows // words
+    hidden = wup.shape[1]
+    step = min(CSTEP, rows)
+    spread = jnp.repeat(counts, slots)
+    row_block = lambda cols: pl.BlockSpec((step, cols), lambda i: (i, 0))
+    whole = lambda shape: pl.BlockSpec(shape, lambda i: (0, 0))
+    tiles = step // TILE
+    return pl.pallas_call(
+        functools.partial(char_backward_kernel, slots),
+        grid=(rows // step,),
+        in_specs=[
+            row_block(width),
+            row_block(1),
+            whole((words, 1)),
+            whole((1, width)),
+            whole((width, 3 * width)),
+            whole((width, width)),
+            whole((1, width)),
+            whole((width, hidden)),
+            whole((hidden, width)),
+            whole((words, width)),
+            whole((words, hidden)),
+            row_block(3 * width),
+            pl.BlockSpec((tiles, CHEADS // 2, slots, 2 * TILE), lambda i: (i, 0, 0, 0)),
+            row_block(width),
+            row_block(width),
+            row_block(hidden),
+        ],
+        out_specs=[
+            row_block(width),
+            whole((8, width)),
+            whole((width, 3 * width)),
+            whole((width, width)),
+            whole((width, hidden)),
+            whole((hidden, width)),
+        ],
+        out_shape=[
+            jax.ShapeDtypeStruct((rows, width), F32),
+            jax.ShapeDtypeStruct((8, width), F32),
+            jax.ShapeDtypeStruct((width, 3 * width), F32),
+            jax.ShapeDtypeStruct((width, width), F32),
+            jax.ShapeDtypeStruct((width, hidden), F32),
+            jax.ShapeDtypeStruct((hidden, width), F32),
+        ],
+        scratch_shapes=[
+            pltpu.VMEM((words, width + hidden), F32),
+            pltpu.VMEM((step, 3 * width), BF),
+            pltpu.VMEM((step, width), BF),
+            pltpu.VMEM((step, hidden), BF),
+            pltpu.VMEM((step, width), F32),
+        ],
+        compiler_params=pltpu.CompilerParams(vmem_limit_bytes=60 << 20),
+        name="char_backward",
+    )(x, spread[:, None], (1.0 / counts.astype(F32))[:, None], gain1[None, :], wqkv, wout, gain2[None, :],
+      wup, wdown, grad_pooled, act_pool, qkv, probs, mixed, first, slope)
+
+
+HD = 64
 
 
 def layer_norm(values, gain_vector):
@@ -157,41 +470,11 @@
     word_down,
 ):
     word_count = char_counts.shape[0]
-    slot_count = char_inputs.shape[0] // word_count
-    char_width = char_inputs.shape[1]
-    shape_four = (word_count, slot_count, CHEADS, CHD)
-    char_scale = CHD ** (-0.5)
     tensor_rank = lax.axis_index("tensor")
-    base_rows = char_inputs.astype(jnp.float32)
-    char_normed, pull_char_one = jax.vjp(layer_norm, base_rows, char_norm_one)
-    char_normed = char_normed.astype(jnp.bfloat16)
-    char_q = matmul(char_normed, char_query).astype(jnp.bfloat16).reshape(shape_four)
-    char_k = matmul(char_normed, char_key).astype(jnp.bfloat16).reshape(shape_four)
-    char_v = matmul(char_normed, char_value).astype(jnp.bfloat16).reshape(shape_four)
-    char_scores = (
-        jnp.einsum("wqhd,wkhd->whqk", char_q, char_k, preferred_element_type=jnp.float32)
-        * char_scale
-    )
-    slot_valid = jnp.arange(slot_count)[None, :] < char_counts[:, None]
-    char_scores = jnp.where(slot_valid[:, None, None, :], char_scores, NEG_LARGE)
-    char_probs = jax.nn.softmax(char_scores, axis=-1)
-    char_probs_low = char_probs.astype(jnp.bfloat16)
-    char_mixed = jnp.einsum(
-        "whqk,wkhd->wqhd", char_probs_low, char_v, preferred_element_type=jnp.float32
-    )
-    char_mixed = char_mixed.astype(jnp.bfloat16).reshape(word_count * slot_count, char_width)
-    char_first = base_rows + matmul(char_mixed, char_out)
-    char_normed_two, pull_char_two = jax.vjp(layer_norm, char_first, char_norm_two)
-    char_normed_two = char_normed_two.astype(jnp.bfloat16)
-    char_hidden, pull_char_gelu = jax.vjp(gelu_tanh, matmul(char_normed_two, char_up))
-    char_hidden = char_hidden.astype(jnp.bfloat16)
-    char_second = char_first + matmul(char_hidden, char_down)
-    slot_weights = slot_valid.astype(jnp.float32) / char_counts.astype(jnp.float32)[:, None]
-    pooled = jnp.sum(
-        char_second.reshape(word_count, slot_count, char_width) * slot_weights[:, :, None], axis=1
-    )
-    pooled = pooled.astype(jnp.bfloat16)
-    word_vectors = matmul(pooled, char_proj).astype(jnp.bfloat16)
+    char_qkv = jnp.concatenate([char_query, char_key, char_value], axis=1)
+    word_vectors, pooled, *saved = char_forward(
+        char_inputs, char_counts, char_norm_one, char_qkv, char_out, char_norm_two, char_up, char_down, char_proj
+    )
     input_whole = lax.all_gather(word_vectors, "tensor", axis=0, tiled=True).astype(jnp.float32)
     normed_whole, pull_first = jax.vjp(layer_norm, input_whole, word_norm_one)
     normed = normed_whole.astype(jnp.bfloat16)
@@ -259,45 +542,12 @@
     grad_vectors = grad_input.astype(jnp.bfloat16)
     grad_proj = contract_rows(pooled, grad_vectors)
     grad_pooled = contract_cols(grad_vectors, char_proj)
-    grad_second = (grad_pooled[:, None, :] * slot_weights[:, :, None]).reshape(
-        word_count * slot_count, char_width
-    )
-    second_low = grad_second.astype(jnp.bfloat16)
-    grad_char_down = contract_rows(char_hidden, second_low)
-    grad_char_pre = pull_char_gelu(contract_cols(second_low, char_down))[0].astype(jnp.bfloat16)
-    grad_char_up = contract_rows(char_normed_two, grad_char_pre)
-    back_char_two, grad_char_gain_two = pull_char_two(contract_cols(grad_char_pre, char_up))
-    grad_first = grad_second + back_char_two
-    first_low = grad_first.astype(jnp.bfloat16)
-    grad_char_out = contract_rows(char_mixed, first_low)
-    grad_char_mixed = contract_cols(first_low, char_out).astype(jnp.bfloat16).reshape(shape_four)
-    grad_char_probs = jnp.einsum(
-        "wqhd,wkhd->whqk", grad_char_mixed, char_v, preferred_element_type=jnp.float32
-    )
-    char_inner = jnp.sum(char_probs * grad_char_probs, axis=-1, keepdims=True)
-    grad_char_scores = (char_probs * (grad_char_probs - char_inner)).astype(jnp.bfloat16)
-    flat_chars = (word_count * slot_count, char_width)
-    grad_cv = jnp.einsum(
-        "whqk,wqhd->wkhd", char_probs_low, grad_char_mixed, preferred_element_type=jnp.float32
-    )
-    grad_cv = grad_cv.astype(jnp.bfloat16).reshape(flat_chars)
-    grad_cq = jnp.einsum(
-        "whqk,wkhd->wqhd", grad_char_scores, char_k, preferred_element_type=jnp.float32
-    )
-    grad_cq = (grad_cq * char_scale).astype(jnp.bfloat16).reshape(flat_chars)
-    grad_ck = jnp.einsum(
-        "whqk,wqhd->wkhd", grad_char_scores, char_q, preferred_element_type=jnp.float32
-    )
-    grad_ck = (grad_ck * char_scale).astype(jnp.bfloat16).reshape(flat_chars)
-    grad_char_query = contract_rows(char_normed, grad_cq)
-    grad_char_key = contract_rows(char_normed, grad_ck)
-    grad_char_value = contract_rows(char_normed, grad_cv)
-    back_char_one, grad_char_gain_one = pull_char_one(
-        contract_cols(grad_cq, char_query)
-        + contract_cols(grad_ck, char_key)
-        + contract_cols(grad_cv, char_value)
-    )
-    char_input_gradient = grad_first + back_char_one
+    char_input_gradient, grad_gains, grad_char_qkv, grad_char_out, grad_char_up, grad_char_down = char_backward(
+        char_inputs, char_counts, char_norm_one, char_qkv, char_out, char_norm_two, char_up, char_down,
+        grad_pooled, saved
+    )
+    grad_char_gain_one, grad_char_gain_two = grad_gains[0], grad_gains[1]
+    grad_char_query, grad_char_key, grad_char_value = jnp.split(grad_char_qkv, 3, axis=1)
     word_sums = lax.psum(
         (grad_query, grad_key, grad_value, grad_out_proj, grad_up, grad_down), "dp"
     )

time: 738 us -> 598 us (0.81); the launches traced: 727 us -> 597 us
  matrix products: 176 us -> 58.7 us
  Pallas kernels: 0 us -> 67.7 us
  local copies, waits for them, and re-layouts: 106 us -> 39.4 us
  other arithmetic: 94.4 us -> 29.1 us
  waiting for transfers between devices: 288 us -> 341 us
    pallas_call x0 -> x2, Pallas kernels: none -> 67.7 us  [the longest x1 34.9 us: char_backward(): pl.pallas_call(functools.partial(char_backward_kernel, slots), grid=(rows...]
    reshape x8 -> x0, local copies, waits for them, and re-layouts: 52.9 us -> none  [the longest x1 7.19 us: per_device(): grad_ck = (grad_ck * char_scale).astype(jnp.bfloat16).reshape(flat_chars)]
    psum x1, waiting for transfers between devices: 86.2 us -> 139 us  [per_device(): lax.psum((grad_char_gain_one, grad_char_query, grad_char_key, grad_char_v...]
    dot_general x6 -> x0, matrix products: 37.8 us -> none  [the longest x1 12.3 us: per_device(): jnp.einsum('wqhd,wkhd->whqk', grad_char_mixed, char_v, preferred_element_...]
    dot_general x13 -> x7, matrix products: 43 us -> 8.64 us  [contract_cols(): lax.dot_general(left, right, (((1,), (1,)), ((), ())), preferred_element_...]
    sub x1 -> x0, other arithmetic: 28.7 us -> none  [per_device(): char_probs = jax.nn.softmax(char_scores, axis=-1)]
    dot_general x13 -> x6, matrix products: 37.2 us -> 9.53 us  [matmul(): return jnp.dot(left, right, preferred_element_type=jnp.float32)]
    dot_general x13 -> x7, matrix products: 32.8 us -> 9.24 us  [contract_rows(): lax.dot_general(left, right, (((0,), (0,)), ((), ())), preferred_element_...]
  transfers between devices with their start and end apart: 6 -> 6, of which waited for: 5 -> 5; matrix products, arithmetic and copies ran while one was open for 23% -> 5% of each run, Pallas kernels for 0% -> 6%
where the time goes in v1:
time: 598 us; the launch traced here: 597 us
  waiting for transfers between devices  341 us (57%)
  Pallas kernels  67.7 us (11%)
  matrix products  58.7 us (10%)
  local copies, waits for them, and re-layouts  39.4 us (7%)
  blocking collectives  39.4 us (7%)
  other arithmetic  29.1 us (5%)
  between operations  14.8 us (2%)
  loops' own time  6.74 us (1%)
    psum x1, waiting for transfers between devices, per_device(): lax.psum((grad_char_gain_one, grad_char_query, grad_char_key, grad_char_v...  139 us
    psum x1, waiting for transfers between devices, per_device(): lax.psum(feedforward_part.astype(jnp.bfloat16), 'tensor')  75.2 us
    psum x1, waiting for transfers between devices, per_device(): lax.psum(attention_part.astype(jnp.bfloat16), 'tensor').astype(jnp.float32)  48.1 us
    psum x1, waiting for transfers between devices, per_device(): lax.psum(mid_part.astype(jnp.bfloat16), 'tensor').astype(jnp.float32)  47.8 us
    psum x1, blocking collectives, per_device(): lax.psum((grad_char_gain_one, grad_char_query, grad_char_key, grad_char_v...  39.4 us
    pallas_call x1, Pallas kernels, char_backward(): pl.pallas_call(functools.partial(char_backward_kernel, slots), grid=(rows...  34.9 us
    pallas_call x1, Pallas kernels, char_forward(): pl.pallas_call(functools.partial(char_forward_kernel, slots), grid=(rows...  32.7 us
    all_gather x1, waiting for transfers between devices, per_device(): lax.all_gather(word_vectors, 'tensor', axis=0, tiled=True)  30.8 us
  transfers between devices with their start and end apart: 6, of which 5 were waited for; matrix products, arithmetic and copies ran while one was open for 5% of the time, Pallas kernels for 6%

profile of v1, /device:TPU:0, one launch (start us, length us, event | category | flops | bytes accessed | tf_op | source)
XLA Modules:
  0.0 597.1 jit_solution(14217569614496791594)
XLA Ops:
  8.1 2.5 broadcast_in_dim_reshape.9.cnt_col_ref
  12.2 32.7 %char_forward.1 = (bf16[256,512]{1,0:T(8,128)(2,1)}, bf16[256,256]{1,0:T(8,128)(2,1)}, bf16[4096,768]{1,0:T(8,128)(2,1)}, bf16[32,2,16,256]{3,2,1,0:T(8,128)(2,1...) custom-call(bf16[4096,256]{1,0:T(8,128)(2,1)} %x_ref.3, ...), custom_call_target="tpu_custom_call" | custom-call | tf_op jit(solution)/shard_map/char_forward/pallas_call | solution.py:159
  45.0 30.8 %all-gather.2.cloned.1.call-done = bf16[1024,512]{1,0:T(8,128)(2,1)} async-done(((bf16[256,512]{1,0:T(8,128)(2,1)}), bf16[1024,512]{1,0:T(8,128)(2,1)}) %all-gather.2.cloned.1.call-update) | async-done | bytes 1048592 | tf_op jit(solution)/shard_map/all_gather | solution.py:478
  82.0 13.8 %while.47 = (s32[]{:T(128)}, bf16[2,512,2,64]{1,3,2,0:T(8,128)(2,1)}, f32[2,2,512]{2,1,0:T(2,128)}, s32[2]{0:T(128)S(1)}, s32[1024]{0:T(1024)S(1)}, /*index=5*/b...) while((s32[]{:T(128)}, ...), condition=%wide.region_5.6_spmd, body=%wide.region_2.5_spmd.sunk | while | flops 282656256 | bytes 15514811 | solution.py:388
  86.8 2.1 fusion.151
  99.5 3.1 fusion.74
  102.6 48.1 %all-reduce.10.cloned.1.call-done = bf16[1024,512]{1,0:T(8,128)(2,1)} async-done(((bf16[1024,512]{1,0:T(8,128)(2,1)}), bf16[1024,512]{1,0:T(8,128)(2,1)}) %all-reduce.10.cloned.1.call-update) | async-done | bytes 1048592 | tf_op jit(solution)/shard_map/psum | solution.py:493
  155.1 3.2 fusion.58
  161.1 3.5 convolution_convert_fusion.2
  164.6 47.8 %all-reduce.12.cloned.1.call-done = bf16[1024,512]{1,0:T(8,128)(2,1)} async-done(((bf16[1024,512]{1,0:T(8,128)(2,1)}), bf16[1024,512]{1,0:T(8,128)(2,1)}) %all-reduce.12.cloned.1.call-update) | async-done | bytes 1048592 | tf_op jit(solution)/shard_map/psum | solution.py:512
  214.5 2.1 fusion.50
  216.6 2.2 add_add_fusion.2
  221.3 38.6 %while.48 = (s32[]{:T(128)}, f32[1024,2,64]{0,2,1:T(8,128)S(1)}, f32[1024,2,64]{0,2,1:T(8,128)}, bf16[2,512,2,64]{1,3,2,0:T(8,128)(2,1)}, s32[2]{0:T(128)S(1)}, ...) while((s32[]{:T(128)}, f32[1024,2,64]{0,2,1:T(8,128)S(1)}, ...), condition=%wide.region_15.16_spmd.clone, body=%wide.region_13.15_spmd.clone.sunk | while | flops 689176064 | bytes 79080000 | solution.py:437
  223.4 2.8 fusion.161
  228.8 4.1 multiply_reduce_fusion.3
  237.3 3.2 fusion.164
  242.6 2.8 fusion.161
  248.0 4.1 multiply_reduce_fusion.3
  256.6 3.4 fusion.164
  275.3 75.2 %all-reduce.18.cloned.1.call-done = (bf16[1024,512]{1,0:T(8,128)(2,1)}, bf16[1024,512]{1,0:T(8,128)(2,1)}) async-done(((bf16[1024,512]{1,0:T(8,128)(2,1)}, bf16[1024,512]{1,0:T(8,128)(2,1)}), (bf16[1024,512]{1,0:T(8,128)(2,1)}, bf16[1024,512]{1,0:T(8,128)(2,1)})) %all-reduce.18.cloned.1.call-update) | async-done | bytes 2097168 | tf_op jit(solution)/shard_map/psum | solution.py:501
  350.5 2.5 fusion.51
  356.3 34.9 %char_backward.1 = (f32[4096,256]{1,0:T(8,128)}, f32[8,256]{1,0:T(8,128)}, f32[256,768]{1,0:T(8,128)}, f32[256,256]{1,0:T(8,128)}, f32[256,1024]{1,0:T(8,128)}, /*index=5*/f32[1024,256]{1,0:T(8,128)}) custom-call(bf16[4096,256]{1,0:T(8,128)(2,1)} %x_ref.3, s32[4096,1]{1,0:T(8,128)} %broadcast_in_dim_reshape.9.cnt_col_ref, f32[256,1]{1,0:T(8,128)} %copy.44.inv_ref, ...), custom_call_target="tpu_custom_call" | custom-call | tf_op jit(solution)/shard_map/char_backward/pallas_call | solution.py:275
  395.8 39.4 %all-reduce = (f32[256]{0:T(256)}, f32[256]{0:T(256)}, f32[512]{0:T(512)}, f32[512]{0:T(512)}) all-reduce(f32[256]{0:T(256)S(1)} %bitcast.142, f32[256]{0:T(256)S(1)} %bitcast.141, f32[512]{0:T(512)S(1)} %get-tuple-element.318, f32[512]{0:T(512)S(1)} %get-tuple-element.317), channel_id=1, replica_groups=mesh['dp'=8,'tensor'=4] {'dp','tensor'}, use_global_device_ids=true, to_apply=%region_19.20 | all-reduce | flops 1536 | bytes 12288 | tf_op jit(solution)/shard_map/psum | solution.py:554
  437.1 138.7 %all-reduce.14.cloned.1.call-done = (f32[256,256]{1,0:T(8,128)}, f32[256,256]{1,0:T(8,128)}, f32[256,256]{1,0:T(8,128)}, f32[256,256]{1,0:T(8,128)}, f32[256,102...) async-done(((f32[256,256]{1,0:T(8,128)}, f32[256,256]{1,0:T(8,128)}, f32[256,256]{1,0:T(8,128)}, f32[256,256]{1,0:T(8,128)}, f32[256,1024]{1,0:T(8,128)}, ...) | async-done | bytes 3670032 | tf_op jit(solution)/shard_map/psum | solution.py:554
  (270 shorter events, 86.5 us)
Async XLA Ops:
  7.2 146.8 %copy-start = (bf16[512,512]{1,0:T(8,128)(2,1)S(1)}, bf16[512,512]{1,0:T(8,128)(2,1)}, u32[]{:S(2)}) copy-start(bf16[512,512]{1,0:T(8,128)(2,1)} %param.44) | copy-start | bytes 1572868
  7.2 68.6 %all-gather.2.cloned.1.call-start = ((), (), s32[]{:S(2)}) async-start(), calls=%async_computation | async-start | bytes 1310720 | tf_op jit(solution)/shard_map/all_gather | solution.py:478
  44.9 34.2 %copy-start.60 = (f32[512]{0:T(512)S(1)}, f32[512]{0:T(512)}, u32[]{:S(2)}) copy-start(f32[512]{0:T(512)} %param.38) | copy-start | bytes 6148
  45.0 105.7 %all-reduce.10.cloned.1.call-start = ((), (), s32[]{:S(2)}) async-start(), calls=%async_computation.1 | async-start | bytes 2097152 | tf_op jit(solution)/shard_map/psum | solution.py:493
  45.0 34.7 %copy-start.38 = (bf16[512,128]{1,0:T(8,128)(2,1)S(1)}, bf16[512,128]{1,0:T(8,128)(2,1)}, u32[]{:S(2)}) copy-start(bf16[512,128]{1,0:T(8,128)(2,1)} %param.39) | copy-start | bytes 393220
  82.0 15.8 %copy-start.37 = (bf16[128,512]{1,0:T(8,128)(2,1)S(1)}, bf16[128,512]{1,0:T(8,128)(2,1)}, u32[]{:S(2)}) copy-start(bf16[128,512]{1,0:T(8,128)(2,1)} %param.42) | copy-start | bytes 393220
  99.3 113.1 %all-reduce.12.cloned.1.call-start = ((), (), s32[]{:S(2)}) async-start(), calls=%async_computation.2 | async-start | bytes 2097152 | tf_op jit(solution)/shard_map/psum | solution.py:512
  161.0 189.4 %all-reduce.18.cloned.1.call-start = ((), (), s32[]{:S(2)}) async-start(), calls=%async_computation.5 | async-start | bytes 4194304 | tf_op jit(solution)/shard_map/psum | solution.py:501
  221.3 4.8 copy-start.11
  221.3 7.4 %copy-start.13 = (bf16[1024,2,64]{0,2,1:T(8,128)(2,1)}, bf16[1024,2,64]{0,2,1:T(8,128)(2,1)S(1)}, u32[]{:S(2)}) copy-start(bf16[1024,2,64]{0,2,1:T(8,128)(2,1)S(1)} %get-tuple-element.521) | copy-start | bytes 786436 | tf_op jit(solution)/shard_map/while/body/eval_jaxpr/while
  221.3 7.4 %copy-start.20 = (bf16[1024,2,64]{0,2,1:T(8,128)(2,1)}, bf16[1024,2,64]{0,2,1:T(8,128)(2,1)S(1)}, u32[]{:S(2)}) copy-start(bf16[1024,2,64]{0,2,1:T(8,128)(2,1)S(1)} %get-tuple-element.520) | copy-start | bytes 786436 | tf_op jit(solution)/shard_map/while/body/eval_jaxpr/while
  240.5 4.8 copy-start.11
  240.5 7.5 %copy-start.13 = (bf16[1024,2,64]{0,2,1:T(8,128)(2,1)}, bf16[1024,2,64]{0,2,1:T(8,128)(2,1)S(1)}, u32[]{:S(2)}) copy-start(bf16[1024,2,64]{0,2,1:T(8,128)(2,1)S(1)} %get-tuple-element.521) | copy-start | bytes 786436 | tf_op jit(solution)/shard_map/while/body/eval_jaxpr/while
  240.5 7.5 %copy-start.20 = (bf16[1024,2,64]{0,2,1:T(8,128)(2,1)}, bf16[1024,2,64]{0,2,1:T(8,128)(2,1)S(1)}, u32[]{:S(2)}) copy-start(bf16[1024,2,64]{0,2,1:T(8,128)(2,1)S(1)} %get-tuple-element.520) | copy-start | bytes 786436 | tf_op jit(solution)/shard_map/while/body/eval_jaxpr/while
  264.8 172.3 %all-reduce.16.cloned.1.call-start = ((), (), s32[]{:S(2)}) async-start(), calls=%async_computation.4 | async-start | bytes 6291456 | tf_op jit(solution)/shard_map/psum | solution.py:551
  275.2 75.3 %copy-start.5 = (bf16[1024,512]{1,0:T(8,128)(2,1)S(1)}, bf16[1024,512]{1,0:T(8,128)(2,1)}, u32[]{:S(2)}) copy-start(bf16[1024,512]{1,0:T(8,128)(2,1)} %all-gather.2.cloned.1.call-done) | copy-start | bytes 3145732
  275.2 75.3 %copy-start.53 = (f32[1024]{0:T(1024)S(1)}, f32[1024]{0:T(1024)}, u32[]{:S(2)}) copy-start(f32[1024]{0:T(1024)} %copy-done.52) | copy-start | bytes 12292
  275.2 75.3 %copy-start.61 = (f32[512]{0:T(512)S(1)}, f32[512]{0:T(512)}, u32[]{:S(2)}) copy-start(f32[512]{0:T(512)} %param.38) | copy-start | bytes 6148
  275.2 77.8 %copy-start.55 = (f32[1024]{0:T(1024)S(1)}, f32[1024]{0:T(1024)}, u32[]{:S(2)}) copy-start(f32[1024]{0:T(1024)} %copy-done.54) | copy-start | bytes 12292
  275.2 300.7 %all-reduce.14.cloned.1.call-start = ((), (), s32[]{:S(2)}) async-start(), calls=%async_computation.3 | async-start | bytes 7340032 | tf_op jit(solution)/shard_map/psum | solution.py:554
  356.3 35.0 %copy-start.48 = (bf16[256,256]{1,0:T(8,128)(2,1)S(1)}, bf16[256,256]{1,0:T(8,128)(2,1)}, u32[]{:S(2)}) copy-start(bf16[256,256]{1,0:T(8,128)(2,1)} %get-tuple-element.204) | copy-start | bytes 393220
  575.9 6.8 %copy-start.30 = (f32[256,1024]{1,0:T(8,128)S(1)}, f32[256,1024]{1,0:T(8,128)}, u32[]{:S(2)}) copy-start(f32[256,1024]{1,0:T(8,128)} %get-tuple-element.535) | copy-start | bytes 3145732
  575.9 7.8 %copy-start.29 = (f32[1024,256]{1,0:T(8,128)S(1)}, f32[1024,256]{1,0:T(8,128)}, u32[]{:S(2)}) copy-start(f32[1024,256]{1,0:T(8,128)} %get-tuple-element.536) | copy-start | bytes 3145732
  583.7 4.6 copy-start.28
  (59 other events, 137.0 us)
Sparse Core Ops, SparseCore 0:
  45.1 30.6 all-gather.1
  99.4 51.2 all-reduce.9
  161.2 51.1 all-reduce.11
  265.0 85.4 all-reduce.17
  355.4 69.6 all-reduce.15
  432.6 143.2 all-reduce.13

commit v2 on v1

v2 whole, which is shorter than its diff:
```python
import functools

import jax
import jax.numpy as jnp
from jax import lax
from jax.experimental import pallas as pl
from jax.experimental.pallas import tpu as pltpu
from jax.sharding import PartitionSpec as P

BF = jnp.bfloat16
F32 = jnp.float32
EPSILON = 1e-05
NEG_LARGE = -1e30
RANKS = 4
CHEADS = 4
CHD = 64
TILE = 128
CHAR_STEPS = 8
GELU_C = 0.7978845608028654
GELU_A = 0.044715


def nn(left, right):
    return lax.dot_general(left, right, (((1,), (0,)), ((), ())), preferred_element_type=F32)


def nt(left, right):
    return lax.dot_general(left, right, (((1,), (1,)), ((), ())), preferred_element_type=F32)


def tn(left, right):
    return lax.dot_general(left, right, (((0,), (0,)), ((), ())), preferred_element_type=F32)


def norm_parts(values):
    centre = values - jnp.mean(values, axis=-1, keepdims=True)
    spread = jnp.mean(centre * centre, axis=-1, keepdims=True)
    rate = lax.rsqrt(spread + EPSILON)
    return centre * rate, rate


def norm_back(upstream, gain, unit, rate):
    scaled = upstream * gain
    first = jnp.mean(scaled, axis=-1, keepdims=True)
    second = jnp.mean(scaled * unit, axis=-1, keepdims=True)
    return rate * (scaled - first - unit * second)


def gelu_parts(values):
    square = values * values
    inner = values * (GELU_C + (GELU_C * GELU_A) * square)
    half = 0.5 + 0.5 * jnp.tanh(inner)
    active = values * half
    slope = half + (active * (1.0 - half)) * (2.0 * GELU_C + (6.0 * GELU_C * GELU_A) * square)
    return active, slope


def split_heads(pair):
    low_half = lax.broadcasted_iota(jnp.int32, pair.shape, 1) < CHD
    zero = jnp.zeros_like(pair)
    return jnp.concatenate([jnp.where(low_half, pair, zero), jnp.where(low_half, zero, pair)], axis=0)


def word_of_lane(shape, slots):
    lane = lax.broadcasted_iota(jnp.int32, shape, 1)
    return jnp.bitwise_and(lane, TILE - 1) // slots


def compact(scores, slots):
    words = word_of_lane((slots, scores.shape[1]), slots)
    result = scores[0:slots]
    for word in range(1, TILE // slots):
        result = jnp.where(words == word, scores[word * slots:(word + 1) * slots], result)
    return result


def expand(packed, slots):
    words = word_of_lane(packed.shape, slots)
    zero = jnp.zeros_like(packed)
    return jnp.concatenate(
        [jnp.where(words == word, packed, zero) for word in range(TILE // slots)], axis=0
    )


def stack_lanes(pair):
    return jnp.concatenate([pair[:, :TILE], pair[:, TILE:]], axis=0)


def pool_matrix(rows, slots, counts_col):
    words = rows // slots
    row = lax.broadcasted_iota(jnp.int32, (rows, words), 0)
    word = lax.broadcasted_iota(jnp.int32, (rows, words), 1)
    mine = (row // slots == word) & (jnp.bitwise_and(row, slots - 1) < counts_col)
    return jnp.where(mine, 1.0 / counts_col.astype(F32), 0.0)


MESH = pl.DeviceIdType.MESH
LANE_SPLIT = 256


class Place:
    def __init__(self):
        self.dp = lax.axis_index("dp")
        self.rank = lax.axis_index("tensor")
        self.core = lax.rem(self.dp, 2)
        self.x = lax.rem(self.dp // 2, 2)
        self.y = lax.rem(self.dp // 4, 2)
        self.core_mate = (self.dp + 1 - 2 * self.core, self.rank)
        self.x_mate = (self.dp + 2 - 4 * self.x, self.rank)
        self.y_mate = (self.dp + 4 - 8 * self.y, self.rank)

    def ring(self, offset):
        return lax.rem(self.rank + offset, RANKS)

    def ring_device(self, offset):
        return (self.dp, self.ring(offset))

    def bit_mate(self, bit):
        size = 1 << bit
        mine = lax.rem(self.dp // size, 2)
        return (self.dp + size - 2 * size * mine, self.rank)

    def mates(self, bits):
        extra = [self.bit_mate(bit) for bit in range(3, bits)]
        return [self.core_mate, self.x_mate, self.y_mate] + extra


def meet(devices):
    barrier = pltpu.get_barrier_semaphore()
    for device in devices:
        pl.semaphore_signal(barrier, inc=1, device_id=device, device_id_type=MESH)
    pl.semaphore_wait(barrier, len(devices))


def remote(source, target, sems, device):
    return pltpu.make_async_remote_copy(
        src_ref=source, dst_ref=target, send_sem=sems[0], recv_sem=sems[1],
        device_id=device, device_id_type=MESH,
    )


class Sems:
    def __init__(self, send, recv, start=0):
        self.send, self.recv, self.next = send, recv, start

    def take(self):
        at = self.next
        self.next += 1
        return self.send.at[at], self.recv.at[at]


def rows_at(start, size):
    return pl.ds(pl.multiple_of(start, 16), size)


def halves(width):
    return (slice(0, LANE_SPLIT), slice(LANE_SPLIT, width))


class Gather:
    def __init__(self, place, local, whole, sems):
        self.stages = [[], [], [], []]
        rows = local.shape[0]
        unit = rows // 8
        p = place
        left, right = halves(local.shape[1])
        left_at = p.core * 4 + p.x * 2 + p.y
        right_at = p.core * 4 + p.y * 2 + p.x
        for offset in range(1, RANKS):
            for lanes, at in ((left, left_at), (right, right_at)):
                at = rows_at(at * unit, unit)
                self.stages[0].append(remote(
                    local.at[at, lanes], whole.at[p.rank, at, lanes], sems.take(), p.ring_device(offset)))
        for offset in range(1, RANKS):
            rank = p.ring(offset)
            for lanes, at, first, second, mate_first, mate_second in (
                (left, left_at, p.x, None, p.y_mate, p.x_mate),
                (right, right_at, p.y, None, p.x_mate, p.y_mate),
            ):
                one = rows_at(at * unit, unit)
                two = rows_at((p.core * 4 + first * 2) * unit, 2 * unit)
                self.stages[1].append(remote(
                    whole.at[rank, one, lanes], whole.at[rank, one, lanes], sems.take(), mate_first))
                self.stages[2].append(remote(
                    whole.at[rank, two, lanes], whole.at[rank, two, lanes], sems.take(), mate_second))
            four = rows_at(p.core * 4 * unit, 4 * unit)
            self.stages[3].append(remote(
                whole.at[rank, four], whole.at[rank, four], sems.take(), p.core_mate))

    def start(self, stage):
        for copy in self.stages[stage]:
            copy.start()

    def wait(self, stage):
        for copy in self.stages[stage]:
            copy.wait()


def gather_copies():
    return 2 * (RANKS - 1) * 3 + (RANKS - 1)


class Reduce:
    def __init__(self, place, bits, buf, out, got_core, got_one, got_two, got_more, got_rank, sems, everywhere):
        p = place
        self.p, self.buf, self.everywhere = p, buf, everywhere
        self.mine = out.at[p.rank] if everywhere else out
        self.got = (got_core, got_one, got_two, got_more, got_rank)
        rows = buf.shape[1]
        unit = rows // 8
        self.unit = unit
        left, right = halves(buf.shape[2])
        self.lanes = (left, right)
        half = lambda core: rows_at(core * 4 * unit, 4 * unit)
        self.core_copy = [remote(buf.at[:, half(1 - p.core)], got_core, sems.take(), p.core_mate)]
        self.core_rows = half(p.core)
        quarter_left = lambda x: rows_at((p.core * 4 + x * 2) * unit, 2 * unit)
        quarter_right = lambda y: rows_at((p.core * 4 + y * 2) * unit, 2 * unit)
        self.one_copy = [
            remote(buf.at[:, quarter_left(1 - p.x), left], got_one.at[:, :, left], sems.take(), p.x_mate),
            remote(buf.at[:, quarter_right(1 - p.y), right], got_one.at[:, :, right], sems.take(), p.y_mate),
        ]
        self.one_rows = (quarter_left(p.x), quarter_right(p.y))
        eighth_left = lambda y: rows_at((p.core * 4 + p.x * 2 + y) * unit, unit)
        eighth_right = lambda x: rows_at((p.core * 4 + p.y * 2 + x) * unit, unit)
        self.two_copy = [
            remote(buf.at[:, eighth_left(1 - p.y), left], got_two.at[:, :, left], sems.take(), p.y_mate),
            remote(buf.at[:, eighth_right(1 - p.x), right], got_two.at[:, :, right], sems.take(), p.x_mate),
        ]
        self.two_rows = (eighth_left(p.y), eighth_right(p.x))
        self.more_copy = []
        for bit in range(3, bits):
            mate = p.bit_mate(bit)
            self.more_copy.append([
                remote(buf.at[:, at, lanes], got_more.at[bit - 3, :, :, lanes], sems.take(), mate)
                for at, lanes in zip(self.two_rows, self.lanes)
            ])
        self.rank_copy, self.rank_back = [], []
        for offset in range(1, RANKS):
            for at, lanes in zip(self.two_rows, self.lanes):
                self.rank_copy.append(remote(
                    buf.at[p.ring(offset), at, lanes], got_rank.at[offset - 1, :, lanes],
                    sems.take(), p.ring_device(offset)))
        if everywhere:
            for offset in range(1, RANKS):
                for at, lanes in zip(self.two_rows, self.lanes):
                    self.rank_back.append(remote(
                        out.at[p.rank, at, lanes], out.at[p.rank, at, lanes], sems.take(), p.ring_device(offset)))

        def back(at, lanes, mate):
            part = out.at[:, at, lanes] if everywhere else out.at[at, lanes]
            return remote(part, part, sems.take(), mate)

        self.back_two = [back(self.two_rows[0], left, p.y_mate), back(self.two_rows[1], right, p.x_mate)]
        self.back_one = [back(self.one_rows[0], left, p.x_mate), back(self.one_rows[1], right, p.y_mate)]
        self.back_core = [back(self.core_rows, slice(None), p.core_mate)]
        names = ["core", "one", "two"] + list(range(len(self.more_copy))) + ["rank"]
        names += ["rank_back"] if everywhere else []
        self.names = names + ["back_two", "back_one", "back_core"]

    def copies(self, name):
        if isinstance(name, int):
            return self.more_copy[name]
        return {"core": self.core_copy, "one": self.one_copy, "two": self.two_copy, "rank": self.rank_copy,
                "rank_back": self.rank_back, "back_two": self.back_two, "back_one": self.back_one,
                "back_core": self.back_core}[name]

    def add(self, at, lanes, terms, who=slice(None)):
        total = self.buf[who, at, lanes].astype(F32)
        for term in terms:
            total = total + term.astype(F32)
        self.buf[who, at, lanes] = total.astype(BF)

    def start(self, index):
        for copy in self.copies(self.names[index]):
            copy.start()

    def finish(self, index):
        name = self.names[index]
        for copy in self.copies(name):
            copy.wait()
        got_core, got_one, got_two, got_more, got_rank = self.got
        if name == "core":
            for quarter in range(RANKS):
                self.add(self.core_rows, slice(None), [got_core[quarter]], quarter)
        elif name == "one":
            for at, lanes in zip(self.one_rows, self.lanes):
                for quarter in range(RANKS):
                    self.add(at, lanes, [got_one[quarter, :, lanes]], quarter)
        elif name == "two":
            for at, lanes in zip(self.two_rows, self.lanes):
                for quarter in range(RANKS):
                    self.add(at, lanes, [got_two[quarter, :, lanes]], quarter)
        elif name == "rank":
            for at, lanes in zip(self.two_rows, self.lanes):
                total = self.buf[self.p.rank, at, lanes].astype(F32)
                for k in range(RANKS - 1):
                    total = total + got_rank[k, :, lanes].astype(F32)
                self.mine[at, lanes] = total.astype(BF)
        elif isinstance(name, int):
            for at, lanes in zip(self.two_rows, self.lanes):
                for quarter in range(RANKS):
                    self.add(at, lanes, [got_more[name, quarter, :, lanes]], quarter)

    def run(self, index):
        self.start(index)
        self.finish(index)


def reduce_copies(bits, everywhere):
    pairs = 2 * (RANKS - 1)
    return 1 + 2 + 2 + 2 * (bits - 3) + pairs + (pairs if everywhere else 0) + 2 + 2 + 1


def reduce_scratch(bits, rows, lanes):
    unit = rows // 8
    return [
        pltpu.VMEM((RANKS, 4 * unit, lanes), BF),
        pltpu.VMEM((RANKS, 2 * unit, lanes), BF),
        pltpu.VMEM((RANKS, unit, lanes), BF),
        pltpu.VMEM((max(bits - 3, 1), RANKS, unit, lanes), BF),
        pltpu.VMEM((RANKS - 1, unit, lanes), BF),
    ]


def char_forward_kernel(slots, x_ref, cnt_lane_ref, cnt_col_ref, gain1_ref, wqkv_ref, wout_ref,
                        gain2_ref, wup_ref, wdown_ref, wproj_ref,
                        lqkv_ref, lout_ref, lup_ref, ldown_ref,
                        vec_ref, pooled_ref, qkv_ref, probs_ref, mixed_ref, first_ref,
                        slope_ref, act_pool_ref, near_ref, wqkv_all, wout_all, wup_all, wdown_all,
                        own_sem, send_sem, recv_sem):
    rows = x_ref.shape[0]
    width = x_ref.shape[1]
    step = pl.program_id(0)
    steps = pl.num_programs(0)
    words = rows // slots
    p = Place()
    pairs = ((lqkv_ref, wqkv_all), (lout_ref, wout_all), (lup_ref, wup_all), (ldown_ref, wdown_all))
    gathers = [Gather(p, mine, whole, Sems(send_sem, recv_sem, gather_copies() * index))
               for index, (mine, whole) in enumerate(pairs)]
    own_copies = [pltpu.make_async_copy(mine, whole.at[p.rank], own_sem.at[index])
                  for index, (mine, whole) in enumerate(pairs)]
    vec_base = gather_copies() * len(pairs)

    def vec_copies(at):
        copies = []
        for slot, offset in ((1, 1), (0, 2)):
            sem = vec_base + 2 * at + slot
            part = rows_at(at * words, words)
            copies.append(remote(vec_ref.at[part], near_ref.at[slot, part],
                                 (send_sem.at[sem], recv_sem.at[sem]), p.ring_device(offset)))
        return copies

    @pl.when(step == 0)
    def _():
        meet([p.ring_device(offset) for offset in (1, 2, 3)] + [p.core_mate, p.x_mate, p.y_mate])
        for copy in own_copies:
            copy.start()

    plan = {at: [] for at in range(CHAR_STEPS)}
    for group, (members, begin) in enumerate((((0, 1), (0, 2, 3, 4)), ((2,), (0, 3, 4, 5)), ((3,), (0, 4, 5, 6)))):
        for stage in range(4):
            for member in members:
                plan[begin[stage]].append((member, stage))
    for at, todo in plan.items():
        if todo:
            @pl.when(step == at)
            def _(todo=todo):
                for member, stage in todo:
                    if stage:
                        gathers[member].wait(stage - 1)
                    gathers[member].start(stage)

    @pl.when(step > 0)
    def _():
        for copy in vec_copies(step - 1):
            copy.start()

    base = x_ref[...].astype(F32)
    unit, _ = norm_parts(base)
    normed = (unit * gain1_ref[...]).astype(BF)
    qkv_ref[...] = nn(normed, wqkv_ref[...]).astype(BF)
    for tile in range(rows // TILE):
        at = pl.ds(tile * TILE, TILE)
        valid = (lax.broadcasted_iota(jnp.int32, (slots, TILE), 0)
                 < cnt_lane_ref[:, tile * TILE:(tile + 1) * TILE])
        for pair in range(CHEADS // 2):
            c0 = pair * TILE
            queries = split_heads(qkv_ref[at, c0:c0 + TILE])
            keys = qkv_ref[at, width + c0:width + c0 + TILE]
            values = split_heads(qkv_ref[at, 2 * width + c0:2 * width + c0 + TILE])
            scores = compact(nt(keys, queries), slots)
            parts = []
            for head in range(2):
                own = jnp.where(valid, scores[:, head * TILE:(head + 1) * TILE], NEG_LARGE)
                top = jnp.max(own, axis=0, keepdims=True)
                weight = jnp.exp((own - top) * (CHD ** -0.5))
                parts.append(weight / jnp.sum(weight, axis=0, keepdims=True))
            probs = jnp.concatenate(parts, axis=1).astype(BF)
            probs_ref[tile, pair] = probs
            mixed_ref[at, c0:c0 + TILE] = tn(stack_lanes(expand(probs, slots)), values).astype(BF)
    first = base + nn(mixed_ref[...], wout_ref[...])
    first_ref[...] = first
    unit2, _ = norm_parts(first)
    normed2 = (unit2 * gain2_ref[...]).astype(BF)
    counts_col = cnt_col_ref[...]
    slot = jnp.bitwise_and(lax.broadcasted_iota(jnp.int32, (rows, 1), 0), slots - 1)
    valid_col = slot < counts_col
    pool = pool_matrix(rows, slots, counts_col).astype(BF)
    chunk = 256
    for part in range(wup_ref.shape[1] // chunk):
        cols = slice(part * chunk, (part + 1) * chunk)
        active, slope = gelu_parts(nn(normed2, wup_ref[:, cols]))
        slope_ref[:, cols] = jnp.where(valid_col, slope, 0.0).astype(BF)
        act_pool_ref[:, cols] = tn(pool, active.astype(BF)).astype(BF)
    pooled = tn(pool, first.astype(BF)) + nn(act_pool_ref[...], wdown_ref[...])
    pooled = pooled.astype(BF)
    pooled_ref[...] = pooled
    vec_ref[rows_at(step * words, words), :] = nn(pooled, wproj_ref[...]).astype(BF)

    @pl.when(step == steps - 1)
    def _():
        for copy in vec_copies(step):
            copy.start()
        for copy in own_copies:
            copy.wait()
        for gather in gathers:
            gather.wait(3)
        for at in range(CHAR_STEPS):
            for copy in vec_copies(at):
                copy.wait()


def char_forward(x, counts, gain1, wqkv, wout, gain2, wup, wdown, wproj, lqkv, lout, lup, ldown):
    rows, width = x.shape
    words = counts.shape[0]
    slots = rows // words
    hidden = wup.shape[1]
    wide = wproj.shape[1]
    step = rows // CHAR_STEPS
    step_words = step // slots
    spread = jnp.repeat(counts, slots)
    row_block = lambda cols: pl.BlockSpec((step, cols), lambda i: (i, 0))
    word_block = lambda cols: pl.BlockSpec((step_words, cols), lambda i: (i, 0))
    whole = lambda shape: pl.BlockSpec(shape, lambda i: (0, 0))
    tiles = step // TILE
    return pl.pallas_call(
        functools.partial(char_forward_kernel, slots),
        grid=(rows // step,),
        in_specs=[
            row_block(width),
            pl.BlockSpec((1, step), lambda i: (0, i)),
            row_block(1),
            whole((1, width)),
            whole((width, 3 * width)),
            whole((width, width)),
            whole((1, width)),
            whole((width, hidden)),
            whole((hidden, width)),
            whole((width, wide)),
            whole(lqkv.shape),
            whole(lout.shape),
            whole(lup.shape),
            whole(ldown.shape),
        ],
        out_specs=[
            whole((words, wide)),
            word_block(width),
            row_block(3 * width),
            pl.BlockSpec((tiles, CHEADS // 2, slots, 2 * TILE), lambda i: (i, 0, 0, 0)),
            row_block(width),
            row_block(width),
            row_block(hidden),
            word_block(hidden),
        ] + [pl.BlockSpec(memory_space=pl.ANY)] * 5,
        out_shape=[
            jax.ShapeDtypeStruct((words, wide), BF),
            jax.ShapeDtypeStruct((words, width), BF),
            jax.ShapeDtypeStruct((rows, 3 * width), BF),
            jax.ShapeDtypeStruct((rows // TILE, CHEADS // 2, slots, 2 * TILE), BF),
            jax.ShapeDtypeStruct((rows, width), BF),
            jax.ShapeDtypeStruct((rows, width), F32),
            jax.ShapeDtypeStruct((rows, hidden), BF),
            jax.ShapeDtypeStruct((words, hidden), BF),
            jax.ShapeDtypeStruct((2, words, wide), BF),
            jax.ShapeDtypeStruct((RANKS,) + lqkv.shape, BF),
            jax.ShapeDtypeStruct((RANKS,) + lout.shape, BF),
            jax.ShapeDtypeStruct((RANKS,) + lup.shape, BF),
            jax.ShapeDtypeStruct((RANKS,) + ldown.shape, BF),
        ],
        scratch_shapes=[
            pltpu.SemaphoreType.DMA((4,)),
            pltpu.SemaphoreType.DMA((gather_copies() * 4 + 2 * CHAR_STEPS,)),
            pltpu.SemaphoreType.DMA((gather_copies() * 4 + 2 * CHAR_STEPS,)),
        ],
        compiler_params=pltpu.CompilerParams(
            vmem_limit_bytes=60 << 20, collective_id=0, has_side_effects=True),
        name="char_forward",
    )(x, spread[None, :], spread[:, None], gain1[None, :], wqkv, wout, gain2[None, :], wup, wdown, wproj,
      lqkv, lout, lup, ldown)


UP, DOWN, OUT, QKV, WORD_ROWS = 0, 512, 1024, 1152, 1536


def word_kernel(bits, vec_ref, near_ref, row_docs_ref, key_docs_ref, cot_ref, wqkv_ref, wout_ref, wup_ref,
                wdown_ref, gain1_ref, gain2_ref, wproj_ref, pooled_ref,
                out_ref, gpl_ref, dproj_ref, dgain_ref, grads_ref,
                n1_ref, q_ref, kv_ref, probs_ref, o_ref, act_ref, slope_ref, go_ref, gq_ref, gkv_ref,
                back_ref, cot_own, cot_sem, part_ref, got_ref, send_sem, recv_sem):
    p = Place()
    words, wide = vec_ref.shape
    window = 3 * words
    fetch = pltpu.make_async_copy(cot_ref.at[rows_at(p.rank * words, words)], cot_own, cot_sem)
    fetch.start()
    meet([p.ring_device(offset) for offset in (1, 2, 3)])

    own = vec_ref[...].astype(F32)
    unit1, rate1 = norm_parts(own)
    n1_ref[2 * words:, :] = (unit1 * gain1_ref[...]).astype(BF)
    for slot in range(2):
        unit, _ = norm_parts(near_ref[slot].astype(F32))
        n1_ref[slot * words:(slot + 1) * words, :] = (unit * gain1_ref[...]).astype(BF)

    def project(rank, carry):
        q_ref[rank] = nn(n1_ref[2 * words:, :], wqkv_ref[rank, :, 0:TILE]).astype(BF)
        kv_ref[rank] = nn(n1_ref[...], wqkv_ref[rank, :, TILE:]).astype(BF)
        scores = nt(split_heads(q_ref[rank]), kv_ref[rank, :, 0:TILE]) * (CHD ** -0.5)
        row = lax.broadcasted_iota(jnp.int32, (words, window), 0)
        key = lax.broadcasted_iota(jnp.int32, (words, window), 1)
        allowed = (row_docs_ref[...] == key_docs_ref[...]) & (key <= row + 2 * words)
        for head in range(2):
            at = slice(head * words, (head + 1) * words)
            masked = jnp.where(allowed, scores[at], NEG_LARGE)
            top = jnp.max(masked, axis=-1, keepdims=True)
            weight = jnp.exp(masked - top)
            probs_ref[rank, at, :] = (weight * (1.0 / jnp.sum(weight, axis=-1, keepdims=True))).astype(BF)
        pair = jnp.concatenate([probs_ref[rank, 0:words, :], probs_ref[rank, words:, :]], axis=1)
        o_ref[rank] = nn(pair, split_heads(kv_ref[rank, :, TILE:])).astype(BF)
        back_ref[...] += nn(o_ref[rank], wout_ref[rank])
        return carry

    back_ref[...] = own
    lax.fori_loop(0, RANKS, project, 0)
    middle = back_ref[...]
    unit2, rate2 = norm_parts(middle)
    normed2 = (unit2 * gain2_ref[...]).astype(BF)

    def feed(rank, carry):
        active, slope = gelu_parts(nn(normed2, wup_ref[rank]))
        act_ref[rank] = active.astype(BF)
        slope_ref[rank] = slope.astype(BF)
        back_ref[...] += nn(act_ref[rank], wdown_ref[rank])
        return carry

    lax.fori_loop(0, RANKS, feed, 0)
    out_ref[...] = back_ref[...].astype(BF)
    fetch.wait()
    back_ref[...] = jnp.zeros_like(back_ref)

    def feed_back(rank, carry):
        upstream = (nt(cot_own[...], wdown_ref[rank]) * slope_ref[rank].astype(F32)).astype(BF)
        back_ref[...] += nt(upstream, wup_ref[rank])
        grads_ref[rank, UP:DOWN, :] = tn(normed2, upstream).astype(BF)
        grads_ref[rank, DOWN:OUT, :] = tn(act_ref[rank], cot_own[...]).astype(BF)
        return carry

    lax.fori_loop(0, RANKS, feed_back, 0)
    upstream2 = back_ref[...]
    dgain_ref[...] = jnp.zeros_like(dgain_ref)
    dgain_ref[1:2, :] = jnp.sum(upstream2 * unit2, axis=0, keepdims=True)
    grad_middle = cot_own[...].astype(F32) + norm_back(upstream2, gain2_ref[...], unit2, rate2)
    middle_low = grad_middle.astype(BF)

    back_ref[...] = jnp.zeros_like(back_ref)
    part_ref[...] = jnp.zeros_like(part_ref)

    def attend_back(rank, carry):
        go_ref[...] = nt(middle_low, wout_ref[rank]).astype(BF)
        grads_ref[rank, OUT:QKV, :] = tn(o_ref[rank], middle_low).astype(BF)
        go_pair = split_heads(go_ref[...])
        grad_probs = nt(go_pair, kv_ref[rank, :, TILE:])
        probs = probs_ref[rank].astype(F32)
        inner = jnp.sum(probs * grad_probs, axis=-1, keepdims=True)
        grad_scores = (probs * (grad_probs - inner) * (CHD ** -0.5)).astype(BF)
        q_pair = split_heads(q_ref[rank])
        gkv_ref[:, 0:TILE] = tn(grad_scores, q_pair).astype(BF)
        gkv_ref[:, TILE:] = tn(probs_ref[rank], go_pair).astype(BF)
        pair = jnp.concatenate([grad_scores[0:words], grad_scores[words:]], axis=1)
        gq_ref[...] = nn(pair, split_heads(kv_ref[rank, :, 0:TILE])).astype(BF)
        part_ref[...] += nt(gkv_ref[0:2 * words, :], wqkv_ref[rank, :, TILE:])
        back_ref[...] += nt(gkv_ref[2 * words:, :], wqkv_ref[rank, :, TILE:])
        back_ref[...] += nt(gq_ref[...], wqkv_ref[rank, :, 0:TILE])
        grads_ref[rank, QKV:QKV + TILE, :] = tn(gq_ref[...], n1_ref[2 * words:, :]).astype(BF)
        grads_ref[rank, QKV + TILE:WORD_ROWS, :] = tn(gkv_ref[...], n1_ref[...]).astype(BF)
        return carry

    lax.fori_loop(0, RANKS, attend_back, 0)
    near_ref_low = got_ref.at[2]
    near_ref_low[...] = part_ref[...].astype(BF).reshape(2, words, wide)
    sends = []
    for slot, offset in ((0, RANKS - 2), (1, RANKS - 1)):
        sends.append(remote(got_ref.at[2, slot], got_ref.at[slot, 0], (send_sem.at[slot], recv_sem.at[slot]),
                            p.ring_device(offset)))
    for copy in sends:
        copy.start()
    for copy in sends:
        copy.wait()
    upstream1 = back_ref[...] + got_ref[0, 0].astype(F32) + got_ref[1, 0].astype(F32)
    dgain_ref[0:1, :] = jnp.sum(upstream1 * unit1, axis=0, keepdims=True)
    grad_vec = (grad_middle + norm_back(upstream1, gain1_ref[...], unit1, rate1)).astype(BF)
    dproj_ref[...] = tn(pooled_ref[...], grad_vec)
    gpl_ref[...] = nt(grad_vec, wproj_ref[...])


def word_layer(bits, vec, near, doc_ids, cotangent, wqkv, wout, wup, wdown, gain1, gain2, wproj, pooled):
    words, wide = vec.shape
    width = pooled.shape[1]
    window = 3 * words
    rank = lax.axis_index("tensor")
    padded = jnp.concatenate([jnp.full((2 * words,), -1, jnp.int32), doc_ids[0]])
    key_docs = lax.dynamic_slice_in_dim(padded, rank * words, window, 0)
    hidden = wup.shape[2]
    vm = pl.BlockSpec(memory_space=pltpu.VMEM)
    return pl.pallas_call(
        functools.partial(word_kernel, bits),
        in_specs=[vm] * 4 + [pl.BlockSpec(memory_space=pl.ANY)] + [vm] * 8,
        out_specs=[vm] * 5,
        out_shape=[
            jax.ShapeDtypeStruct((words, wide), BF),
            jax.ShapeDtypeStruct((words, width), F32),
            jax.ShapeDtypeStruct((width, wide), F32),
            jax.ShapeDtypeStruct((8, wide), F32),
            jax.ShapeDtypeStruct((RANKS, WORD_ROWS, wide), BF),
        ],
        scratch_shapes=[
            pltpu.VMEM((window, wide), BF),
            pltpu.VMEM((RANKS, words, TILE), BF),
            pltpu.VMEM((RANKS, window, 2 * TILE), BF),
            pltpu.VMEM((RANKS, 2 * words, window), BF),
            pltpu.VMEM((RANKS, words, TILE), BF),
            pltpu.VMEM((RANKS, words, hidden), BF),
            pltpu.VMEM((RANKS, words, hidden), BF),
            pltpu.VMEM((words, TILE), BF),
            pltpu.VMEM((words, TILE), BF),
            pltpu.VMEM((window, 2 * TILE), BF),
            pltpu.VMEM((words, wide), F32),
            pltpu.VMEM((words, wide), BF),
            pltpu.SemaphoreType.DMA,
            pltpu.VMEM((2 * words, wide), F32),
            pltpu.VMEM((3, 2, words, wide), BF),
            pltpu.SemaphoreType.DMA((2,)),
            pltpu.SemaphoreType.DMA((2,)),
        ],
        compiler_params=pltpu.CompilerParams(
            vmem_limit_bytes=62 << 20, collective_id=1, has_side_effects=True),
        name="word_layer",
    )(vec, near, key_docs[2 * words:, None], key_docs[None, :], cotangent, wqkv, wout, wup, wdown,
      gain1[None, :], gain2[None, :], wproj, pooled)


def char_backward_kernel(slots, x_ref, cnt_col_ref, inv_ref, gain1_ref, wqkv_ref, wout_ref, gain2_ref,
                         wup_ref, wdown_ref, gpl_ref, act_pool_ref, qkv_ref, probs_ref,
                         mixed_ref, first_ref, slope_ref,
                         dx_ref, dgain_ref, dqkv_ref, dout_ref, dup_ref, ddown_ref,
                         down_ref, gq_ref, gmix_ref, gup_ref, spread_ref):
    step = pl.program_id(0)
    rows, width = x_ref.shape
    words = rows // slots

    @pl.when(step == 0)
    def _():
        dgain_ref[...] = jnp.zeros_like(dgain_ref)
        dqkv_ref[...] = jnp.zeros_like(dqkv_ref)
        dout_ref[...] = jnp.zeros_like(dout_ref)
        dup_ref[...] = jnp.zeros_like(dup_ref)
        low = gpl_ref[...].astype(BF)
        ddown_ref[...] = tn(act_pool_ref[...], low)
        scaled = gpl_ref[...] * inv_ref[...]
        down_ref[:, width:] = nt(scaled.astype(BF), wdown_ref[...])
        down_ref[:, :width] = scaled

    for word in range(words):
        line = down_ref[pl.ds(step * words + word, 1), :width]
        spread_ref[word * slots:(word + 1) * slots, :] = jnp.broadcast_to(line, (slots, width))
        line = down_ref[pl.ds(step * words + word, 1), width:]
        at = slice(word * slots, (word + 1) * slots)
        gup_ref[at, :] = (jnp.broadcast_to(line, (slots, line.shape[1])) * slope_ref[at, :].astype(F32)).astype(BF)

    slot = jnp.bitwise_and(lax.broadcasted_iota(jnp.int32, (rows, 1), 0), slots - 1)
    valid_col = slot < cnt_col_ref[...]
    first = first_ref[...]
    unit2, rate2 = norm_parts(first)
    dup_ref[...] += tn((unit2 * gain2_ref[...]).astype(BF), gup_ref[...])
    upstream = nt(gup_ref[...], wup_ref[...])
    dgain_ref[1:2, :] += jnp.sum(upstream * unit2, axis=0, keepdims=True)
    grad_first = jnp.where(valid_col, spread_ref[...], 0.0) + norm_back(upstream, gain2_ref[...], unit2, rate2)
    spread_ref[...] = grad_first
    low = grad_first.astype(BF)
    dout_ref[...] += tn(mixed_ref[...], low)
    gmix_ref[...] = nt(low, wout_ref[...]).astype(BF)
    for tile in range(rows // TILE):
        at = pl.ds(tile * TILE, TILE)
        for pair in range(CHEADS // 2):
            c0 = pair * TILE
            queries = split_heads(qkv_ref[at, c0:c0 + TILE])
            keys = split_heads(qkv_ref[at, width + c0:width + c0 + TILE])
            values = qkv_ref[at, 2 * width + c0:2 * width + c0 + TILE]
            grads = split_heads(gmix_ref[at, c0:c0 + TILE])
            probs_low = probs_ref[tile, pair]
            probs = probs_low.astype(F32)
            grad_probs = compact(nt(values, grads), slots)
            inner = jnp.sum(probs * grad_probs, axis=0, keepdims=True)
            grad_scores = (probs * (grad_probs - inner) * (CHD ** -0.5)).astype(BF)
            wide_scores = expand(grad_scores, slots)
            wide_probs = expand(probs_low, slots)
            gq_ref[at, c0:c0 + TILE] = tn(stack_lanes(wide_scores), keys).astype(BF)
            gq_ref[at, width + c0:width + c0 + TILE] = nn(wide_scores, queries).astype(BF)
            gq_ref[at, 2 * width + c0:2 * width + c0 + TILE] = nn(wide_probs, grads).astype(BF)
    unit1, rate1 = norm_parts(x_ref[...].astype(F32))
    dqkv_ref[...] += tn((unit1 * gain1_ref[...]).astype(BF), gq_ref[...])
    upstream1 = nt(gq_ref[...], wqkv_ref[...])
    dgain_ref[0:1, :] += jnp.sum(upstream1 * unit1, axis=0, keepdims=True)
    dx_ref[...] = spread_ref[...] + norm_back(upstream1, gain1_ref[...], unit1, rate1)


def char_backward(x, counts, gain1, wqkv, wout, gain2, wup, wdown, grad_pooled, saved):
    qkv, probs, mixed, first, slope, act_pool = saved
    rows, width = x.shape
    words = counts.shape[0]
    slots = rows // words
    hidden = wup.shape[1]
    step = rows // CHAR_STEPS
    spread = jnp.repeat(counts, slots)
    row_block = lambda cols: pl.BlockSpec((step, cols), lambda i: (i, 0))
    whole = lambda shape: pl.BlockSpec(shape, lambda i: (0, 0))
    tiles = step // TILE
    return pl.pallas_call(
        functools.partial(char_backward_kernel, slots),
        grid=(rows // step,),
        in_specs=[
            row_block(width),
            row_block(1),
            whole((words, 1)),
            whole((1, width)),
            whole((width, 3 * width)),
            whole((width, width)),
            whole((1, width)),
            whole((width, hidden)),
            whole((hidden, width)),
            whole((words, width)),
            whole((words, hidden)),
            row_block(3 * width),
            pl.BlockSpec((tiles, CHEADS // 2, slots, 2 * TILE), lambda i: (i, 0, 0, 0)),
            row_block(width),
            row_block(width),
            row_block(hidden),
        ],
        out_specs=[
            row_block(width),
            whole((8, width)),
            whole((width, 3 * width)),
            whole((width, width)),
            whole((width, hidden)),
            whole((hidden, width)),
        ],
        out_shape=[
            jax.ShapeDtypeStruct((rows, width), F32),
            jax.ShapeDtypeStruct((8, width), F32),
            jax.ShapeDtypeStruct((width, 3 * width), F32),
            jax.ShapeDtypeStruct((width, width), F32),
            jax.ShapeDtypeStruct((width, hidden), F32),
            jax.ShapeDtypeStruct((hidden, width), F32),
        ],
        scratch_shapes=[
            pltpu.VMEM((words, width + hidden), F32),
            pltpu.VMEM((step, 3 * width), BF),
            pltpu.VMEM((step, width), BF),
            pltpu.VMEM((step, hidden), BF),
            pltpu.VMEM((step, width), F32),
        ],
        compiler_params=pltpu.CompilerParams(vmem_limit_bytes=60 << 20),
        name="char_backward",
    )(x, spread[:, None], (1.0 / counts.astype(F32))[:, None], gain1[None, :], wqkv, wout, gain2[None, :],
      wup, wdown, grad_pooled, act_pool, qkv, probs, mixed, first, slope)

CHAR_ROWS = 512


def reduce_kernel(bits, word_ref, dgain_ref, dqkv_ref, dout_ref, dup_ref, ddown_ref, dproj_ref, wgain_ref,
                  word_out, char_out, word_buf, char_buf, w1, w2, w3, w4, w5, c1, c2, c3, c4, c5, send_sem, recv_sem, own_sem):
    p = Place()
    meet(p.mates(bits) + [p.ring_device(offset) for offset in (1, 2, 3)])
    fetch = pltpu.make_async_copy(word_ref, word_buf, own_sem)
    fetch.start()
    width = dout_ref.shape[0]
    low = lambda value: value.astype(BF)
    char_buf[0, :, :] = low(jnp.concatenate([dup_ref[:, 0:2 * width], dup_ref[:, 2 * width:]], axis=0))
    char_buf[1, :, :] = low(jnp.concatenate([ddown_ref[0:2 * width, :], ddown_ref[2 * width:, :]], axis=1))
    char_buf[2, 0:width, :] = low(dproj_ref[...])
    char_buf[2, width:, :] = low(dqkv_ref[:, 0:2 * width])
    half = width // 2
    char_buf[3, 0:half, :] = low(jnp.concatenate([dout_ref[0:half, :], dout_ref[half:, :]], axis=1))
    value = dqkv_ref[:, 2 * width:]
    char_buf[3, half:width, :] = low(jnp.concatenate([value[0:half, :], value[half:, :]], axis=1))
    char_buf[3, width:, :] = jnp.zeros_like(char_buf[3, width:, :])
    gains = jnp.concatenate([wgain_ref[...], jnp.concatenate([dgain_ref[...], dgain_ref[...]], axis=1)], axis=0)
    char_buf[3, width:width + 16, :] = low(gains)
    fetch.wait()
    word = Reduce(p, bits, word_buf, word_out, w1, w2, w3, w4, w5, Sems(send_sem, recv_sem), False)
    char = Reduce(p, bits, char_buf, char_out, c1, c2, c3, c4, c5,
                  Sems(send_sem, recv_sem, reduce_copies(bits, False)), True)
    last = len(char.names)
    word.start(0)
    for index in range(last):
        char.start(index)
        if index < len(word.names):
            word.finish(index)
            if index + 1 < len(word.names):
                word.start(index + 1)
        char.finish(index)


def reduce_all(bits, word_grads, dgain, dqkv, dout, dup, ddown, dproj, wgain):
    wide = word_grads.shape[2]
    vm = pl.BlockSpec(memory_space=pltpu.VMEM)
    copies = reduce_copies(bits, False) + reduce_copies(bits, True)
    return pl.pallas_call(
        functools.partial(reduce_kernel, bits),
        in_specs=[pl.BlockSpec(memory_space=pl.ANY)] + [vm] * 7,
        out_specs=[vm, vm],
        out_shape=[
            jax.ShapeDtypeStruct(word_grads.shape[1:], BF),
            jax.ShapeDtypeStruct((RANKS, CHAR_ROWS, wide), BF),
        ],
        scratch_shapes=[pltpu.VMEM(word_grads.shape, BF), pltpu.VMEM((RANKS, CHAR_ROWS, wide), BF)]
        + reduce_scratch(bits, word_grads.shape[1], wide) + reduce_scratch(bits, CHAR_ROWS, wide)
        + [pltpu.SemaphoreType.DMA((copies,)), pltpu.SemaphoreType.DMA((copies,)), pltpu.SemaphoreType.DMA],
        compiler_params=pltpu.CompilerParams(
            vmem_limit_bytes=62 << 20, collective_id=2, has_side_effects=True),
        name="reduce_all",
    )(word_grads, dgain, dqkv, dout, dup, ddown, dproj, wgain)


def per_device(
    bits,
    char_inputs,
    char_counts,
    doc_ids,
    cotangent,
    char_norm_one,
    char_query,
    char_key,
    char_value,
    char_out,
    char_norm_two,
    char_up,
    char_down,
    char_proj,
    word_norm_one,
    word_query,
    word_key,
    word_value,
    word_out_proj,
    word_norm_two,
    word_up,
    word_down,
):
    char_qkv = jnp.concatenate([char_query, char_key, char_value], axis=1)
    word_qkv = jnp.concatenate([word_query, word_key, word_value], axis=1)
    vec, pooled, *saved, near, qkv_all, out_all, up_all, down_all = char_forward(
        char_inputs, char_counts, char_norm_one, char_qkv, char_out, char_norm_two, char_up, char_down, char_proj,
        word_qkv, word_out_proj, word_up, word_down,
    )
    word_output, grad_pooled, grad_proj, word_gains, word_grads = word_layer(
        bits, vec, near, doc_ids, cotangent, qkv_all, out_all, up_all, down_all,
        word_norm_one, word_norm_two, char_proj, pooled,
    )
    char_input_gradient, char_gains, char_dqkv, char_dout, char_dup, char_ddown = char_backward(
        char_inputs, char_counts, char_norm_one, char_qkv, char_out, char_norm_two, char_up, char_down,
        grad_pooled, saved,
    )
    word_sum, char_sum = reduce_all(
        bits, word_grads, char_gains, char_dqkv, char_dout, char_dup, char_ddown, grad_proj, word_gains
    )
    word_sum = word_sum.astype(F32)
    char_sum = char_sum.astype(F32)
    width = char_out.shape[0]
    half = width // 2
    join = lambda rows: jnp.concatenate([rows[:, :width], rows[:, width:]], axis=0)
    gains = char_sum[3, width:]
    return (
        word_output,
        char_input_gradient,
        gains[8, :width],
        char_sum[2, width:, :width],
        char_sum[2, width:, width:],
        join(char_sum[3, half:width]),
        join(char_sum[3, :half]),
        gains[9, :width],
        jnp.concatenate([char_sum[0, :width], char_sum[0, width:]], axis=1),
        join(char_sum[1]),
        char_sum[2, :width],
        gains[0],
        word_sum[QKV:QKV + TILE].T,
        word_sum[QKV + TILE:QKV + 2 * TILE].T,
        word_sum[QKV + 2 * TILE:].T,
        word_sum[OUT:QKV],
        gains[1],
        word_sum[UP:DOWN],
        word_sum[DOWN:OUT],
    )


def solution(mesh):
    in_specs = (
        P(("dp", "tensor"), None),
        P(("dp", "tensor")),
        P("dp", None),
        P("dp", None),
        P(),
        P(),
        P(),
        P(),
        P(),
        P(),
        P(),
        P(),
        P(),
        P(),
        P(None, "tensor"),
        P(None, "tensor"),
        P(None, "tensor"),
        P("tensor", None),
        P(),
        P(None, "tensor"),
        P("tensor", None),
    )
    out_specs = (
        P(("dp", "tensor"), None),
        P(("dp", "tensor"), None),
        P(),
        P(),
        P(),
        P(),
        P(),
        P(),
        P(),
        P(),
        P(),
        P(),
        P(None, "tensor"),
        P(None, "tensor"),
        P(None, "tensor"),
        P("tensor", None),
        P(),
        P(None, "tensor"),
        P("tensor", None),
    )
    assert mesh.shape["tensor"] == RANKS
    bits = mesh.shape["dp"].bit_length() - 1
    assert bits >= 3 and mesh.shape["dp"] == 1 << bits
    return jax.shard_map(
        functools.partial(per_device, bits), mesh=mesh, in_specs=in_specs, out_specs=out_specs, check_vma=False
    )
```

time: 598 us -> 263 us (0.44)
  waiting for transfers between devices: 341 us -> 0 us
  Pallas kernels: 67.7 us -> 233 us
  matrix products: 58.7 us -> 0 us
  blocking collectives: 39.4 us -> 0 us
  other arithmetic: 29.1 us -> 8.79 us
  local copies, waits for them, and re-layouts: 39.4 us -> 20.1 us
  between operations: 14.8 us -> 0.77 us
  loops' own time: 6.74 us -> 0 us
    psum x5 -> x0, waiting for transfers between devices: 310 us -> none  [the longest x1 139 us: per_device(): lax.psum((grad_char_gain_one, grad_char_query, grad_char_key, grad_char_v...]
    pallas_call x0 -> x2, Pallas kernels: none -> 139 us  [the longest x1 96 us: reduce_all(): pl.pallas_call(functools.partial(reduce_kernel, bits), in_specs=[pl.Block...]
    dot_general x34 -> x0, matrix products: 58.7 us -> none  [the longest x6 9.53 us: matmul(): return jnp.dot(left, right, preferred_element_type=jnp.float32)]
    psum x1 -> x0, blocking collectives: 39.4 us -> none  [per_device(): lax.psum((grad_char_gain_one, grad_char_query, grad_char_key, grad_char_v...]
    all_gather x1 -> x0, waiting for transfers between devices: 30.8 us -> none  [per_device(): lax.all_gather(word_vectors, 'tensor', axis=0, tiled=True)]
    pallas_call x1, Pallas kernels: 32.7 us -> 59 us  [char_forward(): pl.pallas_call(functools.partial(char_forward_kernel, slots), grid=(rows...]
    unnamed x131 -> x12, local copies, waits for them, and re-layouts: 21.9 us -> 5.05 us
    reduce_sum x10 -> x0, other arithmetic: 15.5 us -> none  [the longest x3 6.71 us: layer_norm(): return centre * lax.rsqrt(spread + EPSILON) * gain_vector]
  transfers between devices with their start and end apart: 6 -> 0, of which waited for: 5 -> 0; matrix products, arithmetic and copies ran while one was open for 5% -> 0% of each run, Pallas kernels for 6% -> 0%
where the time goes in v2:
time: 263 us
  Pallas kernels  233 us (89%)
  local copies, waits for them, and re-layouts  20.1 us (8%)
  other arithmetic  8.79 us (3%)
    pallas_call x1, Pallas kernels, reduce_all(): pl.pallas_call(functools.partial(reduce_kernel, bits), in_specs=[pl.Block...  96 us
    pallas_call x1, Pallas kernels, char_forward(): pl.pallas_call(functools.partial(char_forward_kernel, slots), grid=(rows...  59 us
    pallas_call x1, Pallas kernels, word_layer(): pl.pallas_call(functools.partial(word_kernel, bits), in_specs=[vm] * 4 +...  42.9 us
    pallas_call x1, Pallas kernels, char_backward(): pl.pallas_call(functools.partial(char_backward_kernel, slots), grid=(rows...  35.1 us

profile of v2, /device:TPU:0, one launch (start us, length us, event | category | flops | bytes accessed | tf_op | source)
XLA Modules:
  0.0 262.7 jit_solution(17549537194789653565)
XLA Ops:
  1.3 0.8 pad_dynamic-slice_fusion
  2.7 0.8 copy.44.row_docs_ref
  3.5 0.8 copy.46.inv_ref
  4.3 0.8 broadcast_in_dim.28
  5.8 0.9 constant_dynamic-update-slice_fusion.2
  6.7 0.9 constant_dynamic-update-slice_fusion.1
  7.6 0.9 constant_dynamic-update-slice_fusion.wqkv_ref
  8.6 2.0 pad_maximum_fusion.2.lqkv_ref
  10.5 2.5 broadcast_in_dim_reshape.9.cnt_col_ref
  13.0 59.0 %char_forward.1 = (bf16[256,512]{1,0:T(8,128)(2,1)}, bf16[256,256]{1,0:T(8,128)(2,1)}, bf16[4096,768]{1,0:T(8,128)(2,1)}, bf16[32,2,16,256]{3,2,1,0:T(8,128)(2,1...) custom-call(bf16[4096,256]{1,0:T(8,128)(2,1)} %x_ref.3, ...), custom_call_target="tpu_custom_call" | custom-call | tf_op jit(solution)/shard_map/char_forward/pallas_call | solution.py:447
  72.1 42.9 %word_layer.1 = (bf16[256,512]{1,0:T(8,128)(2,1)}, f32[256,256]{1,0:T(8,128)}, f32[256,512]{1,0:T(8,128)}, f32[8,512]{1,0:T(8,128)}, bf16[4,1536,512]{2,1,0:T(8,128)(2,1)}) custom-call(bf16[256,512]{1,0:T(8,128)(2,1)} %get-tuple-element.45.vec_ref, bf16[2,256,512]{2,1,0:T(8,128)(2,1)} %get-tuple-element.46.near_ref, s32[256,1]{1,0:T(8,128)} %copy.44.row_docs_ref, ...), custom_call_target="tpu_custom_call" | custom-call | tf_op jit(solution)/shard_map/word_layer/pallas_call | solution.py:625
  115.0 35.1 %char_backward.1 = (f32[4096,256]{1,0:T(8,128)}, f32[8,256]{1,0:T(8,128)}, f32[256,768]{1,0:T(8,128)}, f32[256,256]{1,0:T(8,128)}, f32[256,1024]{1,0:T(8,128)}, /*index=5*/f32[1024,256]{1,0:T(8,128)}) custom-call(bf16[4096,256]{1,0:T(8,128)(2,1)} %x_ref.3, s32[4096,1]{1,0:T(8,128)} %broadcast_in_dim_reshape.9.cnt_col_ref, f32[256,1]{1,0:T(8,128)} %copy.46.inv_ref, ...), custom_call_target="tpu_custom_call" | custom-call | tf_op jit(solution)/shard_map/char_backward/pallas_call | solution.py:738
  150.1 96.0 %reduce_all.1 = (bf16[1536,512]{1,0:T(8,128)(2,1)}, bf16[4,512,512]{2,1,0:T(8,128)(2,1)}) custom-call(bf16[4,1536,512]{2,1,0:T(8,128)(2,1)} %get-tuple-element.61.word_ref, f32[8,256]{1,0:T(8,128)} %get-tuple-element.62.dgain_ref, f32[256,768]{1,0:T(8,128)} %get-tuple-element.63.dqkv_ref, f32[256,256]{1,0:T(8,128)} %get-tuple-element.64.dout_ref, ...), custom_call_target="tpu_custom_call" | custom-call | tf_op jit(solution)/shard_map/reduce_all/pallas_call | solution.py:828
  246.1 1.4 fusion
  247.5 1.6 slice.129
  249.1 2.2 convert_element_type.10
  251.3 0.8 slice_bitcast_fusion.10
  253.7 1.0 slice_bitcast_fusion.1
  254.8 1.0 pad_maximum_fusion.1
  256.4 1.1 pad_maximum_fusion
  257.4 1.6 fusion.1
  259.5 0.8 copy.49
  260.4 0.8 copy.48
  261.2 0.8 copy.47
  (20 shorter events, 5.4 us)
Async XLA Ops:
  8.5 4.5 %copy-start.1 = (bf16[256,768]{1,0:T(8,128)(2,1)}, bf16[256,768]{1,0:T(8,128)(2,1)S(1)}, u32[]{:S(2)}) copy-start(bf16[256,768]{1,0:T(8,128)(2,1)S(1)} %constant_dynamic-update-slice_fusion.wqkv_ref) | copy-start | bytes 1179652
  254.7 2.7 %copy-start = (bf16[1536,512]{1,0:T(8,128)(2,1)S(1)}, bf16[1536,512]{1,0:T(8,128)(2,1)}, u32[]{:S(2)}) copy-start(bf16[1536,512]{1,0:T(8,128)(2,1)} %get-tuple-element.70) | copy-start | bytes 4718596
  259.0 3.0 %copy-start.2 = (bf16[256,512]{1,0:T(8,128)(2,1)S(1)}, bf16[256,512]{1,0:T(8,128)(2,1)}, u32[]{:S(2)}) copy-start(bf16[256,512]{1,0:T(8,128)(2,1)} %get-tuple-element.153) | copy-start | bytes 786436

commit v3 on v2

--- a/solution.py
+++ b/solution.py
@@ -200,121 +200,111 @@
     return 2 * (RANKS - 1) * 3 + (RANKS - 1)
 
 
-class Reduce:
-    def __init__(self, place, bits, buf, out, got_core, got_one, got_two, got_more, got_rank, sems, everywhere):
+class Chain:
+    def __init__(self, place, bits, src, refs, sems, everywhere):
         p = place
-        self.p, self.buf, self.everywhere = p, buf, everywhere
+        buf, got_core, got_one, got_two, got_more, got_rank, out = refs
+        self.p, self.src, self.everywhere = p, src, everywhere
+        self.buf, self.got_core, self.got_one, self.got_two = buf, got_core, got_one, got_two
+        self.got_more, self.got_rank = got_more, got_rank
         self.mine = out.at[p.rank] if everywhere else out
-        self.got = (got_core, got_one, got_two, got_more, got_rank)
-        rows = buf.shape[1]
-        unit = rows // 8
-        self.unit = unit
-        left, right = halves(buf.shape[2])
-        self.lanes = (left, right)
-        half = lambda core: rows_at(core * 4 * unit, 4 * unit)
-        self.core_copy = [remote(buf.at[:, half(1 - p.core)], got_core, sems.take(), p.core_mate)]
-        self.core_rows = half(p.core)
-        quarter_left = lambda x: rows_at((p.core * 4 + x * 2) * unit, 2 * unit)
-        quarter_right = lambda y: rows_at((p.core * 4 + y * 2) * unit, 2 * unit)
-        self.one_copy = [
-            remote(buf.at[:, quarter_left(1 - p.x), left], got_one.at[:, :, left], sems.take(), p.x_mate),
-            remote(buf.at[:, quarter_right(1 - p.y), right], got_one.at[:, :, right], sems.take(), p.y_mate),
-        ]
-        self.one_rows = (quarter_left(p.x), quarter_right(p.y))
-        eighth_left = lambda y: rows_at((p.core * 4 + p.x * 2 + y) * unit, unit)
-        eighth_right = lambda x: rows_at((p.core * 4 + p.y * 2 + x) * unit, unit)
-        self.two_copy = [
-            remote(buf.at[:, eighth_left(1 - p.y), left], got_two.at[:, :, left], sems.take(), p.y_mate),
-            remote(buf.at[:, eighth_right(1 - p.x), right], got_two.at[:, :, right], sems.take(), p.x_mate),
-        ]
-        self.two_rows = (eighth_left(p.y), eighth_right(p.x))
-        self.more_copy = []
+        unit = src.shape[1] // 8
+        lanes = left, right = halves(src.shape[2])
+        self.lanes = lanes
+        self.own = rows_at(p.core * 4 * unit, 4 * unit)
+        stages = [("core", [remote(src.at[:, rows_at((1 - p.core) * 4 * unit, 4 * unit)], got_core,
+                                   sems.take(), p.core_mate)])]
+        first, second = (p.x, p.y), (p.y, p.x)
+        first_mate, second_mate = (p.x_mate, p.y_mate), (p.y_mate, p.x_mate)
+        one = lambda side, at: rows_at(at * 2 * unit, 2 * unit)
+        two = lambda side, at: rows_at((first[side] * 2 + at) * unit, unit)
+        self.one_rows = [one(side, first[side]) for side in (0, 1)]
+        self.two_rows = [two(side, second[side]) for side in (0, 1)]
+        stages.append(("one", [
+            remote(buf.at[:, one(side, 1 - first[side]), lanes[side]], got_one.at[:, :, lanes[side]],
+                   sems.take(), first_mate[side]) for side in (0, 1)]))
+        stages.append(("two", [
+            remote(buf.at[:, two(side, 1 - second[side]), lanes[side]], got_two.at[:, :, lanes[side]],
+                   sems.take(), second_mate[side]) for side in (0, 1)]))
         for bit in range(3, bits):
-            mate = p.bit_mate(bit)
-            self.more_copy.append([
-                remote(buf.at[:, at, lanes], got_more.at[bit - 3, :, :, lanes], sems.take(), mate)
-                for at, lanes in zip(self.two_rows, self.lanes)
-            ])
-        self.rank_copy, self.rank_back = [], []
-        for offset in range(1, RANKS):
-            for at, lanes in zip(self.two_rows, self.lanes):
-                self.rank_copy.append(remote(
-                    buf.at[p.ring(offset), at, lanes], got_rank.at[offset - 1, :, lanes],
-                    sems.take(), p.ring_device(offset)))
+            stages.append((bit - 3, [
+                remote(buf.at[:, self.two_rows[side], lanes[side]], got_more.at[bit - 3, :, :, lanes[side]],
+                       sems.take(), p.bit_mate(bit)) for side in (0, 1)]))
+        stages.append(("rank", [
+            remote(buf.at[p.ring(offset), self.two_rows[side], lanes[side]],
+                   got_rank.at[offset - 1, :, lanes[side]], sems.take(), p.ring_device(offset))
+            for offset in range(1, RANKS) for side in (0, 1)]))
+        base = p.core * 4 * unit
+        self.out_two = [rows_at(base + (first[side] * 2 + second[side]) * unit, unit) for side in (0, 1)]
+        out_one = [rows_at(base + first[side] * 2 * unit, 2 * unit) for side in (0, 1)]
         if everywhere:
-            for offset in range(1, RANKS):
-                for at, lanes in zip(self.two_rows, self.lanes):
-                    self.rank_back.append(remote(
-                        out.at[p.rank, at, lanes], out.at[p.rank, at, lanes], sems.take(), p.ring_device(offset)))
-
-        def back(at, lanes, mate):
-            part = out.at[:, at, lanes] if everywhere else out.at[at, lanes]
+            stages.append(("rank_back", [
+                remote(out.at[p.rank, self.out_two[side], lanes[side]], out.at[p.rank, self.out_two[side], lanes[side]],
+                       sems.take(), p.ring_device(offset))
+                for offset in range(1, RANKS) for side in (0, 1)]))
+
+        def back(at, part_lanes, mate):
+            part = out.at[:, at, part_lanes] if everywhere else out.at[at, part_lanes]
             return remote(part, part, sems.take(), mate)
 
-        self.back_two = [back(self.two_rows[0], left, p.y_mate), back(self.two_rows[1], right, p.x_mate)]
-        self.back_one = [back(self.one_rows[0], left, p.x_mate), back(self.one_rows[1], right, p.y_mate)]
-        self.back_core = [back(self.core_rows, slice(None), p.core_mate)]
-        names = ["core", "one", "two"] + list(range(len(self.more_copy))) + ["rank"]
-        names += ["rank_back"] if everywhere else []
-        self.names = names + ["back_two", "back_one", "back_core"]
-
-    def copies(self, name):
-        if isinstance(name, int):
-            return self.more_copy[name]
-        return {"core": self.core_copy, "one": self.one_copy, "two": self.two_copy, "rank": self.rank_copy,
-                "rank_back": self.rank_back, "back_two": self.back_two, "back_one": self.back_one,
-                "back_core": self.back_core}[name]
-
-    def add(self, at, lanes, terms, who=slice(None)):
-        total = self.buf[who, at, lanes].astype(F32)
-        for term in terms:
-            total = total + term.astype(F32)
-        self.buf[who, at, lanes] = total.astype(BF)
+        stages.append(("back_two", [back(self.out_two[side], lanes[side], second_mate[side]) for side in (0, 1)]))
+        stages.append(("back_one", [back(out_one[side], lanes[side], first_mate[side]) for side in (0, 1)]))
+        stages.append(("back_core", [back(self.own, slice(None), p.core_mate)]))
+        self.stages = stages
+
+    def fetch(self, sem):
+        return pltpu.make_async_copy(self.src.at[:, self.own], self.buf, sem)
 
     def start(self, index):
-        for copy in self.copies(self.names[index]):
+        for copy in self.stages[index][1]:
             copy.start()
 
     def finish(self, index):
-        name = self.names[index]
-        for copy in self.copies(name):
+        name, copies = self.stages[index]
+        for copy in copies:
             copy.wait()
-        got_core, got_one, got_two, got_more, got_rank = self.got
+        buf = self.buf
         if name == "core":
+            own = self.src if self.everywhere else None
             for quarter in range(RANKS):
-                self.add(self.core_rows, slice(None), [got_core[quarter]], quarter)
+                mine = own[quarter, self.own, :] if self.everywhere else buf[quarter]
+                buf[quarter] = mine + self.got_core[quarter]
         elif name == "one":
             for at, lanes in zip(self.one_rows, self.lanes):
                 for quarter in range(RANKS):
-                    self.add(at, lanes, [got_one[quarter, :, lanes]], quarter)
+                    buf[quarter, at, lanes] += self.got_one[quarter, :, lanes]
         elif name == "two":
             for at, lanes in zip(self.two_rows, self.lanes):
                 for quarter in range(RANKS):
-                    self.add(at, lanes, [got_two[quarter, :, lanes]], quarter)
+                    buf[quarter, at, lanes] += self.got_two[quarter, :, lanes]
         elif name == "rank":
-            for at, lanes in zip(self.two_rows, self.lanes):
-                total = self.buf[self.p.rank, at, lanes].astype(F32)
+            for side in (0, 1):
+                at, lanes = self.two_rows[side], self.lanes[side]
+                total = buf[self.p.rank, at, lanes].astype(F32)
                 for k in range(RANKS - 1):
-                    total = total + got_rank[k, :, lanes].astype(F32)
-                self.mine[at, lanes] = total.astype(BF)
+                    total = total + self.got_rank[k, :, lanes].astype(F32)
+                self.mine[self.out_two[side], lanes] = total.astype(BF)
         elif isinstance(name, int):
             for at, lanes in zip(self.two_rows, self.lanes):
                 for quarter in range(RANKS):
-                    self.add(at, lanes, [got_more[name, quarter, :, lanes]], quarter)
-
-    def run(self, index):
-        self.start(index)
-        self.finish(index)
-
-
-def reduce_copies(bits, everywhere):
+                    buf[quarter, at, lanes] += self.got_more[name, quarter, :, lanes]
+
+    def step(self, index):
+        if index:
+            self.finish(index - 1)
+        if index < len(self.stages):
+            self.start(index)
+
+
+def chain_copies(bits, everywhere):
     pairs = 2 * (RANKS - 1)
     return 1 + 2 + 2 + 2 * (bits - 3) + pairs + (pairs if everywhere else 0) + 2 + 2 + 1
 
 
-def reduce_scratch(bits, rows, lanes):
+def chain_scratch(bits, rows, lanes):
     unit = rows // 8
     return [
+        pltpu.VMEM((RANKS, 4 * unit, lanes), BF),
         pltpu.VMEM((RANKS, 4 * unit, lanes), BF),
         pltpu.VMEM((RANKS, 2 * unit, lanes), BF),
         pltpu.VMEM((RANKS, unit, lanes), BF),
@@ -500,12 +490,9 @@
       lqkv, lout, lup, ldown)
 
 
-UP, DOWN, OUT, QKV, WORD_ROWS = 0, 512, 1024, 1152, 1536
-
-
 def word_kernel(bits, vec_ref, near_ref, row_docs_ref, key_docs_ref, cot_ref, wqkv_ref, wout_ref, wup_ref,
                 wdown_ref, gain1_ref, gain2_ref, wproj_ref, pooled_ref,
-                out_ref, gpl_ref, dproj_ref, dgain_ref, grads_ref,
+                out_ref, gpl_ref, dproj_ref, dgain_ref, up_grad_ref, down_grad_ref, mix_grad_ref,
                 n1_ref, q_ref, kv_ref, probs_ref, o_ref, act_ref, slope_ref, go_ref, gq_ref, gkv_ref,
                 back_ref, cot_own, cot_sem, part_ref, got_ref, send_sem, recv_sem):
     p = Place()
@@ -561,8 +548,8 @@
     def feed_back(rank, carry):
         upstream = (nt(cot_own[...], wdown_ref[rank]) * slope_ref[rank].astype(F32)).astype(BF)
         back_ref[...] += nt(upstream, wup_ref[rank])
-        grads_ref[rank, UP:DOWN, :] = tn(normed2, upstream).astype(BF)
-        grads_ref[rank, DOWN:OUT, :] = tn(act_ref[rank], cot_own[...]).astype(BF)
+        up_grad_ref[rank] = tn(normed2, upstream).astype(BF)
+        down_grad_ref[rank] = tn(act_ref[rank], cot_own[...]).astype(BF)
         return carry
 
     lax.fori_loop(0, RANKS, feed_back, 0)
@@ -577,7 +564,7 @@
 
     def attend_back(rank, carry):
         go_ref[...] = nt(middle_low, wout_ref[rank]).astype(BF)
-        grads_ref[rank, OUT:QKV, :] = tn(o_ref[rank], middle_low).astype(BF)
+        mix_grad_ref[rank, :, 3 * TILE:] = tn(middle_low, o_ref[rank]).astype(BF)
         go_pair = split_heads(go_ref[...])
         grad_probs = nt(go_pair, kv_ref[rank, :, TILE:])
         probs = probs_ref[rank].astype(F32)
@@ -591,8 +578,8 @@
         part_ref[...] += nt(gkv_ref[0:2 * words, :], wqkv_ref[rank, :, TILE:])
         back_ref[...] += nt(gkv_ref[2 * words:, :], wqkv_ref[rank, :, TILE:])
         back_ref[...] += nt(gq_ref[...], wqkv_ref[rank, :, 0:TILE])
-        grads_ref[rank, QKV:QKV + TILE, :] = tn(gq_ref[...], n1_ref[2 * words:, :]).astype(BF)
-        grads_ref[rank, QKV + TILE:WORD_ROWS, :] = tn(gkv_ref[...], n1_ref[...]).astype(BF)
+        mix_grad_ref[rank, :, 0:TILE] = tn(n1_ref[2 * words:, :], gq_ref[...]).astype(BF)
+        mix_grad_ref[rank, :, TILE:3 * TILE] = tn(n1_ref[...], gkv_ref[...]).astype(BF)
         return carry
 
     lax.fori_loop(0, RANKS, attend_back, 0)
@@ -609,7 +596,7 @@
     upstream1 = back_ref[...] + got_ref[0, 0].astype(F32) + got_ref[1, 0].astype(F32)
     dgain_ref[0:1, :] = jnp.sum(upstream1 * unit1, axis=0, keepdims=True)
     grad_vec = (grad_middle + norm_back(upstream1, gain1_ref[...], unit1, rate1)).astype(BF)
-    dproj_ref[...] = tn(pooled_ref[...], grad_vec)
+    dproj_ref[...] = tn(pooled_ref[...], grad_vec).astype(BF)
     gpl_ref[...] = nt(grad_vec, wproj_ref[...])
 
 
@@ -625,13 +612,14 @@
     return pl.pallas_call(
         functools.partial(word_kernel, bits),
         in_specs=[vm] * 4 + [pl.BlockSpec(memory_space=pl.ANY)] + [vm] * 8,
-        out_specs=[vm] * 5,
+        out_specs=[vm] * 7,
         out_shape=[
             jax.ShapeDtypeStruct((words, wide), BF),
             jax.ShapeDtypeStruct((words, width), F32),
-            jax.ShapeDtypeStruct((width, wide), F32),
+            jax.ShapeDtypeStruct((width, wide), BF),
             jax.ShapeDtypeStruct((8, wide), F32),
-            jax.ShapeDtypeStruct((RANKS, WORD_ROWS, wide), BF),
+        ] + [
+            jax.ShapeDtypeStruct((RANKS, wide, wide), BF) for _ in range(3)
         ],
         scratch_shapes=[
             pltpu.VMEM((window, wide), BF),
@@ -659,14 +647,59 @@
       gain1[None, :], gain2[None, :], wproj, pooled)
 
 
-def char_backward_kernel(slots, x_ref, cnt_col_ref, inv_ref, gain1_ref, wqkv_ref, wout_ref, gain2_ref,
-                         wup_ref, wdown_ref, gpl_ref, act_pool_ref, qkv_ref, probs_ref,
-                         mixed_ref, first_ref, slope_ref,
-                         dx_ref, dgain_ref, dqkv_ref, dout_ref, dup_ref, ddown_ref,
-                         down_ref, gq_ref, gmix_ref, gup_ref, spread_ref):
+CHAINS = 6
+PLAN = (
+    (0, 2, 5, 7, 9, 10, 11),
+    (0, 4, 7, 9, 11, 12, 13),
+    (1, 6, 9, 11, 13, 14, 15),
+    (1, 3, 6, 8, 10, 12, 13, 14),
+    (8, 10, 12, 14, 15),
+)
+
+
+def char_backward_kernel(slots, bits, x_ref, cnt_col_ref, inv_ref, gain1_ref, wqkv_ref, wout_ref, gain2_ref,
+                         wup_ref, wdown_ref, gpl_ref, act_pool_ref, dproj_ref, wgain_ref, qkv_ref, probs_ref,
+                         mixed_ref, first_ref, slope_ref, up_grad_ref, down_grad_ref, mix_grad_ref,
+                         dx_ref, up_out, down_out, mix_out, early_out, mid_out, late_out,
+                         down_ref, gq_ref, gmix_ref, gup_ref, spread_ref, dgain_ref, dqkv_ref, dout_ref, dup_ref,
+                         early_ref, mid_ref, late_ref, *rest):
     step = pl.program_id(0)
+    steps = pl.num_programs(0)
+    half_steps = CHAR_STEPS
     rows, width = x_ref.shape
     words = rows // slots
+    p = Place()
+    send_sem, recv_sem, own_sem = rest[-3:]
+    sources = (up_grad_ref, down_grad_ref, mix_grad_ref, early_ref, mid_ref, late_ref)
+    results = (up_out, down_out, mix_out, early_out, mid_out, late_out)
+    outs = rest[6 * CHAINS:7 * CHAINS]
+    leave = [pltpu.make_async_copy(out, result, own_sem.at[CHAINS + index])
+             for index, (out, result) in enumerate(zip(outs, results))]
+    word_chains = 3
+    chains, first_sem = [], 0
+    for index in range(CHAINS):
+        everywhere = index >= word_chains
+        refs = tuple(rest[6 * index:6 * index + 6]) + (outs[index],)
+        chains.append(Chain(p, bits, sources[index], refs, Sems(send_sem, recv_sem, first_sem), everywhere))
+        first_sem += chain_copies(bits, everywhere)
+
+    @pl.when(step == 0)
+    def _():
+        meet(p.mates(bits) + [p.ring_device(offset) for offset in (1, 2, 3)])
+        for index in range(word_chains):
+            chains[index].fetch(own_sem.at[index]).start()
+
+    for at in range(2 * half_steps):
+        todo = [(index, stages.index(at)) for index, stages in enumerate(PLAN) if at in stages]
+        if todo:
+            @pl.when(step == at)
+            def _(todo=todo):
+                for index, stage in todo:
+                    if stage == 1 and index < word_chains:
+                        chains[index].fetch(own_sem.at[index]).wait()
+                    chains[index].step(stage)
+
+    low = lambda value: value.astype(BF)
 
     @pl.when(step == 0)
     def _():
@@ -674,73 +707,128 @@
         dqkv_ref[...] = jnp.zeros_like(dqkv_ref)
         dout_ref[...] = jnp.zeros_like(dout_ref)
         dup_ref[...] = jnp.zeros_like(dup_ref)
-        low = gpl_ref[...].astype(BF)
-        ddown_ref[...] = tn(act_pool_ref[...], low)
+        grad_down = low(tn(act_pool_ref[...], low(gpl_ref[...])))
+        quarter = early_ref.shape[1]
+        for index in range(RANKS):
+            early_ref[index, :, 0:width] = grad_down[index * quarter:(index + 1) * quarter]
+            early_ref[index, :, width:] = grad_down[(RANKS + index) * quarter:(RANKS + index + 1) * quarter]
         scaled = gpl_ref[...] * inv_ref[...]
         down_ref[:, width:] = nt(scaled.astype(BF), wdown_ref[...])
         down_ref[:, :width] = scaled
 
-    for word in range(words):
-        line = down_ref[pl.ds(step * words + word, 1), :width]
-        spread_ref[word * slots:(word + 1) * slots, :] = jnp.broadcast_to(line, (slots, width))
-        line = down_ref[pl.ds(step * words + word, 1), width:]
-        at = slice(word * slots, (word + 1) * slots)
-        gup_ref[at, :] = (jnp.broadcast_to(line, (slots, line.shape[1])) * slope_ref[at, :].astype(F32)).astype(BF)
-
-    slot = jnp.bitwise_and(lax.broadcasted_iota(jnp.int32, (rows, 1), 0), slots - 1)
-    valid_col = slot < cnt_col_ref[...]
-    first = first_ref[...]
-    unit2, rate2 = norm_parts(first)
-    dup_ref[...] += tn((unit2 * gain2_ref[...]).astype(BF), gup_ref[...])
-    upstream = nt(gup_ref[...], wup_ref[...])
-    dgain_ref[1:2, :] += jnp.sum(upstream * unit2, axis=0, keepdims=True)
-    grad_first = jnp.where(valid_col, spread_ref[...], 0.0) + norm_back(upstream, gain2_ref[...], unit2, rate2)
-    spread_ref[...] = grad_first
-    low = grad_first.astype(BF)
-    dout_ref[...] += tn(mixed_ref[...], low)
-    gmix_ref[...] = nt(low, wout_ref[...]).astype(BF)
-    for tile in range(rows // TILE):
-        at = pl.ds(tile * TILE, TILE)
-        for pair in range(CHEADS // 2):
-            c0 = pair * TILE
-            queries = split_heads(qkv_ref[at, c0:c0 + TILE])
-            keys = split_heads(qkv_ref[at, width + c0:width + c0 + TILE])
-            values = qkv_ref[at, 2 * width + c0:2 * width + c0 + TILE]
-            grads = split_heads(gmix_ref[at, c0:c0 + TILE])
-            probs_low = probs_ref[tile, pair]
-            probs = probs_low.astype(F32)
-            grad_probs = compact(nt(values, grads), slots)
-            inner = jnp.sum(probs * grad_probs, axis=0, keepdims=True)
-            grad_scores = (probs * (grad_probs - inner) * (CHD ** -0.5)).astype(BF)
-            wide_scores = expand(grad_scores, slots)
-            wide_probs = expand(probs_low, slots)
-            gq_ref[at, c0:c0 + TILE] = tn(stack_lanes(wide_scores), keys).astype(BF)
-            gq_ref[at, width + c0:width + c0 + TILE] = nn(wide_scores, queries).astype(BF)
-            gq_ref[at, 2 * width + c0:2 * width + c0 + TILE] = nn(wide_probs, grads).astype(BF)
-    unit1, rate1 = norm_parts(x_ref[...].astype(F32))
-    dqkv_ref[...] += tn((unit1 * gain1_ref[...]).astype(BF), gq_ref[...])
-    upstream1 = nt(gq_ref[...], wqkv_ref[...])
-    dgain_ref[0:1, :] += jnp.sum(upstream1 * unit1, axis=0, keepdims=True)
-    dx_ref[...] = spread_ref[...] + norm_back(upstream1, gain1_ref[...], unit1, rate1)
-
-
-def char_backward(x, counts, gain1, wqkv, wout, gain2, wup, wdown, grad_pooled, saved):
+    @pl.when(step < half_steps)
+    def _():
+        here = rows_at(step * rows, rows)
+        for word in range(words):
+            line = down_ref[pl.ds(step * words + word, 1), :width]
+            at = slice(word * slots, (word + 1) * slots)
+            gq_ref[at, :width] = jnp.broadcast_to(line, (slots, width))
+            line = down_ref[pl.ds(step * words + word, 1), width:]
+            gup_ref[at, :] = (jnp.broadcast_to(line, (slots, line.shape[1])) * slope_ref[at, :].astype(F32)).astype(BF)
+
+        slot = jnp.bitwise_and(lax.broadcasted_iota(jnp.int32, (rows, 1), 0), slots - 1)
+        valid_col = slot < cnt_col_ref[...]
+        unit2, rate2 = norm_parts(first_ref[...])
+        dup_ref[...] += tn((unit2 * gain2_ref[...]).astype(BF), gup_ref[...])
+        upstream = nt(gup_ref[...], wup_ref[...])
+        dgain_ref[1:2, :] += jnp.sum(upstream * unit2, axis=0, keepdims=True)
+        grad_first = jnp.where(valid_col, gq_ref[:, :width], 0.0) + norm_back(upstream, gain2_ref[...], unit2, rate2)
+        spread_ref[here, :] = grad_first
+        grad_low = low(grad_first)
+        dout_ref[...] += tn(mixed_ref[...], grad_low)
+        gmix_ref[here, :] = low(nt(grad_low, wout_ref[...]))
+
+    @pl.when(step == half_steps - 1)
+    def _():
+        mid_ref[0] = low(dup_ref[:, 0:2 * width])
+        mid_ref[1] = low(dup_ref[:, 2 * width:])
+        mid_ref[2] = dproj_ref[...]
+        half = width // 2
+        mid_ref[3, 0:half, 0:width] = low(dout_ref[0:half, :])
+        mid_ref[3, 0:half, width:] = low(dout_ref[half:, :])
+        mid_ref[3, half:, :] = jnp.zeros_like(mid_ref[3, half:, :])
+        both = jnp.concatenate([dgain_ref[...], dgain_ref[...]], axis=1)
+        mid_ref[3, half:half + 16, :] = low(jnp.concatenate([wgain_ref[...], both], axis=0))
+
+    @pl.when(step >= half_steps)
+    def _():
+        for tile in range(rows // TILE):
+            at = pl.ds(tile * TILE, TILE)
+            here = rows_at((step - half_steps) * rows + tile * TILE, TILE)
+            for pair in range(CHEADS // 2):
+                c0 = pair * TILE
+                queries = split_heads(qkv_ref[at, c0:c0 + TILE])
+                keys = split_heads(qkv_ref[at, width + c0:width + c0 + TILE])
+                values = qkv_ref[at, 2 * width + c0:2 * width + c0 + TILE]
+                grads = split_heads(gmix_ref[here, c0:c0 + TILE])
+                probs_low = probs_ref[tile, pair]
+                probs = probs_low.astype(F32)
+                grad_probs = compact(nt(values, grads), slots)
+                inner = jnp.sum(probs * grad_probs, axis=0, keepdims=True)
+                grad_scores = (probs * (grad_probs - inner) * (CHD ** -0.5)).astype(BF)
+                wide_scores = expand(grad_scores, slots)
+                wide_probs = expand(probs_low, slots)
+                gup_ref[at, c0:c0 + TILE] = tn(stack_lanes(wide_scores), keys).astype(BF)
+                gup_ref[at, width + c0:width + c0 + TILE] = nn(wide_scores, queries).astype(BF)
+                gup_ref[at, 2 * width + c0:2 * width + c0 + TILE] = nn(wide_probs, grads).astype(BF)
+        unit1, rate1 = norm_parts(x_ref[...].astype(F32))
+        grads = gup_ref[:, 0:3 * width]
+        dqkv_ref[...] += tn((unit1 * gain1_ref[...]).astype(BF), grads)
+        upstream1 = nt(grads, wqkv_ref[...])
+        dgain_ref[0:1, :] += jnp.sum(upstream1 * unit1, axis=0, keepdims=True)
+        here = rows_at((step - half_steps) * rows, rows)
+        dx_ref[...] = low(spread_ref[here, :] + norm_back(upstream1, gain1_ref[...], unit1, rate1))
+
+    @pl.when(step == steps - 1)
+    def _():
+        half = width // 2
+        for index in range(2):
+            late_ref[index] = low(dqkv_ref[index * half:(index + 1) * half, 0:2 * width])
+            late_ref[2, :, index * width:(index + 1) * width] = low(dqkv_ref[index * half:(index + 1) * half, 2 * width:])
+        late_ref[3] = jnp.zeros_like(late_ref[3])
+        both = jnp.concatenate([dgain_ref[...], dgain_ref[...]], axis=1)
+        late_ref[3, 0:16, :] = low(jnp.concatenate([both, both], axis=0))
+        done = [len(stages) for stages in PLAN] + [0]
+        while any(done[index] <= len(chains[index].stages) for index in range(CHAINS)):
+            for index in reversed(range(CHAINS)):
+                if done[index] <= len(chains[index].stages):
+                    chains[index].step(done[index])
+                    done[index] += 1
+                    if done[index] > len(chains[index].stages):
+                        leave[index].start()
+        for copy in leave:
+            copy.wait()
+
+
+def char_backward(bits, x, counts, gain1, wqkv, wout, gain2, wup, wdown, grad_pooled, saved, grad_proj,
+                  word_gains, word_grads):
     qkv, probs, mixed, first, slope, act_pool = saved
     rows, width = x.shape
     words = counts.shape[0]
     slots = rows // words
     hidden = wup.shape[1]
+    wide = word_gains.shape[1]
     step = rows // CHAR_STEPS
     spread = jnp.repeat(counts, slots)
-    row_block = lambda cols: pl.BlockSpec((step, cols), lambda i: (i, 0))
-    whole = lambda shape: pl.BlockSpec(shape, lambda i: (0, 0))
+    last = CHAR_STEPS - 1
+    ahead = lambda i: i - (i // CHAR_STEPS) * (i - last)
+    behind = lambda i: (i // CHAR_STEPS) * (i - CHAR_STEPS)
+    ahead_block = lambda cols: pl.BlockSpec((step, cols), lambda i: (ahead(i), 0))
+    behind_block = lambda cols: pl.BlockSpec((step, cols), lambda i: (behind(i), 0))
+    whole = lambda shape: pl.BlockSpec(shape, lambda i: (0,) * len(shape))
     tiles = step // TILE
+    sum_shapes = [(wide, wide)] * 3 + [(RANKS, width // 2, wide), (RANKS, width, wide), (RANKS, width // 2, wide)]
+    sources = [(RANKS,) + shape if len(shape) == 2 else shape for shape in sum_shapes]
+    copies = sum(chain_copies(bits, index >= 3) for index in range(CHAINS))
+    scratch = []
+    for shape in sources:
+        scratch += chain_scratch(bits, shape[1], wide)
     return pl.pallas_call(
-        functools.partial(char_backward_kernel, slots),
-        grid=(rows // step,),
+        functools.partial(char_backward_kernel, slots, bits),
+        grid=(2 * CHAR_STEPS,),
         in_specs=[
-            row_block(width),
-            row_block(1),
+            behind_block(width),
+            ahead_block(1),
             whole((words, 1)),
             whole((1, width)),
             whole((width, 3 * width)),
@@ -750,96 +838,93 @@
             whole((hidden, width)),
             whole((words, width)),
             whole((words, hidden)),
-            row_block(3 * width),
-            pl.BlockSpec((tiles, CHEADS // 2, slots, 2 * TILE), lambda i: (i, 0, 0, 0)),
-            row_block(width),
-            row_block(width),
-            row_block(hidden),
-        ],
-        out_specs=[
-            row_block(width),
-            whole((8, width)),
-            whole((width, 3 * width)),
-            whole((width, width)),
-            whole((width, hidden)),
-            whole((hidden, width)),
-        ],
-        out_shape=[
-            jax.ShapeDtypeStruct((rows, width), F32),
-            jax.ShapeDtypeStruct((8, width), F32),
-            jax.ShapeDtypeStruct((width, 3 * width), F32),
-            jax.ShapeDtypeStruct((width, width), F32),
-            jax.ShapeDtypeStruct((width, hidden), F32),
-            jax.ShapeDtypeStruct((hidden, width), F32),
-        ],
+            whole((width, wide)),
+            whole((8, wide)),
+            behind_block(3 * width),
+            pl.BlockSpec((tiles, CHEADS // 2, slots, 2 * TILE), lambda i: (behind(i), 0, 0, 0)),
+            ahead_block(width),
+            ahead_block(width),
+            ahead_block(hidden),
+        ] + [pl.BlockSpec(memory_space=pl.ANY)] * 3,
+        out_specs=[behind_block(width)] + [pl.BlockSpec(memory_space=pl.ANY)] * CHAINS,
+        out_shape=[jax.ShapeDtypeStruct((rows, width), BF)]
+        + [jax.ShapeDtypeStruct(shape, BF) for shape in sum_shapes],
         scratch_shapes=[
             pltpu.VMEM((words, width + hidden), F32),
-            pltpu.VMEM((step, 3 * width), BF),
-            pltpu.VMEM((step, width), BF),
+            pltpu.VMEM((step, width), F32),
+            pltpu.VMEM((rows, width), BF),
             pltpu.VMEM((step, hidden), BF),
-            pltpu.VMEM((step, width), F32),
-        ],
-        compiler_params=pltpu.CompilerParams(vmem_limit_bytes=60 << 20),
+            pltpu.VMEM((rows, width), F32),
+            pltpu.VMEM((8, width), F32),
+            pltpu.VMEM((width, 3 * width), F32),
+            pltpu.VMEM((width, width), F32),
+            pltpu.VMEM((width, hidden), F32),
+        ] + [pltpu.VMEM(shape, BF) for shape in sources[3:]] + scratch
+        + [pltpu.VMEM(shape, BF) for shape in sum_shapes] + [pltpu.SemaphoreType.DMA((copies,)), pltpu.SemaphoreType.DMA((copies,)), pltpu.SemaphoreType.DMA((2 * CHAINS,))],
+        compiler_params=pltpu.CompilerParams(
+            vmem_limit_bytes=63 << 20, collective_id=2, has_side_effects=True),
         name="char_backward",
     )(x, spread[:, None], (1.0 / counts.astype(F32))[:, None], gain1[None, :], wqkv, wout, gain2[None, :],
-      wup, wdown, grad_pooled, act_pool, qkv, probs, mixed, first, slope)
-
-CHAR_ROWS = 512
-
-
-def reduce_kernel(bits, word_ref, dgain_ref, dqkv_ref, dout_ref, dup_ref, ddown_ref, dproj_ref, wgain_ref,
-                  word_out, char_out, word_buf, char_buf, w1, w2, w3, w4, w5, c1, c2, c3, c4, c5, send_sem, recv_sem, own_sem):
-    p = Place()
-    meet(p.mates(bits) + [p.ring_device(offset) for offset in (1, 2, 3)])
-    fetch = pltpu.make_async_copy(word_ref, word_buf, own_sem)
-    fetch.start()
+      wup, wdown, grad_pooled, act_pool, grad_proj, word_gains, qkv, probs, mixed, first, slope, *word_grads)
+
+
+def unpack_kernel(out_in, dx_in, up_in, down_in, mix_in, early_in, mid_in, late_in,
+                  out_ref, dx_ref, gain1_ref, dq_ref, dk_ref, dv_ref, dout_ref, gain2_ref, dup_ref, ddown_ref, dproj_ref,
+                  wgain1_ref, wq_ref, wk_ref, wv_ref, wout_ref, wgain2_ref, wup_ref, wdown_ref):
+    dx_ref[...] = dx_in[...].astype(F32)
+    out_ref[...] = out_in[...]
     width = dout_ref.shape[0]
-    low = lambda value: value.astype(BF)
-    char_buf[0, :, :] = low(jnp.concatenate([dup_ref[:, 0:2 * width], dup_ref[:, 2 * width:]], axis=0))
-    char_buf[1, :, :] = low(jnp.concatenate([ddown_ref[0:2 * width, :], ddown_ref[2 * width:, :]], axis=1))
-    char_buf[2, 0:width, :] = low(dproj_ref[...])
-    char_buf[2, width:, :] = low(dqkv_ref[:, 0:2 * width])
     half = width // 2
-    char_buf[3, 0:half, :] = low(jnp.concatenate([dout_ref[0:half, :], dout_ref[half:, :]], axis=1))
-    value = dqkv_ref[:, 2 * width:]
-    char_buf[3, half:width, :] = low(jnp.concatenate([value[0:half, :], value[half:, :]], axis=1))
-    char_buf[3, width:, :] = jnp.zeros_like(char_buf[3, width:, :])
-    gains = jnp.concatenate([wgain_ref[...], jnp.concatenate([dgain_ref[...], dgain_ref[...]], axis=1)], axis=0)
-    char_buf[3, width:width + 16, :] = low(gains)
-    fetch.wait()
-    word = Reduce(p, bits, word_buf, word_out, w1, w2, w3, w4, w5, Sems(send_sem, recv_sem), False)
-    char = Reduce(p, bits, char_buf, char_out, c1, c2, c3, c4, c5,
-                  Sems(send_sem, recv_sem, reduce_copies(bits, False)), True)
-    last = len(char.names)
-    word.start(0)
-    for index in range(last):
-        char.start(index)
-        if index < len(word.names):
-            word.finish(index)
-            if index + 1 < len(word.names):
-                word.start(index + 1)
-        char.finish(index)
-
-
-def reduce_all(bits, word_grads, dgain, dqkv, dout, dup, ddown, dproj, wgain):
-    wide = word_grads.shape[2]
-    vm = pl.BlockSpec(memory_space=pltpu.VMEM)
-    copies = reduce_copies(bits, False) + reduce_copies(bits, True)
-    return pl.pallas_call(
-        functools.partial(reduce_kernel, bits),
-        in_specs=[pl.BlockSpec(memory_space=pl.ANY)] + [vm] * 7,
-        out_specs=[vm, vm],
-        out_shape=[
-            jax.ShapeDtypeStruct(word_grads.shape[1:], BF),
-            jax.ShapeDtypeStruct((RANKS, CHAR_ROWS, wide), BF),
-        ],
-        scratch_shapes=[pltpu.VMEM(word_grads.shape, BF), pltpu.VMEM((RANKS, CHAR_ROWS, wide), BF)]
-        + reduce_scratch(bits, word_grads.shape[1], wide) + reduce_scratch(bits, CHAR_ROWS, wide)
-        + [pltpu.SemaphoreType.DMA((copies,)), pltpu.SemaphoreType.DMA((copies,)), pltpu.SemaphoreType.DMA],
-        compiler_params=pltpu.CompilerParams(
-            vmem_limit_bytes=62 << 20, collective_id=2, has_side_effects=True),
-        name="reduce_all",
-    )(word_grads, dgain, dqkv, dout, dup, ddown, dproj, wgain)
+
+    @pl.when(pl.program_id(0) == 0)
+    def _():
+        wup_ref[...] = up_in[...].astype(F32)
+        wdown_ref[...] = down_in[...].astype(F32)
+        wq_ref[...] = mix_in[:, 0:TILE].astype(F32)
+        wk_ref[...] = mix_in[:, TILE:2 * TILE].astype(F32)
+        wv_ref[...] = mix_in[:, 2 * TILE:3 * TILE].astype(F32)
+        wout_ref[...] = mix_in[:, 3 * TILE:].astype(F32).T
+        for index in range(RANKS):
+            quarter = early_in.shape[1]
+            ddown_ref[index * quarter:(index + 1) * quarter, :] = early_in[index, :, 0:width].astype(F32)
+            ddown_ref[(RANKS + index) * quarter:(RANKS + index + 1) * quarter, :] = early_in[index, :, width:].astype(F32)
+        dup_ref[:, 0:2 * width] = mid_in[0].astype(F32)
+        dup_ref[:, 2 * width:] = mid_in[1].astype(F32)
+        dproj_ref[...] = mid_in[2].astype(F32)
+        gains = mid_in[3, half:half + 16, :].astype(F32)
+        wgain1_ref[...] = gains[0:1]
+        wgain2_ref[...] = gains[1:2]
+        gain2_ref[...] = gains[9:10, 0:width]
+        gain1_ref[...] = late_in[3, 0:16, 0:width].astype(F32)[0:1]
+        for index in range(2):
+            at = slice(index * half, (index + 1) * half)
+            cols = slice(index * width, (index + 1) * width)
+            dout_ref[at, :] = mid_in[3, 0:half, cols].astype(F32)
+            dq_ref[at, :] = late_in[index, :, 0:width].astype(F32)
+            dk_ref[at, :] = late_in[index, :, width:].astype(F32)
+            dv_ref[at, :] = late_in[2, :, cols].astype(F32)
+
+
+def unpack(word_output, grad_inputs, sums, width, hidden):
+    steps = 8
+    rows = grad_inputs.shape[0]
+    words, wide = word_output.shape
+    whole = lambda shape: pl.BlockSpec(shape, lambda i: (0,) * len(shape))
+    split = lambda array: pl.BlockSpec((array.shape[0] // steps, array.shape[1]), lambda i: (i, 0))
+    shapes = [(1, width), (width, width), (width, width), (width, width), (width, width), (1, width),
+              (width, hidden), (hidden, width), (width, wide),
+              (1, wide), (wide, TILE), (wide, TILE), (wide, TILE), (TILE, wide), (1, wide), (wide, wide), (wide, wide)]
+    results = pl.pallas_call(
+        unpack_kernel,
+        grid=(steps,),
+        in_specs=[split(word_output), split(grad_inputs)] + [whole(array.shape) for array in sums],
+        out_specs=[split(word_output), split(grad_inputs)] + [whole(shape) for shape in shapes],
+        out_shape=[jax.ShapeDtypeStruct(word_output.shape, BF), jax.ShapeDtypeStruct(grad_inputs.shape, F32)]
+        + [jax.ShapeDtypeStruct(shape, F32) for shape in shapes],
+        compiler_params=pltpu.CompilerParams(vmem_limit_bytes=60 << 20),
+        name="unpack",
+    )(word_output, grad_inputs, *sums)
+    return tuple(array[0] if array.shape[0] == 1 else array for array in results)
 
 
 def per_device(
@@ -872,44 +957,15 @@
         char_inputs, char_counts, char_norm_one, char_qkv, char_out, char_norm_two, char_up, char_down, char_proj,
         word_qkv, word_out_proj, word_up, word_down,
     )
-    word_output, grad_pooled, grad_proj, word_gains, word_grads = word_layer(
+    word_output, grad_pooled, grad_proj, word_gains, *word_grads = word_layer(
         bits, vec, near, doc_ids, cotangent, qkv_all, out_all, up_all, down_all,
         word_norm_one, word_norm_two, char_proj, pooled,
     )
-    char_input_gradient, char_gains, char_dqkv, char_dout, char_dup, char_ddown = char_backward(
-        char_inputs, char_counts, char_norm_one, char_qkv, char_out, char_norm_two, char_up, char_down,
-        grad_pooled, saved,
+    grad_inputs, *sums = char_backward(
+        bits, char_inputs, char_counts, char_norm_one, char_qkv, char_out, char_norm_two, char_up, char_down,
+        grad_pooled, saved, grad_proj, word_gains, word_grads,
     )
-    word_sum, char_sum = reduce_all(
-        bits, word_grads, char_gains, char_dqkv, char_dout, char_dup, char_ddown, grad_proj, word_gains
-    )
-    word_sum = word_sum.astype(F32)
-    char_sum = char_sum.astype(F32)
-    width = char_out.shape[0]
-    half = width // 2
-    join = lambda rows: jnp.concatenate([rows[:, :width], rows[:, width:]], axis=0)
-    gains = char_sum[3, width:]
-    return (
-        word_output,
-        char_input_gradient,
-        gains[8, :width],
-        char_sum[2, width:, :width],
-        char_sum[2, width:, width:],
-        join(char_sum[3, half:width]),
-        join(char_sum[3, :half]),
-        gains[9, :width],
-        jnp.concatenate([char_sum[0, :width], char_sum[0, width:]], axis=1),
-        join(char_sum[1]),
-        char_sum[2, :width],
-        gains[0],
-        word_sum[QKV:QKV + TILE].T,
-        word_sum[QKV + TILE:QKV + 2 * TILE].T,
-        word_sum[QKV + 2 * TILE:].T,
-        word_sum[OUT:QKV],
-        gains[1],
-        word_sum[UP:DOWN],
-        word_sum[DOWN:OUT],
-    )
+    return unpack(word_output, grad_inputs, sums, char_out.shape[0], char_up.shape[1])
 
 
 def solution(mesh):

time: 263 us -> 215 us (0.82)
  Pallas kernels: 233 us -> 207 us
  local copies, waits for them, and re-layouts: 20.1 us -> 6.38 us
  other arithmetic: 8.79 us -> 0.8 us
    pallas_call x2, Pallas kernels: 131 us -> 105 us  [the longest x1 94.6 us: char_backward(): pl.pallas_call(functools.partial(char_backward_kernel, slots, bits), grid...]
    slice x6 -> x0, local copies, waits for them, and re-layouts: 5.27 us -> none  [the longest x1 1.63 us: per_device(): word_sum[OUT:QKV]]
    unnamed x12 -> x20, local copies, waits for them, and re-layouts: 5.05 us -> 0.06 us
    concatenate x4 -> x0, other arithmetic: 3.53 us -> none  [the longest x3 2.48 us: per_device(): jnp.concatenate([rows[:, :width], rows[:, width:]], axis=0)]
where the time goes in v3:
time: 215 us
  Pallas kernels  207 us (96%)
  local copies, waits for them, and re-layouts  6.38 us (3%)
    pallas_call x1, Pallas kernels, char_backward(): pl.pallas_call(functools.partial(char_backward_kernel, slots, bits), grid...  94.6 us
    pallas_call x1, Pallas kernels, char_forward(): pl.pallas_call(functools.partial(char_forward_kernel, slots), grid=(rows...  58.9 us
    pallas_call x1, Pallas kernels, word_layer(): pl.pallas_call(functools.partial(word_kernel, bits), in_specs=[vm] * 4 +...  43.4 us
    pallas_call x1, Pallas kernels, unpack(): pl.pallas_call(unpack_kernel, grid=(steps,), in_specs=[split(word_output)...  9.99 us

profile of v3, /device:TPU:0, one launch (start us, length us, event | category | flops | bytes accessed | tf_op | source)
XLA Modules:
  0.0 215.1 jit_solution(3194669675766654801)
XLA Ops:
  0.7 0.0 copy-start.1
  0.7 0.0 copy-start.2
  0.7 0.0 copy-start.3
  0.7 0.0 copy-start.6
  0.7 0.0 copy-start.5
  0.7 0.0 copy-start.4
  0.7 0.9 broadcast_in_dim.28
  1.6 2.5 %broadcast_in_dim_reshape.9.cnt_col_ref = s32[4096,1]{1,0:T(8,128)} reshape(s32[256,16]{1,0:T(8,128)S(1)} %broadcast_in_dim.28) | data formatting | bytes 32768 | tf_op jit(solution)/shard_map/broadcast_in_dim;reshape | solution.py:489
  4.0 0.0 copy-done.1
  4.1 0.0 copy-done.2
  4.1 0.0 copy-done.3
  4.1 0.0 copy-start
  4.1 0.7 broadcast_in_dim_reshape.7.cnt_lane_ref
  4.9 0.0 copy-done.6
  4.9 0.8 pad_maximum_fusion.lqkv_ref
  5.7 58.9 %char_forward.1 = (bf16[256,512]{1,0:T(8,128)(2,1)}, bf16[256,256]{1,0:T(8,128)(2,1)}, bf16[4096,768]{1,0:T(8,128)(2,1)}, bf16[32,2,16,256]{3,2,1,0:T(8,128)(2,1...) custom-call(bf16[4096,256]{1,0:T(8,128)(2,1)} %x_ref.3, ...), custom_call_target="tpu_custom_call" | custom-call | tf_op jit(solution)/shard_map/char_forward/pallas_call | solution.py:437
  64.6 0.0 copy-done.8
  64.6 0.1 pad_dynamic-slice_fusion
  64.7 0.8 copy.41.row_docs_ref
  65.5 0.6 broadcast_in_dim.32.key_docs_ref
  66.1 43.4 %word_layer.1 = (bf16[256,512]{1,0:T(8,128)(2,1)}, f32[256,256]{1,0:T(8,128)}, bf16[256,512]{1,0:T(8,128)(2,1)}, f32[8,512]{1,0:T(8,128)}, bf16[4,512,512]{2,1,0...) custom-call(bf16[256,512]{1,0:T(8,128)(2,1)} %get-tuple-element.65.vec_ref, ...), custom_call_target="tpu_custom_call" | custom-call | tf_op jit(solution)/shard_map/word_layer/pallas_call | solution.py:612
  109.5 0.8 copy.43.inv_ref
  110.3 94.6 %char_backward.1 = (bf16[4096,256]{1,0:T(8,128)(2,1)}, bf16[512,512]{1,0:T(8,128)(2,1)}, bf16[512,512]{1,0:T(8,128)(2,1)}, bf16[512,512]{1,0:T(8,128)(2,1)}, bf1...) custom-call(bf16[4096,256]{1,0:T(8,128)(2,1)} %x_ref.3, ...), custom_call_target="tpu_custom_call" | custom-call | tf_op jit(solution)/shard_map/char_backward/pallas_call | solution.py:826
  205.0 10.0 %unpack.1 = (bf16[256,512]{1,0:T(8,128)(2,1)}, f32[4096,256]{1,0:T(8,128)}, f32[1,256]{1,0:T(1,128)}, f32[256,256]{1,0:T(8,128)}, f32[256,256]{1,0:T(8,128)}, /*...) custom-call(bf16[256,512]{1,0:T(8,128)(2,1)} %get-tuple-element.72.o, ...), custom_call_target="tpu_custom_call" | custom-call | tf_op jit(solution)/shard_map/unpack/pallas_call | solution.py:917
  (11 shorter events, 0.1 us)
Async XLA Ops:
  0.7 3.4 %copy-start.1 = (bf16[256,256]{1,0:T(8,128)(2,1)S(1)}, bf16[256,256]{1,0:T(8,128)(2,1)}, u32[]{:S(2)}) copy-start(bf16[256,256]{1,0:T(8,128)(2,1)} %param.26) | copy-start | bytes 393220
  0.7 3.4 %copy-start.2 = (bf16[256,256]{1,0:T(8,128)(2,1)S(1)}, bf16[256,256]{1,0:T(8,128)(2,1)}, u32[]{:S(2)}) copy-start(bf16[256,256]{1,0:T(8,128)(2,1)} %param.27) | copy-start | bytes 393220
  0.7 3.4 %copy-start.3 = (bf16[256,256]{1,0:T(8,128)(2,1)S(1)}, bf16[256,256]{1,0:T(8,128)(2,1)}, u32[]{:S(2)}) copy-start(bf16[256,256]{1,0:T(8,128)(2,1)} %param.28) | copy-start | bytes 393220
  0.7 4.2 %copy-start.6 = (bf16[512,128]{1,0:T(8,128)(2,1)S(1)}, bf16[512,128]{1,0:T(8,128)(2,1)}, u32[]{:S(2)}) copy-start(bf16[512,128]{1,0:T(8,128)(2,1)} %param.35) | copy-start | bytes 393220
  0.7 4.2 %copy-start.5 = (bf16[512,128]{1,0:T(8,128)(2,1)S(1)}, bf16[512,128]{1,0:T(8,128)(2,1)}, u32[]{:S(2)}) copy-start(bf16[512,128]{1,0:T(8,128)(2,1)} %param.36) | copy-start | bytes 393220
  0.7 4.2 %copy-start.4 = (bf16[512,128]{1,0:T(8,128)(2,1)S(1)}, bf16[512,128]{1,0:T(8,128)(2,1)}, u32[]{:S(2)}) copy-start(bf16[512,128]{1,0:T(8,128)(2,1)} %param.37) | copy-start | bytes 393220
  4.1 1.5 copy-start
  5.7 59.0 %copy-start.8 = (s32[1,1024]{1,0:T(1,128)S(1)}, s32[1,1024]{1,0:T(1,128)}, u32[]{:S(2)}) copy-start(s32[1,1024]{1,0:T(1,128)} %param.23) | copy-start | bytes 12292
  66.1 43.4 %copy-start.7 = (s32[256]{0:T(256)S(1)}, s32[256]{0:T(256)}, u32[]{:S(2)}) copy-start(s32[256]{0:T(256)} %param.22) | copy-start | bytes 3076

commit v4 on v3

--- a/solution.py
+++ b/solution.py
@@ -649,11 +649,12 @@
 
 CHAINS = 6
 PLAN = (
-    (0, 2, 5, 7, 9, 10, 11),
-    (0, 4, 7, 9, 11, 12, 13),
-    (1, 6, 9, 11, 13, 14, 15),
-    (1, 3, 6, 8, 10, 12, 13, 14),
-    (8, 10, 12, 14, 15),
+    (0, 1, 4, 7, 10, 12, 13),
+    (0, 2, 7, 10, 13, 14, 15),
+    (1, 5, 9, 12, 15, 16, 17),
+    (2, 6, 8, 9, 11, 12, 14, 15),
+    (8, 10, 12, 13, 15, 16, 17, 18),
+    (16, 17, 19, 20, 23),
 )
 
 
@@ -662,7 +663,7 @@
                          mixed_ref, first_ref, slope_ref, up_grad_ref, down_grad_ref, mix_grad_ref,
                          dx_ref, up_out, down_out, mix_out, early_out, mid_out, late_out,
                          down_ref, gq_ref, gmix_ref, gup_ref, spread_ref, dgain_ref, dqkv_ref, dout_ref, dup_ref,
-                         early_ref, mid_ref, late_ref, *rest):
+                         all_ref, early_ref, mid_ref, late_ref, *rest):
     step = pl.program_id(0)
     steps = pl.num_programs(0)
     half_steps = CHAR_STEPS
@@ -689,7 +690,7 @@
         for index in range(word_chains):
             chains[index].fetch(own_sem.at[index]).start()
 
-    for at in range(2 * half_steps):
+    for at in range(3 * half_steps):
         todo = [(index, stages.index(at)) for index, stages in enumerate(PLAN) if at in stages]
         if todo:
             @pl.when(step == at)
@@ -750,11 +751,12 @@
         both = jnp.concatenate([dgain_ref[...], dgain_ref[...]], axis=1)
         mid_ref[3, half:half + 16, :] = low(jnp.concatenate([wgain_ref[...], both], axis=0))
 
-    @pl.when(step >= half_steps)
-    def _():
+    @pl.when((step >= half_steps) & (step < 2 * half_steps))
+    def _():
+        base = (step - half_steps) * rows
         for tile in range(rows // TILE):
             at = pl.ds(tile * TILE, TILE)
-            here = rows_at((step - half_steps) * rows + tile * TILE, TILE)
+            here = rows_at(base + tile * TILE, TILE)
             for pair in range(CHEADS // 2):
                 c0 = pair * TILE
                 queries = split_heads(qkv_ref[at, c0:c0 + TILE])
@@ -768,27 +770,30 @@
                 grad_scores = (probs * (grad_probs - inner) * (CHD ** -0.5)).astype(BF)
                 wide_scores = expand(grad_scores, slots)
                 wide_probs = expand(probs_low, slots)
-                gup_ref[at, c0:c0 + TILE] = tn(stack_lanes(wide_scores), keys).astype(BF)
-                gup_ref[at, width + c0:width + c0 + TILE] = nn(wide_scores, queries).astype(BF)
-                gup_ref[at, 2 * width + c0:2 * width + c0 + TILE] = nn(wide_probs, grads).astype(BF)
-        unit1, rate1 = norm_parts(x_ref[...].astype(F32))
-        grads = gup_ref[:, 0:3 * width]
-        dqkv_ref[...] += tn((unit1 * gain1_ref[...]).astype(BF), grads)
-        upstream1 = nt(grads, wqkv_ref[...])
-        dgain_ref[0:1, :] += jnp.sum(upstream1 * unit1, axis=0, keepdims=True)
-        here = rows_at((step - half_steps) * rows, rows)
-        dx_ref[...] = low(spread_ref[here, :] + norm_back(upstream1, gain1_ref[...], unit1, rate1))
-
-    @pl.when(step == steps - 1)
+                all_ref[here, c0:c0 + TILE] = tn(stack_lanes(wide_scores), keys).astype(BF)
+                all_ref[here, width + c0:width + c0 + TILE] = nn(wide_scores, queries).astype(BF)
+                all_ref[here, 2 * width + c0:2 * width + c0 + TILE] = nn(wide_probs, grads).astype(BF)
+        unit1, _ = norm_parts(x_ref[...].astype(F32))
+        dqkv_ref[...] += tn((unit1 * gain1_ref[...]).astype(BF), all_ref[rows_at(base, rows), :])
+
+    @pl.when(step == 2 * half_steps - 1)
     def _():
         half = width // 2
         for index in range(2):
             late_ref[index] = low(dqkv_ref[index * half:(index + 1) * half, 0:2 * width])
             late_ref[2, :, index * width:(index + 1) * width] = low(dqkv_ref[index * half:(index + 1) * half, 2 * width:])
         late_ref[3] = jnp.zeros_like(late_ref[3])
-        both = jnp.concatenate([dgain_ref[...], dgain_ref[...]], axis=1)
-        late_ref[3, 0:16, :] = low(jnp.concatenate([both, both], axis=0))
-        done = [len(stages) for stages in PLAN] + [0]
+
+    @pl.when(step >= 2 * half_steps)
+    def _():
+        here = rows_at((step - 2 * half_steps) * rows, rows)
+        unit1, rate1 = norm_parts(x_ref[...].astype(F32))
+        upstream1 = nt(all_ref[here, :], wqkv_ref[...])
+        dx_ref[...] = low(spread_ref[here, :] + norm_back(upstream1, gain1_ref[...], unit1, rate1))
+
+    @pl.when(step == steps - 1)
+    def _():
+        done = [len(stages) for stages in PLAN]
         while any(done[index] <= len(chains[index].stages) for index in range(CHAINS)):
             for index in reversed(range(CHAINS)):
                 if done[index] <= len(chains[index].stages):
@@ -811,8 +816,10 @@
     step = rows // CHAR_STEPS
     spread = jnp.repeat(counts, slots)
     last = CHAR_STEPS - 1
-    ahead = lambda i: i - (i // CHAR_STEPS) * (i - last)
-    behind = lambda i: (i // CHAR_STEPS) * (i - CHAR_STEPS)
+    ahead = lambda i: i - ((i // CHAR_STEPS + 1) // 2) * (i - last)
+    behind = lambda i: (i // CHAR_STEPS % 2) * (i - CHAR_STEPS) + (i // CHAR_STEPS // 2) * last
+    inputs = lambda i: (i % CHAR_STEPS) * ((i // CHAR_STEPS + 1) // 2)
+    final = lambda i: (i // CHAR_STEPS // 2) * (i - 2 * CHAR_STEPS)
     ahead_block = lambda cols: pl.BlockSpec((step, cols), lambda i: (ahead(i), 0))
     behind_block = lambda cols: pl.BlockSpec((step, cols), lambda i: (behind(i), 0))
     whole = lambda shape: pl.BlockSpec(shape, lambda i: (0,) * len(shape))
@@ -825,9 +832,9 @@
         scratch += chain_scratch(bits, shape[1], wide)
     return pl.pallas_call(
         functools.partial(char_backward_kernel, slots, bits),
-        grid=(2 * CHAR_STEPS,),
+        grid=(3 * CHAR_STEPS,),
         in_specs=[
-            behind_block(width),
+            pl.BlockSpec((step, width), lambda i: (inputs(i), 0)),
             ahead_block(1),
             whole((words, 1)),
             whole((1, width)),
@@ -846,7 +853,7 @@
             ahead_block(width),
             ahead_block(hidden),
         ] + [pl.BlockSpec(memory_space=pl.ANY)] * 3,
-        out_specs=[behind_block(width)] + [pl.BlockSpec(memory_space=pl.ANY)] * CHAINS,
+        out_specs=[pl.BlockSpec((step, width), lambda i: (final(i), 0))] + [pl.BlockSpec(memory_space=pl.ANY)] * CHAINS,
         out_shape=[jax.ShapeDtypeStruct((rows, width), BF)]
         + [jax.ShapeDtypeStruct(shape, BF) for shape in sum_shapes],
         scratch_shapes=[
@@ -859,6 +866,7 @@
             pltpu.VMEM((width, 3 * width), F32),
             pltpu.VMEM((width, width), F32),
             pltpu.VMEM((width, hidden), F32),
+            pltpu.VMEM((rows, 3 * width), BF),
         ] + [pltpu.VMEM(shape, BF) for shape in sources[3:]] + scratch
         + [pltpu.VMEM(shape, BF) for shape in sum_shapes] + [pltpu.SemaphoreType.DMA((copies,)), pltpu.SemaphoreType.DMA((copies,)), pltpu.SemaphoreType.DMA((2 * CHAINS,))],
         compiler_params=pltpu.CompilerParams(
@@ -868,7 +876,7 @@
       wup, wdown, grad_pooled, act_pool, grad_proj, word_gains, qkv, probs, mixed, first, slope, *word_grads)
 
 
-def unpack_kernel(out_in, dx_in, up_in, down_in, mix_in, early_in, mid_in, late_in,
+def unpack_kernel(out_in, dx_in, wqkv_in, gain1_in, up_in, down_in, mix_in, early_in, mid_in, late_in,
                   out_ref, dx_ref, gain1_ref, dq_ref, dk_ref, dv_ref, dout_ref, gain2_ref, dup_ref, ddown_ref, dproj_ref,
                   wgain1_ref, wq_ref, wk_ref, wv_ref, wout_ref, wgain2_ref, wup_ref, wdown_ref):
     dx_ref[...] = dx_in[...].astype(F32)
@@ -895,7 +903,17 @@
         wgain1_ref[...] = gains[0:1]
         wgain2_ref[...] = gains[1:2]
         gain2_ref[...] = gains[9:10, 0:width]
-        gain1_ref[...] = late_in[3, 0:16, 0:width].astype(F32)[0:1]
+        parts = []
+        for index in range(2):
+            at = slice(index * half, (index + 1) * half)
+            cols = slice(index * width, (index + 1) * width)
+            own = wqkv_in[at, 0:2 * width].astype(F32) * late_in[index].astype(F32)
+            last = wqkv_in[at, 2 * width:].astype(F32) * late_in[2, :, cols].astype(F32)
+            parts.append(jnp.sum(own, axis=1, keepdims=True) + jnp.sum(last, axis=1, keepdims=True))
+        column = jnp.concatenate(parts, axis=0)
+        diagonal = (lax.broadcasted_iota(jnp.int32, (width, width), 0)
+                    == lax.broadcasted_iota(jnp.int32, (width, width), 1))
+        gain1_ref[...] = jnp.sum(jnp.where(diagonal, column, 0.0), axis=0, keepdims=True) / gain1_in[...]
         for index in range(2):
             at = slice(index * half, (index + 1) * half)
             cols = slice(index * width, (index + 1) * width)
@@ -905,7 +923,7 @@
             dv_ref[at, :] = late_in[2, :, cols].astype(F32)
 
 
-def unpack(word_output, grad_inputs, sums, width, hidden):
+def unpack(word_output, grad_inputs, char_qkv, gain1, sums, width, hidden):
     steps = 8
     rows = grad_inputs.shape[0]
     words, wide = word_output.shape
@@ -917,13 +935,13 @@
     results = pl.pallas_call(
         unpack_kernel,
         grid=(steps,),
-        in_specs=[split(word_output), split(grad_inputs)] + [whole(array.shape) for array in sums],
+        in_specs=[split(word_output), split(grad_inputs), whole(char_qkv.shape), whole((1, width))] + [whole(array.shape) for array in sums],
         out_specs=[split(word_output), split(grad_inputs)] + [whole(shape) for shape in shapes],
         out_shape=[jax.ShapeDtypeStruct(word_output.shape, BF), jax.ShapeDtypeStruct(grad_inputs.shape, F32)]
         + [jax.ShapeDtypeStruct(shape, F32) for shape in shapes],
         compiler_params=pltpu.CompilerParams(vmem_limit_bytes=60 << 20),
         name="unpack",
-    )(word_output, grad_inputs, *sums)
+    )(word_output, grad_inputs, char_qkv, gain1[None, :], *sums)
     return tuple(array[0] if array.shape[0] == 1 else array for array in results)
 
 
@@ -965,7 +983,7 @@
         bits, char_inputs, char_counts, char_norm_one, char_qkv, char_out, char_norm_two, char_up, char_down,
         grad_pooled, saved, grad_proj, word_gains, word_grads,
     )
-    return unpack(word_output, grad_inputs, sums, char_out.shape[0], char_up.shape[1])
+    return unpack(word_output, grad_inputs, char_qkv, char_norm_one, sums, char_out.shape[0], char_up.shape[1])
 
 
 def solution(mesh):

time: 215 us -> 219 us (1.019)
  Pallas kernels: 207 us -> 211 us
    pallas_call x1, Pallas kernels: 94.6 us -> 97.8 us  [char_backward(): pl.pallas_call(functools.partial(char_backward_kernel, slots, bits), grid...]
where the time goes in v4:
time: 219 us
  Pallas kernels  211 us (96%)
  local copies, waits for them, and re-layouts  6.38 us (3%)
    pallas_call x1, Pallas kernels, char_backward(): pl.pallas_call(functools.partial(char_backward_kernel, slots, bits), grid...  97.8 us
    pallas_call x1, Pallas kernels, char_forward(): pl.pallas_call(functools.partial(char_forward_kernel, slots), grid=(rows...  58.9 us
    pallas_call x1, Pallas kernels, word_layer(): pl.pallas_call(functools.partial(word_kernel, bits), in_specs=[vm] * 4 +...  43.4 us
    pallas_call x1, Pallas kernels, unpack(): pl.pallas_call(unpack_kernel, grid=(steps,), in_specs=[split(word_output)...  10.4 us

profile of v4, /device:TPU:0, one launch (start us, length us, event | category | flops | bytes accessed | tf_op | source)
XLA Modules:
  0.0 218.7 jit_solution(8193702115387381247)
XLA Ops:
  0.7 0.0 copy-start.1
  0.7 0.0 copy-start.2
  0.7 0.0 copy-start.3
  0.7 0.0 copy-start.6
  0.7 0.0 copy-start.5
  0.7 0.0 copy-start.4
  0.7 0.9 broadcast_in_dim.29
  1.6 2.5 %broadcast_in_dim_reshape.9.cnt_col_ref = s32[4096,1]{1,0:T(8,128)} reshape(s32[256,16]{1,0:T(8,128)S(1)} %broadcast_in_dim.29) | data formatting | bytes 32768 | tf_op jit(solution)/shard_map/broadcast_in_dim;reshape | solution.py:489
  4.0 0.0 copy-done.1
  4.1 0.0 copy-done.2
  4.1 0.0 copy-done.3
  4.1 0.0 copy-start
  4.1 0.7 broadcast_in_dim_reshape.7.cnt_lane_ref
  4.9 0.0 copy-done.4
  4.9 0.8 pad_maximum_fusion.lqkv_ref
  5.7 0.0 copy-done
  5.7 58.9 %char_forward.1 = (bf16[256,512]{1,0:T(8,128)(2,1)}, bf16[256,256]{1,0:T(8,128)(2,1)}, bf16[4096,768]{1,0:T(8,128)(2,1)}, bf16[32,2,16,256]{3,2,1,0:T(8,128)(2,1...) custom-call(bf16[4096,256]{1,0:T(8,128)(2,1)} %x_ref.3, ...), custom_call_target="tpu_custom_call" | custom-call | tf_op jit(solution)/shard_map/char_forward/pallas_call | solution.py:437
  64.6 0.1 pad_dynamic-slice_fusion
  64.7 0.8 copy.41.row_docs_ref
  65.5 0.6 broadcast_in_dim.33.key_docs_ref
  66.1 43.4 %word_layer.1 = (bf16[256,512]{1,0:T(8,128)(2,1)}, f32[256,256]{1,0:T(8,128)}, bf16[256,512]{1,0:T(8,128)(2,1)}, f32[8,512]{1,0:T(8,128)}, bf16[4,512,512]{2,1,0...) custom-call(bf16[256,512]{1,0:T(8,128)(2,1)} %get-tuple-element.65.vec_ref, ...), custom_call_target="tpu_custom_call" | custom-call | tf_op jit(solution)/shard_map/word_layer/pallas_call | solution.py:612
  109.5 0.8 copy.43.inv_ref
  110.3 97.8 %char_backward.1 = (bf16[4096,256]{1,0:T(8,128)(2,1)}, bf16[512,512]{1,0:T(8,128)(2,1)}, bf16[512,512]{1,0:T(8,128)(2,1)}, bf16[512,512]{1,0:T(8,128)(2,1)}, bf1...) custom-call(bf16[4096,256]{1,0:T(8,128)(2,1)} %x_ref.3, ...), custom_call_target="tpu_custom_call" | custom-call | tf_op jit(solution)/shard_map/char_backward/pallas_call | solution.py:833
  208.2 10.4 %unpack.1 = (bf16[256,512]{1,0:T(8,128)(2,1)}, f32[4096,256]{1,0:T(8,128)}, f32[1,256]{1,0:T(1,128)}, f32[256,256]{1,0:T(8,128)}, f32[256,256]{1,0:T(8,128)}, /*...) custom-call(bf16[256,512]{1,0:T(8,128)(2,1)} %get-tuple-element.72.o, ...), custom_call_target="tpu_custom_call" | custom-call | tf_op jit(solution)/shard_map/unpack/pallas_call | solution.py:935
  (11 shorter events, 0.1 us)
Async XLA Ops:
  0.7 3.4 %copy-start.1 = (bf16[256,256]{1,0:T(8,128)(2,1)S(1)}, bf16[256,256]{1,0:T(8,128)(2,1)}, u32[]{:S(2)}) copy-start(bf16[256,256]{1,0:T(8,128)(2,1)} %param.26) | copy-start | bytes 393220
  0.7 3.4 %copy-start.2 = (bf16[256,256]{1,0:T(8,128)(2,1)S(1)}, bf16[256,256]{1,0:T(8,128)(2,1)}, u32[]{:S(2)}) copy-start(bf16[256,256]{1,0:T(8,128)(2,1)} %param.27) | copy-start | bytes 393220
  0.7 3.4 %copy-start.3 = (bf16[256,256]{1,0:T(8,128)(2,1)S(1)}, bf16[256,256]{1,0:T(8,128)(2,1)}, u32[]{:S(2)}) copy-start(bf16[256,256]{1,0:T(8,128)(2,1)} %param.28) | copy-start | bytes 393220
  0.7 4.2 %copy-start.6 = (bf16[512,128]{1,0:T(8,128)(2,1)S(1)}, bf16[512,128]{1,0:T(8,128)(2,1)}, u32[]{:S(2)}) copy-start(bf16[512,128]{1,0:T(8,128)(2,1)} %param.35) | copy-start | bytes 393220
  0.7 4.2 %copy-start.5 = (bf16[512,128]{1,0:T(8,128)(2,1)S(1)}, bf16[512,128]{1,0:T(8,128)(2,1)}, u32[]{:S(2)}) copy-start(bf16[512,128]{1,0:T(8,128)(2,1)} %param.36) | copy-start | bytes 393220
  0.7 4.1 %copy-start.4 = (bf16[512,128]{1,0:T(8,128)(2,1)S(1)}, bf16[512,128]{1,0:T(8,128)(2,1)}, u32[]{:S(2)}) copy-start(bf16[512,128]{1,0:T(8,128)(2,1)} %param.37) | copy-start | bytes 393220
  4.1 1.5 copy-start
  5.7 58.9 %copy-start.8 = (s32[1,1024]{1,0:T(1,128)S(1)}, s32[1,1024]{1,0:T(1,128)}, u32[]{:S(2)}) copy-start(s32[1,1024]{1,0:T(1,128)} %param.23) | copy-start | bytes 12292
  66.1 43.4 %copy-start.7 = (s32[256]{0:T(256)S(1)}, s32[256]{0:T(256)}, u32[]{:S(2)}) copy-start(s32[256]{0:T(256)} %param.22) | copy-start | bytes 3076

commit v5 on v4

--- a/solution.py
+++ b/solution.py
@@ -86,12 +86,33 @@
     return jnp.concatenate([pair[:, :TILE], pair[:, TILE:]], axis=0)
 
 
-def pool_matrix(rows, slots, counts_col):
+def split_counts(counts_ref, table_ref, words):
+    for step in range(CHAR_STEPS):
+        table_ref[step:step + 1, 0:words] = counts_ref[:, step * words:(step + 1) * words]
+
+
+def valid_slots(rows, slots, mine):
     words = rows // slots
     row = lax.broadcasted_iota(jnp.int32, (rows, words), 0)
     word = lax.broadcasted_iota(jnp.int32, (rows, words), 1)
-    mine = (row // slots == word) & (jnp.bitwise_and(row, slots - 1) < counts_col)
-    return jnp.where(mine, 1.0 / counts_col.astype(F32), 0.0)
+    return (row // slots == word) & (jnp.bitwise_and(row, slots - 1) < mine)
+
+
+def join_lanes(parts, whole_ref):
+    width = parts[0].shape[1]
+    for index, part in enumerate(parts):
+        whole_ref[:, index * width:(index + 1) * width] = part[...]
+
+
+def any_lane(mask):
+    return jnp.max(jnp.where(mask, 1.0, 0.0), axis=1, keepdims=True) > 0.0
+
+
+def column(row):
+    size = row.shape[1]
+    diagonal = (lax.broadcasted_iota(jnp.int32, (size, size), 0)
+                == lax.broadcasted_iota(jnp.int32, (size, size), 1))
+    return jnp.sum(jnp.where(diagonal, row, 0.0), axis=1, keepdims=True)
 
 
 MESH = pl.DeviceIdType.MESH
@@ -313,12 +334,22 @@
     ]
 
 
-def char_forward_kernel(slots, x_ref, cnt_lane_ref, cnt_col_ref, gain1_ref, wqkv_ref, wout_ref,
+FORWARD_PLAN = {
+    2: ((0, 1), (1, 1)),
+    3: ((2, 1), (0, 2), (1, 2)),
+    4: ((3, 1), (2, 2)),
+    5: ((0, 3), (1, 3), (3, 2)),
+    6: ((2, 3),),
+    7: ((3, 3),),
+}
+
+
+def char_forward_kernel(slots, x_ref, counts_ref, gain1_ref, wq_ref, wk_ref, wv_ref, wout_ref,
                         gain2_ref, wup_ref, wdown_ref, wproj_ref,
-                        lqkv_ref, lout_ref, lup_ref, ldown_ref,
+                        lq_ref, lk_ref, lv_ref, lout_ref, lup_ref, ldown_ref,
                         vec_ref, pooled_ref, qkv_ref, probs_ref, mixed_ref, first_ref,
                         slope_ref, act_pool_ref, near_ref, wqkv_all, wout_all, wup_all, wdown_all,
-                        own_sem, send_sem, recv_sem):
+                        wqkv_ref, lqkv_ref, table_ref, own_sem, send_sem, recv_sem):
     rows = x_ref.shape[0]
     width = x_ref.shape[1]
     step = pl.program_id(0)
@@ -343,37 +374,28 @@
 
     @pl.when(step == 0)
     def _():
+        join_lanes((lq_ref, lk_ref, lv_ref), lqkv_ref)
+        join_lanes((wq_ref, wk_ref, wv_ref), wqkv_ref)
         meet([p.ring_device(offset) for offset in (1, 2, 3)] + [p.core_mate, p.x_mate, p.y_mate])
+        split_counts(counts_ref, table_ref, words)
         for copy in own_copies:
             copy.start()
-
-    plan = {at: [] for at in range(CHAR_STEPS)}
-    for group, (members, begin) in enumerate((((0, 1), (0, 2, 3, 4)), ((2,), (0, 3, 4, 5)), ((3,), (0, 4, 5, 6)))):
-        for stage in range(4):
-            for member in members:
-                plan[begin[stage]].append((member, stage))
-    for at, todo in plan.items():
-        if todo:
-            @pl.when(step == at)
-            def _(todo=todo):
-                for member, stage in todo:
-                    if stage:
-                        gathers[member].wait(stage - 1)
-                    gathers[member].start(stage)
-
-    @pl.when(step > 0)
-    def _():
-        for copy in vec_copies(step - 1):
-            copy.start()
+        for gather in gathers:
+            gather.start(0)
 
     base = x_ref[...].astype(F32)
     unit, _ = norm_parts(base)
     normed = (unit * gain1_ref[...]).astype(BF)
     qkv_ref[...] = nn(normed, wqkv_ref[...]).astype(BF)
+    mine = table_ref[pl.ds(step, 1), 0:words]
+    word_at = lax.broadcasted_iota(jnp.int32, (words, rows), 0)
+    row_at = lax.broadcasted_iota(jnp.int32, (words, rows), 1)
+    onto_rows = jnp.where(row_at // slots == word_at, 1.0, 0.0).astype(BF)
+    row_counts = nn(jnp.broadcast_to(mine.astype(F32), (16, words)).astype(BF), onto_rows)[0:1]
     for tile in range(rows // TILE):
         at = pl.ds(tile * TILE, TILE)
-        valid = (lax.broadcasted_iota(jnp.int32, (slots, TILE), 0)
-                 < cnt_lane_ref[:, tile * TILE:(tile + 1) * TILE])
+        valid = (lax.broadcasted_iota(jnp.int32, (slots, TILE), 0).astype(F32)
+                 < row_counts[:, tile * TILE:(tile + 1) * TILE])
         for pair in range(CHEADS // 2):
             c0 = pair * TILE
             queries = split_heads(qkv_ref[at, c0:c0 + TILE])
@@ -389,14 +411,26 @@
             probs = jnp.concatenate(parts, axis=1).astype(BF)
             probs_ref[tile, pair] = probs
             mixed_ref[at, c0:c0 + TILE] = tn(stack_lanes(expand(probs, slots)), values).astype(BF)
+
+    for at, todo in FORWARD_PLAN.items():
+        @pl.when(step == at)
+        def _(todo=todo):
+            for member, stage in todo:
+                gathers[member].wait(stage - 1)
+                gathers[member].start(stage)
+
+    @pl.when(step > 0)
+    def _():
+        for copy in vec_copies(step - 1):
+            copy.start()
+
     first = base + nn(mixed_ref[...], wout_ref[...])
     first_ref[...] = first
     unit2, _ = norm_parts(first)
     normed2 = (unit2 * gain2_ref[...]).astype(BF)
-    counts_col = cnt_col_ref[...]
-    slot = jnp.bitwise_and(lax.broadcasted_iota(jnp.int32, (rows, 1), 0), slots - 1)
-    valid_col = slot < counts_col
-    pool = pool_matrix(rows, slots, counts_col).astype(BF)
+    members = valid_slots(rows, slots, mine)
+    valid_col = any_lane(members)
+    pool = jnp.where(members, 1.0 / mine.astype(F32), 0.0).astype(BF)
     chunk = 256
     for part in range(wup_ref.shape[1] // chunk):
         cols = slice(part * chunk, (part + 1) * chunk)
@@ -421,7 +455,7 @@
                 copy.wait()
 
 
-def char_forward(x, counts, gain1, wqkv, wout, gain2, wup, wdown, wproj, lqkv, lout, lup, ldown):
+def char_forward(x, counts, gain1, weights, wout, gain2, wup, wdown, wproj, local, lout, lup, ldown):
     rows, width = x.shape
     words = counts.shape[0]
     slots = rows // words
@@ -429,7 +463,6 @@
     wide = wproj.shape[1]
     step = rows // CHAR_STEPS
     step_words = step // slots
-    spread = jnp.repeat(counts, slots)
     row_block = lambda cols: pl.BlockSpec((step, cols), lambda i: (i, 0))
     word_block = lambda cols: pl.BlockSpec((step_words, cols), lambda i: (i, 0))
     whole = lambda shape: pl.BlockSpec(shape, lambda i: (0, 0))
@@ -439,16 +472,19 @@
         grid=(rows // step,),
         in_specs=[
             row_block(width),
-            pl.BlockSpec((1, step), lambda i: (0, i)),
-            row_block(1),
+            whole((1, words)),
             whole((1, width)),
-            whole((width, 3 * width)),
+            whole((width, width)),
+            whole((width, width)),
+            whole((width, width)),
             whole((width, width)),
             whole((1, width)),
             whole((width, hidden)),
             whole((hidden, width)),
             whole((width, wide)),
-            whole(lqkv.shape),
+            whole(local[0].shape),
+            whole(local[0].shape),
+            whole(local[0].shape),
             whole(lout.shape),
             whole(lup.shape),
             whole(ldown.shape),
@@ -473,12 +509,15 @@
             jax.ShapeDtypeStruct((rows, hidden), BF),
             jax.ShapeDtypeStruct((words, hidden), BF),
             jax.ShapeDtypeStruct((2, words, wide), BF),
-            jax.ShapeDtypeStruct((RANKS,) + lqkv.shape, BF),
+            jax.ShapeDtypeStruct((RANKS, wide, 3 * TILE), BF),
             jax.ShapeDtypeStruct((RANKS,) + lout.shape, BF),
             jax.ShapeDtypeStruct((RANKS,) + lup.shape, BF),
             jax.ShapeDtypeStruct((RANKS,) + ldown.shape, BF),
         ],
         scratch_shapes=[
+            pltpu.VMEM((width, 3 * width), BF),
+            pltpu.VMEM((wide, 3 * TILE), BF),
+            pltpu.VMEM((CHAR_STEPS, TILE), jnp.int32),
             pltpu.SemaphoreType.DMA((4,)),
             pltpu.SemaphoreType.DMA((gather_copies() * 4 + 2 * CHAR_STEPS,)),
             pltpu.SemaphoreType.DMA((gather_copies() * 4 + 2 * CHAR_STEPS,)),
@@ -486,15 +525,15 @@
         compiler_params=pltpu.CompilerParams(
             vmem_limit_bytes=60 << 20, collective_id=0, has_side_effects=True),
         name="char_forward",
-    )(x, spread[None, :], spread[:, None], gain1[None, :], wqkv, wout, gain2[None, :], wup, wdown, wproj,
-      lqkv, lout, lup, ldown)
-
-
-def word_kernel(bits, vec_ref, near_ref, row_docs_ref, key_docs_ref, cot_ref, wqkv_ref, wout_ref, wup_ref,
+    )(x, counts[None, :], gain1[None, :], *weights, wout, gain2[None, :], wup, wdown, wproj,
+      *local, lout, lup, ldown)
+
+
+def word_kernel(bits, vec_ref, near_ref, docs_ref, cot_ref, wqkv_ref, wout_ref, wup_ref,
                 wdown_ref, gain1_ref, gain2_ref, wproj_ref, pooled_ref,
                 out_ref, gpl_ref, dproj_ref, dgain_ref, up_grad_ref, down_grad_ref, mix_grad_ref,
                 n1_ref, q_ref, kv_ref, probs_ref, o_ref, act_ref, slope_ref, go_ref, gq_ref, gkv_ref,
-                back_ref, cot_own, cot_sem, part_ref, got_ref, send_sem, recv_sem):
+                back_ref, cot_own, cot_sem, part_ref, got_ref, table_ref, send_sem, recv_sem):
     p = Place()
     words, wide = vec_ref.shape
     window = 3 * words
@@ -502,6 +541,12 @@
     fetch.start()
     meet([p.ring_device(offset) for offset in (1, 2, 3)])
 
+    table_ref[:, 0:2 * words] = jnp.full((1, 2 * words), -1, jnp.int32)
+    table_ref[:, 2 * words:] = docs_ref[...]
+    start = pl.multiple_of(p.rank * words, TILE)
+    key_docs = table_ref[:, pl.ds(start, window)].astype(F32)
+    row_docs = column(key_docs[:, 2 * words:])
+
     own = vec_ref[...].astype(F32)
     unit1, rate1 = norm_parts(own)
     n1_ref[2 * words:, :] = (unit1 * gain1_ref[...]).astype(BF)
@@ -515,7 +560,7 @@
         scores = nt(split_heads(q_ref[rank]), kv_ref[rank, :, 0:TILE]) * (CHD ** -0.5)
         row = lax.broadcasted_iota(jnp.int32, (words, window), 0)
         key = lax.broadcasted_iota(jnp.int32, (words, window), 1)
-        allowed = (row_docs_ref[...] == key_docs_ref[...]) & (key <= row + 2 * words)
+        allowed = (row_docs == key_docs) & (key <= row + 2 * words)
         for head in range(2):
             at = slice(head * words, (head + 1) * words)
             masked = jnp.where(allowed, scores[at], NEG_LARGE)
@@ -604,14 +649,11 @@
     words, wide = vec.shape
     width = pooled.shape[1]
     window = 3 * words
-    rank = lax.axis_index("tensor")
-    padded = jnp.concatenate([jnp.full((2 * words,), -1, jnp.int32), doc_ids[0]])
-    key_docs = lax.dynamic_slice_in_dim(padded, rank * words, window, 0)
     hidden = wup.shape[2]
     vm = pl.BlockSpec(memory_space=pltpu.VMEM)
     return pl.pallas_call(
         functools.partial(word_kernel, bits),
-        in_specs=[vm] * 4 + [pl.BlockSpec(memory_space=pl.ANY)] + [vm] * 8,
+        in_specs=[vm] * 3 + [pl.BlockSpec(memory_space=pl.ANY)] + [vm] * 8,
         out_specs=[vm] * 7,
         out_shape=[
             jax.ShapeDtypeStruct((words, wide), BF),
@@ -637,33 +679,34 @@
             pltpu.SemaphoreType.DMA,
             pltpu.VMEM((2 * words, wide), F32),
             pltpu.VMEM((3, 2, words, wide), BF),
+            pltpu.VMEM((1, 2 * words + doc_ids.shape[1]), jnp.int32),
             pltpu.SemaphoreType.DMA((2,)),
             pltpu.SemaphoreType.DMA((2,)),
         ],
         compiler_params=pltpu.CompilerParams(
             vmem_limit_bytes=62 << 20, collective_id=1, has_side_effects=True),
         name="word_layer",
-    )(vec, near, key_docs[2 * words:, None], key_docs[None, :], cotangent, wqkv, wout, wup, wdown,
+    )(vec, near, doc_ids, cotangent, wqkv, wout, wup, wdown,
       gain1[None, :], gain2[None, :], wproj, pooled)
 
 
 CHAINS = 6
 PLAN = (
-    (0, 1, 4, 7, 10, 12, 13),
-    (0, 2, 7, 10, 13, 14, 15),
-    (1, 5, 9, 12, 15, 16, 17),
-    (2, 6, 8, 9, 11, 12, 14, 15),
-    (8, 10, 12, 13, 15, 16, 17, 18),
-    (16, 17, 19, 20, 23),
+    (0, 2, 7, 10, 14, 16, 20,),
+    (1, 5, 10, 13, 18, 22,),
+    (2, 11, 15, 19,),
+    (1, 4, 9, 12, 15, 19,),
+    (7, 9, 14, 16,),
+    (15, 17, 22,),
 )
 
 
-def char_backward_kernel(slots, bits, x_ref, cnt_col_ref, inv_ref, gain1_ref, wqkv_ref, wout_ref, gain2_ref,
+def char_backward_kernel(slots, bits, x_ref, counts_ref, gain1_ref, wq_ref, wk_ref, wv_ref, wout_ref, gain2_ref,
                          wup_ref, wdown_ref, gpl_ref, act_pool_ref, dproj_ref, wgain_ref, qkv_ref, probs_ref,
                          mixed_ref, first_ref, slope_ref, up_grad_ref, down_grad_ref, mix_grad_ref,
                          dx_ref, up_out, down_out, mix_out, early_out, mid_out, late_out,
                          down_ref, gq_ref, gmix_ref, gup_ref, spread_ref, dgain_ref, dqkv_ref, dout_ref, dup_ref,
-                         all_ref, early_ref, mid_ref, late_ref, *rest):
+                         all_ref, wqkv_ref, table_ref, early_ref, mid_ref, late_ref, *rest):
     step = pl.program_id(0)
     steps = pl.num_programs(0)
     half_steps = CHAR_STEPS
@@ -690,16 +733,6 @@
         for index in range(word_chains):
             chains[index].fetch(own_sem.at[index]).start()
 
-    for at in range(3 * half_steps):
-        todo = [(index, stages.index(at)) for index, stages in enumerate(PLAN) if at in stages]
-        if todo:
-            @pl.when(step == at)
-            def _(todo=todo):
-                for index, stage in todo:
-                    if stage == 1 and index < word_chains:
-                        chains[index].fetch(own_sem.at[index]).wait()
-                    chains[index].step(stage)
-
     low = lambda value: value.astype(BF)
 
     @pl.when(step == 0)
@@ -713,7 +746,9 @@
         for index in range(RANKS):
             early_ref[index, :, 0:width] = grad_down[index * quarter:(index + 1) * quarter]
             early_ref[index, :, width:] = grad_down[(RANKS + index) * quarter:(RANKS + index + 1) * quarter]
-        scaled = gpl_ref[...] * inv_ref[...]
+        split_counts(counts_ref, table_ref, words)
+        join_lanes((wq_ref, wk_ref, wv_ref), wqkv_ref)
+        scaled = gpl_ref[...] * (1.0 / column(counts_ref[...].astype(F32)))
         down_ref[:, width:] = nt(scaled.astype(BF), wdown_ref[...])
         down_ref[:, :width] = scaled
 
@@ -727,8 +762,7 @@
             line = down_ref[pl.ds(step * words + word, 1), width:]
             gup_ref[at, :] = (jnp.broadcast_to(line, (slots, line.shape[1])) * slope_ref[at, :].astype(F32)).astype(BF)
 
-        slot = jnp.bitwise_and(lax.broadcasted_iota(jnp.int32, (rows, 1), 0), slots - 1)
-        valid_col = slot < cnt_col_ref[...]
+        valid_col = any_lane(valid_slots(rows, slots, table_ref[pl.ds(step, 1), 0:words]))
         unit2, rate2 = norm_parts(first_ref[...])
         dup_ref[...] += tn((unit2 * gain2_ref[...]).astype(BF), gup_ref[...])
         upstream = nt(gup_ref[...], wup_ref[...])
@@ -791,6 +825,16 @@
         upstream1 = nt(all_ref[here, :], wqkv_ref[...])
         dx_ref[...] = low(spread_ref[here, :] + norm_back(upstream1, gain1_ref[...], unit1, rate1))
 
+    for at in range(3 * half_steps):
+        todo = [(index, stages.index(at)) for index, stages in reversed(list(enumerate(PLAN))) if at in stages]
+        if todo:
+            @pl.when(step == at)
+            def _(todo=todo):
+                for index, stage in todo:
+                    if stage == 1 and index < word_chains:
+                        chains[index].fetch(own_sem.at[index]).wait()
+                    chains[index].step(stage)
+
     @pl.when(step == steps - 1)
     def _():
         done = [len(stages) for stages in PLAN]
@@ -805,7 +849,7 @@
             copy.wait()
 
 
-def char_backward(bits, x, counts, gain1, wqkv, wout, gain2, wup, wdown, grad_pooled, saved, grad_proj,
+def char_backward(bits, x, counts, gain1, weights, wout, gain2, wup, wdown, grad_pooled, saved, grad_proj,
                   word_gains, word_grads):
     qkv, probs, mixed, first, slope, act_pool = saved
     rows, width = x.shape
@@ -814,7 +858,6 @@
     hidden = wup.shape[1]
     wide = word_gains.shape[1]
     step = rows // CHAR_STEPS
-    spread = jnp.repeat(counts, slots)
     last = CHAR_STEPS - 1
     ahead = lambda i: i - ((i // CHAR_STEPS + 1) // 2) * (i - last)
     behind = lambda i: (i // CHAR_STEPS % 2) * (i - CHAR_STEPS) + (i // CHAR_STEPS // 2) * last
@@ -835,10 +878,11 @@
         grid=(3 * CHAR_STEPS,),
         in_specs=[
             pl.BlockSpec((step, width), lambda i: (inputs(i), 0)),
-            ahead_block(1),
-            whole((words, 1)),
+            whole((1, words)),
             whole((1, width)),
-            whole((width, 3 * width)),
+            whole((width, width)),
+            whole((width, width)),
+            whole((width, width)),
             whole((width, width)),
             whole((1, width)),
             whole((width, hidden)),
@@ -867,16 +911,18 @@
             pltpu.VMEM((width, width), F32),
             pltpu.VMEM((width, hidden), F32),
             pltpu.VMEM((rows, 3 * width), BF),
+            pltpu.VMEM((width, 3 * width), BF),
+            pltpu.VMEM((CHAR_STEPS, TILE), jnp.int32),
         ] + [pltpu.VMEM(shape, BF) for shape in sources[3:]] + scratch
         + [pltpu.VMEM(shape, BF) for shape in sum_shapes] + [pltpu.SemaphoreType.DMA((copies,)), pltpu.SemaphoreType.DMA((copies,)), pltpu.SemaphoreType.DMA((2 * CHAINS,))],
         compiler_params=pltpu.CompilerParams(
             vmem_limit_bytes=63 << 20, collective_id=2, has_side_effects=True),
         name="char_backward",
-    )(x, spread[:, None], (1.0 / counts.astype(F32))[:, None], gain1[None, :], wqkv, wout, gain2[None, :],
+    )(x, counts[None, :], gain1[None, :], *weights, wout, gain2[None, :],
       wup, wdown, grad_pooled, act_pool, grad_proj, word_gains, qkv, probs, mixed, first, slope, *word_grads)
 
 
-def unpack_kernel(out_in, dx_in, wqkv_in, gain1_in, up_in, down_in, mix_in, early_in, mid_in, late_in,
+def unpack_kernel(out_in, dx_in, wq_in, wk_in, wv_in, gain1_in, up_in, down_in, mix_in, early_in, mid_in, late_in,
                   out_ref, dx_ref, gain1_ref, dq_ref, dk_ref, dv_ref, dout_ref, gain2_ref, dup_ref, ddown_ref, dproj_ref,
                   wgain1_ref, wq_ref, wk_ref, wv_ref, wout_ref, wgain2_ref, wup_ref, wdown_ref):
     dx_ref[...] = dx_in[...].astype(F32)
@@ -907,13 +953,14 @@
         for index in range(2):
             at = slice(index * half, (index + 1) * half)
             cols = slice(index * width, (index + 1) * width)
-            own = wqkv_in[at, 0:2 * width].astype(F32) * late_in[index].astype(F32)
-            last = wqkv_in[at, 2 * width:].astype(F32) * late_in[2, :, cols].astype(F32)
-            parts.append(jnp.sum(own, axis=1, keepdims=True) + jnp.sum(last, axis=1, keepdims=True))
-        column = jnp.concatenate(parts, axis=0)
+            total = wq_in[at].astype(F32) * late_in[index, :, 0:width].astype(F32)
+            total += wk_in[at].astype(F32) * late_in[index, :, width:].astype(F32)
+            total += wv_in[at].astype(F32) * late_in[2, :, cols].astype(F32)
+            parts.append(jnp.sum(total, axis=1, keepdims=True))
+        sums = jnp.concatenate(parts, axis=0)
         diagonal = (lax.broadcasted_iota(jnp.int32, (width, width), 0)
                     == lax.broadcasted_iota(jnp.int32, (width, width), 1))
-        gain1_ref[...] = jnp.sum(jnp.where(diagonal, column, 0.0), axis=0, keepdims=True) / gain1_in[...]
+        gain1_ref[...] = jnp.sum(jnp.where(diagonal, sums, 0.0), axis=0, keepdims=True) / gain1_in[...]
         for index in range(2):
             at = slice(index * half, (index + 1) * half)
             cols = slice(index * width, (index + 1) * width)
@@ -923,7 +970,7 @@
             dv_ref[at, :] = late_in[2, :, cols].astype(F32)
 
 
-def unpack(word_output, grad_inputs, char_qkv, gain1, sums, width, hidden):
+def unpack(word_output, grad_inputs, weights, gain1, sums, width, hidden):
     steps = 8
     rows = grad_inputs.shape[0]
     words, wide = word_output.shape
@@ -935,13 +982,13 @@
     results = pl.pallas_call(
         unpack_kernel,
         grid=(steps,),
-        in_specs=[split(word_output), split(grad_inputs), whole(char_qkv.shape), whole((1, width))] + [whole(array.shape) for array in sums],
+        in_specs=[split(word_output), split(grad_inputs)] + [whole((width, width))] * 3 + [whole((1, width))] + [whole(array.shape) for array in sums],
         out_specs=[split(word_output), split(grad_inputs)] + [whole(shape) for shape in shapes],
         out_shape=[jax.ShapeDtypeStruct(word_output.shape, BF), jax.ShapeDtypeStruct(grad_inputs.shape, F32)]
         + [jax.ShapeDtypeStruct(shape, F32) for shape in shapes],
         compiler_params=pltpu.CompilerParams(vmem_limit_bytes=60 << 20),
         name="unpack",
-    )(word_output, grad_inputs, char_qkv, gain1[None, :], *sums)
+    )(word_output, grad_inputs, *weights, gain1[None, :], *sums)
     return tuple(array[0] if array.shape[0] == 1 else array for array in results)
 
 
@@ -969,8 +1016,8 @@
     word_up,
     word_down,
 ):
-    char_qkv = jnp.concatenate([char_query, char_key, char_value], axis=1)
-    word_qkv = jnp.concatenate([word_query, word_key, word_value], axis=1)
+    char_qkv = (char_query, char_key, char_value)
+    word_qkv = (word_query, word_key, word_value)
     vec, pooled, *saved, near, qkv_all, out_all, up_all, down_all = char_forward(
         char_inputs, char_counts, char_norm_one, char_qkv, char_out, char_norm_two, char_up, char_down, char_proj,
         word_qkv, word_out_proj, word_up, word_down,

time: 219 us -> 192 us (0.88)
  Pallas kernels: 211 us -> 191 us
  local copies, waits for them, and re-layouts: 6.38 us -> 0 us
    pallas_call x1, Pallas kernels: 97.8 us -> 81.3 us  [char_backward(): pl.pallas_call(functools.partial(char_backward_kernel, slots, bits), grid...]
    another operation x2 -> x0, local copies, waits for them, and re-layouts: 3.19 us -> none  [the longest x1 2.46 us: char_forward(): spread[:, None]]
    broadcast_in_dim x4 -> x0, local copies, waits for them, and re-layouts: 3.04 us -> none  [the longest x1 0.85 us: char_forward(): spread = jnp.repeat(counts, slots)]
    pallas_call x1, Pallas kernels: 58.9 us -> 56 us  [char_forward(): pl.pallas_call(functools.partial(char_forward_kernel, slots), grid=(rows...]
where the time goes in v5:
time: 192 us
  Pallas kernels  191 us (99%)
    pallas_call x1, Pallas kernels, char_backward(): pl.pallas_call(functools.partial(char_backward_kernel, slots, bits), grid...  81.3 us
    pallas_call x1, Pallas kernels, char_forward(): pl.pallas_call(functools.partial(char_forward_kernel, slots), grid=(rows...  56 us
    pallas_call x1, Pallas kernels, word_layer(): pl.pallas_call(functools.partial(word_kernel, bits), in_specs=[vm] * 3 +...  43.5 us
    pallas_call x1, Pallas kernels, unpack(): pl.pallas_call(unpack_kernel, grid=(steps,), in_specs=[split(word_output)...  10.4 us

profile of v5, /device:TPU:0, one launch (start us, length us, event | category | flops | bytes accessed | tf_op | source)
XLA Modules:
  0.0 192.1 jit_solution(843796852860401188)
XLA Ops:
  0.7 56.0 %char_forward.1 = (bf16[256,512]{1,0:T(8,128)(2,1)}, bf16[256,256]{1,0:T(8,128)(2,1)}, bf16[4096,768]{1,0:T(8,128)(2,1)}, bf16[32,2,16,256]{3,2,1,0:T(8,128)(2,1...) custom-call(bf16[4096,256]{1,0:T(8,128)(2,1)} %x_ref.3, ...), custom_call_target="tpu_custom_call" | custom-call | tf_op jit(solution)/shard_map/char_forward/pallas_call | solution.py:470
  56.7 43.5 %word_layer.1 = (bf16[256,512]{1,0:T(8,128)(2,1)}, f32[256,256]{1,0:T(8,128)}, bf16[256,512]{1,0:T(8,128)(2,1)}, f32[8,512]{1,0:T(8,128)}, bf16[4,512,512]{2,1,0...) custom-call(bf16[256,512]{1,0:T(8,128)(2,1)} %get-tuple-element.65.vec_ref, ...), custom_call_target="tpu_custom_call" | custom-call | tf_op jit(solution)/shard_map/word_layer/pallas_call | solution.py:654
  100.2 81.3 %char_backward.1 = (bf16[4096,256]{1,0:T(8,128)(2,1)}, bf16[512,512]{1,0:T(8,128)(2,1)}, bf16[512,512]{1,0:T(8,128)(2,1)}, bf16[512,512]{1,0:T(8,128)(2,1)}, bf1...) custom-call(bf16[4096,256]{1,0:T(8,128)(2,1)} %x_ref.3, s32[1,256]{1,0:T(1,128)} %bitcast.13, ...), custom_call_target="tpu_custom_call" | custom-call | tf_op jit(solution)/shard_map/char_backward/pallas_call | solution.py:876
  181.6 10.4 %unpack.1 = (bf16[256,512]{1,0:T(8,128)(2,1)}, f32[4096,256]{1,0:T(8,128)}, f32[1,256]{1,0:T(1,128)}, f32[256,256]{1,0:T(8,128)}, f32[256,256]{1,0:T(8,128)}, /*...) custom-call(bf16[256,512]{1,0:T(8,128)(2,1)} %get-tuple-element.72.o, ...), custom_call_target="tpu_custom_call" | custom-call | tf_op jit(solution)/shard_map/unpack/pallas_call | solution.py:982

commit v6 on v5

--- a/solution.py
+++ b/solution.py
@@ -372,6 +372,22 @@
                                  (send_sem.at[sem], recv_sem.at[sem]), p.ring_device(offset)))
         return copies
 
+    def send_vec(at):
+        for offset, copy in zip((1, 2), vec_copies(at)):
+            @pl.when(p.rank + offset < RANKS)
+            def _(copy=copy):
+                copy.start()
+
+    def wait_vec(at):
+        for offset, copy in zip((1, 2), vec_copies(at)):
+            @pl.when(p.rank + offset < RANKS)
+            def _(copy=copy):
+                copy.wait_send()
+
+            @pl.when(p.rank >= offset)
+            def _(copy=copy):
+                copy.wait_recv()
+
     @pl.when(step == 0)
     def _():
         join_lanes((lq_ref, lk_ref, lv_ref), lqkv_ref)
@@ -421,8 +437,7 @@
 
     @pl.when(step > 0)
     def _():
-        for copy in vec_copies(step - 1):
-            copy.start()
+        send_vec(step - 1)
 
     first = base + nn(mixed_ref[...], wout_ref[...])
     first_ref[...] = first
@@ -444,15 +459,13 @@
 
     @pl.when(step == steps - 1)
     def _():
-        for copy in vec_copies(step):
-            copy.start()
+        send_vec(step)
         for copy in own_copies:
             copy.wait()
         for gather in gathers:
             gather.wait(3)
         for at in range(CHAR_STEPS):
-            for copy in vec_copies(at):
-                copy.wait()
+            wait_vec(at)
 
 
 def char_forward(x, counts, gain1, weights, wout, gain2, wup, wdown, wproj, local, lout, lup, ldown):
@@ -529,15 +542,26 @@
       *local, lout, lup, ldown)
 
 
-def word_kernel(bits, vec_ref, near_ref, docs_ref, cot_ref, wqkv_ref, wout_ref, wup_ref,
-                wdown_ref, gain1_ref, gain2_ref, wproj_ref, pooled_ref,
-                out_ref, gpl_ref, dproj_ref, dgain_ref, up_grad_ref, down_grad_ref, mix_grad_ref,
+def word_kernel(bits, vec_ref, near_ref, docs_ref, cot_ref, wqkv_in, wout_in, wup_in,
+                wdown_in, gain1_ref, gain2_ref, wproj_ref, pooled_ref,
+                out_ref, gpl_ref, dproj_ref, dgain_ref, up_grad_out, down_grad_out, mix_grad_out,
                 n1_ref, q_ref, kv_ref, probs_ref, o_ref, act_ref, slope_ref, go_ref, gq_ref, gkv_ref,
-                back_ref, cot_own, cot_sem, part_ref, got_ref, table_ref, send_sem, recv_sem):
+                back_ref, cot_own, cot_sem, part_ref, got_ref, table_ref, wqkv_ref, wout_ref, wup_ref, wdown_ref,
+                up_grad_ref, down_grad_ref, mix_grad_ref, io_sem, send_sem, recv_sem):
     p = Place()
     words, wide = vec_ref.shape
     window = 3 * words
     fetch = pltpu.make_async_copy(cot_ref.at[rows_at(p.rank * words, words)], cot_own, cot_sem)
+    loads = [pltpu.make_async_copy(source, target, io_sem.at[index]) for index, (source, target) in enumerate((
+        (wqkv_in, wqkv_ref), (wout_in, wout_ref), (wup_in, wup_ref), (wdown_in, wdown_ref)))]
+    stores = [pltpu.make_async_copy(source, target, io_sem.at[4 + index]) for index, (source, target) in enumerate((
+        (up_grad_ref, up_grad_out), (down_grad_ref, down_grad_out)))]
+
+    def store_mix(rank):
+        return pltpu.make_async_copy(mix_grad_ref.at[rank], mix_grad_out.at[rank], io_sem.at[6 + rank])
+
+    for copy in loads:
+        copy.start()
     fetch.start()
     meet([p.ring_device(offset) for offset in (1, 2, 3)])
 
@@ -551,7 +575,8 @@
     unit1, rate1 = norm_parts(own)
     n1_ref[2 * words:, :] = (unit1 * gain1_ref[...]).astype(BF)
     for slot in range(2):
-        unit, _ = norm_parts(near_ref[slot].astype(F32))
+        near = jnp.where(p.rank + slot >= 2, near_ref[slot].astype(F32), 0.0)
+        unit, _ = norm_parts(near)
         n1_ref[slot * words:(slot + 1) * words, :] = (unit * gain1_ref[...]).astype(BF)
 
     def project(rank, carry):
@@ -573,6 +598,8 @@
         return carry
 
     back_ref[...] = own
+    loads[0].wait()
+    loads[1].wait()
     lax.fori_loop(0, RANKS, project, 0)
     middle = back_ref[...]
     unit2, rate2 = norm_parts(middle)
@@ -585,6 +612,8 @@
         back_ref[...] += nn(act_ref[rank], wdown_ref[rank])
         return carry
 
+    loads[2].wait()
+    loads[3].wait()
     lax.fori_loop(0, RANKS, feed, 0)
     out_ref[...] = back_ref[...].astype(BF)
     fetch.wait()
@@ -598,6 +627,8 @@
         return carry
 
     lax.fori_loop(0, RANKS, feed_back, 0)
+    for copy in stores:
+        copy.start()
     upstream2 = back_ref[...]
     dgain_ref[...] = jnp.zeros_like(dgain_ref)
     dgain_ref[1:2, :] = jnp.sum(upstream2 * unit2, axis=0, keepdims=True)
@@ -625,6 +656,7 @@
         back_ref[...] += nt(gq_ref[...], wqkv_ref[rank, :, 0:TILE])
         mix_grad_ref[rank, :, 0:TILE] = tn(n1_ref[2 * words:, :], gq_ref[...]).astype(BF)
         mix_grad_ref[rank, :, TILE:3 * TILE] = tn(n1_ref[...], gkv_ref[...]).astype(BF)
+        store_mix(rank).start()
         return carry
 
     lax.fori_loop(0, RANKS, attend_back, 0)
@@ -643,6 +675,8 @@
     grad_vec = (grad_middle + norm_back(upstream1, gain1_ref[...], unit1, rate1)).astype(BF)
     dproj_ref[...] = tn(pooled_ref[...], grad_vec).astype(BF)
     gpl_ref[...] = nt(grad_vec, wproj_ref[...])
+    for copy in stores + [store_mix(rank) for rank in range(RANKS)]:
+        copy.wait()
 
 
 def word_layer(bits, vec, near, doc_ids, cotangent, wqkv, wout, wup, wdown, gain1, gain2, wproj, pooled):
@@ -653,8 +687,8 @@
     vm = pl.BlockSpec(memory_space=pltpu.VMEM)
     return pl.pallas_call(
         functools.partial(word_kernel, bits),
-        in_specs=[vm] * 3 + [pl.BlockSpec(memory_space=pl.ANY)] + [vm] * 8,
-        out_specs=[vm] * 7,
+        in_specs=[vm] * 3 + [pl.BlockSpec(memory_space=pl.ANY)] * 5 + [vm] * 4,
+        out_specs=[vm] * 4 + [pl.BlockSpec(memory_space=pl.ANY)] * 3,
         out_shape=[
             jax.ShapeDtypeStruct((words, wide), BF),
             jax.ShapeDtypeStruct((words, width), F32),
@@ -680,6 +714,11 @@
             pltpu.VMEM((2 * words, wide), F32),
             pltpu.VMEM((3, 2, words, wide), BF),
             pltpu.VMEM((1, 2 * words + doc_ids.shape[1]), jnp.int32),
+        ] + [pltpu.VMEM(array.shape, BF) for array in (wqkv, wout, wup, wdown)] + [
+            pltpu.VMEM((RANKS, wide, wide), BF),
+            pltpu.VMEM((RANKS, wide, wide), BF),
+            pltpu.VMEM((RANKS, wide, wide), BF),
+            pltpu.SemaphoreType.DMA((6 + RANKS,)),
             pltpu.SemaphoreType.DMA((2,)),
             pltpu.SemaphoreType.DMA((2,)),
         ],
@@ -922,74 +961,96 @@
       wup, wdown, grad_pooled, act_pool, grad_proj, word_gains, qkv, probs, mixed, first, slope, *word_grads)
 
 
-def unpack_kernel(out_in, dx_in, wq_in, wk_in, wv_in, gain1_in, up_in, down_in, mix_in, early_in, mid_in, late_in,
+def unpack_kernel(out_in, dx_in, wq_in, wk_in, wv_in, gain1_in, up_in, down_in, mix_in, turn_in, early_in, mid_in, late_in,
                   out_ref, dx_ref, gain1_ref, dq_ref, dk_ref, dv_ref, dout_ref, gain2_ref, dup_ref, ddown_ref, dproj_ref,
                   wgain1_ref, wq_ref, wk_ref, wv_ref, wout_ref, wgain2_ref, wup_ref, wdown_ref):
+    step = pl.program_id(0)
     dx_ref[...] = dx_in[...].astype(F32)
     out_ref[...] = out_in[...]
-    width = dout_ref.shape[0]
+    width = dq_ref.shape[0]
     half = width // 2
-
-    @pl.when(pl.program_id(0) == 0)
-    def _():
-        wup_ref[...] = up_in[...].astype(F32)
-        wdown_ref[...] = down_in[...].astype(F32)
-        wq_ref[...] = mix_in[:, 0:TILE].astype(F32)
-        wk_ref[...] = mix_in[:, TILE:2 * TILE].astype(F32)
-        wv_ref[...] = mix_in[:, 2 * TILE:3 * TILE].astype(F32)
-        wout_ref[...] = mix_in[:, 3 * TILE:].astype(F32).T
-        for index in range(RANKS):
-            quarter = early_in.shape[1]
-            ddown_ref[index * quarter:(index + 1) * quarter, :] = early_in[index, :, 0:width].astype(F32)
-            ddown_ref[(RANKS + index) * quarter:(RANKS + index + 1) * quarter, :] = early_in[index, :, width:].astype(F32)
-        dup_ref[:, 0:2 * width] = mid_in[0].astype(F32)
-        dup_ref[:, 2 * width:] = mid_in[1].astype(F32)
-        dproj_ref[...] = mid_in[2].astype(F32)
-        gains = mid_in[3, half:half + 16, :].astype(F32)
+    wup_ref[...] = up_in[...].astype(F32)
+    wdown_ref[...] = down_in[...].astype(F32)
+    wq_ref[...] = mix_in[:, 0:TILE].astype(F32)
+    wk_ref[...] = mix_in[:, TILE:2 * TILE].astype(F32)
+    wv_ref[...] = mix_in[:, 2 * TILE:3 * TILE].astype(F32)
+    for side in range(2):
+        cols = slice(side * width, (side + 1) * width)
+        ddown_ref[side] = early_in[0, :, cols].astype(F32)
+        dup_ref[:, side * 2 * width:(side + 1) * 2 * width] = mid_in[side].astype(F32)
+    dproj_ref[...] = mid_in[2].astype(F32)
+
+    @pl.when(step < UNPACK_STEPS // 2)
+    def _():
+        for side in range(2):
+            dout_ref[side] = mid_in[3, :, side * width:(side + 1) * width].astype(F32)
+
+    @pl.when(step == UNPACK_STEPS // 2)
+    def _():
+        gains = mid_in[3, 0:16, :].astype(F32)
         wgain1_ref[...] = gains[0:1]
         wgain2_ref[...] = gains[1:2]
         gain2_ref[...] = gains[9:10, 0:width]
+
+    @pl.when(step == 0)
+    def _():
+        wout_ref[...] = turn_in[...].astype(F32).T
         parts = []
         for index in range(2):
             at = slice(index * half, (index + 1) * half)
             cols = slice(index * width, (index + 1) * width)
-            total = wq_in[at].astype(F32) * late_in[index, :, 0:width].astype(F32)
-            total += wk_in[at].astype(F32) * late_in[index, :, width:].astype(F32)
-            total += wv_in[at].astype(F32) * late_in[2, :, cols].astype(F32)
+            grads = (late_in[index, :, 0:width].astype(F32), late_in[index, :, width:].astype(F32),
+                     late_in[2, :, cols].astype(F32))
+            total = 0.0
+            for grad, weight, target in zip(grads, (wq_in, wk_in, wv_in), (dq_ref, dk_ref, dv_ref)):
+                target[at, :] = grad
+                total += weight[at].astype(F32) * grad
             parts.append(jnp.sum(total, axis=1, keepdims=True))
         sums = jnp.concatenate(parts, axis=0)
         diagonal = (lax.broadcasted_iota(jnp.int32, (width, width), 0)
                     == lax.broadcasted_iota(jnp.int32, (width, width), 1))
         gain1_ref[...] = jnp.sum(jnp.where(diagonal, sums, 0.0), axis=0, keepdims=True) / gain1_in[...]
-        for index in range(2):
-            at = slice(index * half, (index + 1) * half)
-            cols = slice(index * width, (index + 1) * width)
-            dout_ref[at, :] = mid_in[3, 0:half, cols].astype(F32)
-            dq_ref[at, :] = late_in[index, :, 0:width].astype(F32)
-            dk_ref[at, :] = late_in[index, :, width:].astype(F32)
-            dv_ref[at, :] = late_in[2, :, cols].astype(F32)
+
+
+UNPACK_STEPS = 8
 
 
 def unpack(word_output, grad_inputs, weights, gain1, sums, width, hidden):
-    steps = 8
-    rows = grad_inputs.shape[0]
-    words, wide = word_output.shape
+    steps = UNPACK_STEPS
+    up, down, mix, early, mid, late = sums
+    wide = word_output.shape[1]
     whole = lambda shape: pl.BlockSpec(shape, lambda i: (0,) * len(shape))
-    split = lambda array: pl.BlockSpec((array.shape[0] // steps, array.shape[1]), lambda i: (i, 0))
-    shapes = [(1, width), (width, width), (width, width), (width, width), (width, width), (1, width),
-              (width, hidden), (hidden, width), (width, wide),
-              (1, wide), (wide, TILE), (wide, TILE), (wide, TILE), (TILE, wide), (1, wide), (wide, wide), (wide, wide)]
+    split = lambda shape: pl.BlockSpec((shape[0] // steps, shape[1]), lambda i: (i, 0))
+    middle = lambda shape: pl.BlockSpec((shape[0], shape[1] // steps, shape[2]), lambda i: (0, i, 0))
+    per = early.shape[1] * RANKS // steps
+    blocks = early.shape[1] // per
+    pinned = lambda i: i - (i // (steps // 2)) * (i - (steps // 2 - 1))
+    outs = [
+        (whole, (1, width)), (whole, (width, width)), (whole, (width, width)), (whole, (width, width)),
+        (lambda shape: pl.BlockSpec((2, shape[1] * 2 // steps, width), lambda i: (0, pinned(i), 0)), (2, width // 2, width)),
+        (whole, (1, width)), (split, (width, hidden)), (middle, (2, hidden // 2, width)), (split, (width, wide)),
+        (whole, (1, wide)), (split, (wide, TILE)), (split, (wide, TILE)), (split, (wide, TILE)),
+        (whole, (TILE, wide)), (whole, (1, wide)), (split, (wide, wide)), (split, (wide, wide)),
+    ]
     results = pl.pallas_call(
         unpack_kernel,
         grid=(steps,),
-        in_specs=[split(word_output), split(grad_inputs)] + [whole((width, width))] * 3 + [whole((1, width))] + [whole(array.shape) for array in sums],
-        out_specs=[split(word_output), split(grad_inputs)] + [whole(shape) for shape in shapes],
+        in_specs=[split(word_output.shape), split(grad_inputs.shape)] + [whole((width, width))] * 3 + [whole((1, width))]
+        + [split(up.shape), split(down.shape), split(mix.shape), pl.BlockSpec((wide, TILE), lambda i: (0, 3)),
+           pl.BlockSpec((1, per, wide), lambda i: (i // blocks, i % blocks, 0)), middle(mid.shape), whole(late.shape)],
+        out_specs=[split(word_output.shape), split(grad_inputs.shape)] + [spec(shape) for spec, shape in outs],
         out_shape=[jax.ShapeDtypeStruct(word_output.shape, BF), jax.ShapeDtypeStruct(grad_inputs.shape, F32)]
-        + [jax.ShapeDtypeStruct(shape, F32) for shape in shapes],
+        + [jax.ShapeDtypeStruct(shape, F32) for _, shape in outs],
         compiler_params=pltpu.CompilerParams(vmem_limit_bytes=60 << 20),
         name="unpack",
-    )(word_output, grad_inputs, *weights, gain1[None, :], *sums)
-    return tuple(array[0] if array.shape[0] == 1 else array for array in results)
+    )(word_output, grad_inputs, *weights, gain1[None, :], up, down, mix, mix, early, mid, late)
+
+    def shaped(array):
+        if array.ndim == 3:
+            return array.reshape(-1, array.shape[2])
+        return array[0] if array.shape[0] == 1 else array
+
+    return tuple(shaped(array) for array in results)
 
 
 def per_device(

time: 192 us -> 188 us (0.979)
  Pallas kernels: 191 us -> 187 us
    pallas_call x1, Pallas kernels: 56 us -> 51.5 us  [char_forward(): pl.pallas_call(functools.partial(char_forward_kernel, slots), grid=(rows...]
where the time goes in v6:
time: 188 us; the launch traced here: 187 us
  Pallas kernels  187 us (99%)
    pallas_call x1, Pallas kernels, char_backward(): pl.pallas_call(functools.partial(char_backward_kernel, slots, bits), grid...  82.1 us
    pallas_call x1, Pallas kernels, char_forward(): pl.pallas_call(functools.partial(char_forward_kernel, slots), grid=(rows...  51.5 us
    pallas_call x1, Pallas kernels, word_layer(): pl.pallas_call(functools.partial(word_kernel, bits), in_specs=[vm] * 3 +...  43.3 us
    pallas_call x1, Pallas kernels, unpack(): pl.pallas_call(unpack_kernel, grid=(steps,), in_specs=[split(word_output....  9.68 us

profile of v6, /device:TPU:0, one launch (start us, length us, event | category | flops | bytes accessed | tf_op | source)
XLA Modules:
  0.0 187.4 jit_solution(12049798137702515482)
XLA Ops:
  0.7 51.5 %char_forward.1 = (bf16[256,512]{1,0:T(8,128)(2,1)}, bf16[256,256]{1,0:T(8,128)(2,1)}, bf16[4096,768]{1,0:T(8,128)(2,1)}, bf16[32,2,16,256]{3,2,1,0:T(8,128)(2,1...) custom-call(bf16[4096,256]{1,0:T(8,128)(2,1)} %x_ref.3, ...), custom_call_target="tpu_custom_call" | custom-call | tf_op jit(solution)/shard_map/char_forward/pallas_call | solution.py:483
  52.2 43.3 %word_layer.1 = (bf16[256,512]{1,0:T(8,128)(2,1)}, f32[256,256]{1,0:T(8,128)}, bf16[256,512]{1,0:T(8,128)(2,1)}, f32[8,512]{1,0:T(8,128)}, bf16[4,512,512]{2,1,0...) custom-call(bf16[256,512]{1,0:T(8,128)(2,1)} %get-tuple-element.65.vec_ref, ...), custom_call_target="tpu_custom_call" | custom-call | tf_op jit(solution)/shard_map/word_layer/pallas_call | solution.py:688
  95.5 82.1 %char_backward.1 = (bf16[4096,256]{1,0:T(8,128)(2,1)}, bf16[512,512]{1,0:T(8,128)(2,1)}, bf16[512,512]{1,0:T(8,128)(2,1)}, bf16[512,512]{1,0:T(8,128)(2,1)}, bf1...) custom-call(bf16[4096,256]{1,0:T(8,128)(2,1)} %x_ref.3, s32[1,256]{1,0:T(1,128)} %bitcast.15, ...), custom_call_target="tpu_custom_call" | custom-call | tf_op jit(solution)/shard_map/char_backward/pallas_call | solution.py:915
  177.5 9.7 %unpack.1 = (bf16[256,512]{1,0:T(8,128)(2,1)}, f32[4096,256]{1,0:T(8,128)}, f32[1,256]{1,0:T(1,128)}, f32[256,256]{1,0:T(8,128)}, f32[256,256]{1,0:T(8,128)}, /*...) custom-call(bf16[256,512]{1,0:T(8,128)(2,1)} %get-tuple-element.72.o, ...), custom_call_target="tpu_custom_call" | custom-call | tf_op jit(solution)/shard_map/unpack/pallas_call | solution.py:1035

commit v7 on v6

--- a/solution.py
+++ b/solution.py
@@ -222,74 +222,87 @@
 
 
 class Chain:
-    def __init__(self, place, bits, src, refs, sems, everywhere):
+    def __init__(self, place, bits, src, refs, sems, everywhere, begin=0):
         p = place
         buf, got_core, got_one, got_two, got_more, got_rank, out = refs
-        self.p, self.src, self.everywhere = p, src, everywhere
+        self.p, self.src, self.everywhere, self.begin = p, src, everywhere, begin
         self.buf, self.got_core, self.got_one, self.got_two = buf, got_core, got_one, got_two
-        self.got_more, self.got_rank = got_more, got_rank
-        self.mine = out.at[p.rank] if everywhere else out
-        unit = src.shape[1] // 8
-        lanes = left, right = halves(src.shape[2])
+        self.got_more, self.got_rank, self.out = got_more, got_rank, out
+        unit = buf.shape[1] // 4
+        lanes = halves(buf.shape[2])
         self.lanes = lanes
-        self.own = rows_at(p.core * 4 * unit, 4 * unit)
-        stages = [("core", [remote(src.at[:, rows_at((1 - p.core) * 4 * unit, 4 * unit)], got_core,
-                                   sems.take(), p.core_mate)])]
+        base = p.core * 4 * unit
+        self.own = rows_at(base, 4 * unit)
         first, second = (p.x, p.y), (p.y, p.x)
         first_mate, second_mate = (p.x_mate, p.y_mate), (p.y_mate, p.x_mate)
         one = lambda side, at: rows_at(at * 2 * unit, 2 * unit)
         two = lambda side, at: rows_at((first[side] * 2 + at) * unit, unit)
         self.one_rows = [one(side, first[side]) for side in (0, 1)]
         self.two_rows = [two(side, second[side]) for side in (0, 1)]
-        stages.append(("one", [
-            remote(buf.at[:, one(side, 1 - first[side]), lanes[side]], got_one.at[:, :, lanes[side]],
-                   sems.take(), first_mate[side]) for side in (0, 1)]))
-        stages.append(("two", [
-            remote(buf.at[:, two(side, 1 - second[side]), lanes[side]], got_two.at[:, :, lanes[side]],
-                   sems.take(), second_mate[side]) for side in (0, 1)]))
-        for bit in range(3, bits):
-            stages.append((bit - 3, [
-                remote(buf.at[:, self.two_rows[side], lanes[side]], got_more.at[bit - 3, :, :, lanes[side]],
-                       sems.take(), p.bit_mate(bit)) for side in (0, 1)]))
-        stages.append(("rank", [
-            remote(buf.at[p.ring(offset), self.two_rows[side], lanes[side]],
-                   got_rank.at[offset - 1, :, lanes[side]], sems.take(), p.ring_device(offset))
-            for offset in range(1, RANKS) for side in (0, 1)]))
-        base = p.core * 4 * unit
         self.out_two = [rows_at(base + (first[side] * 2 + second[side]) * unit, unit) for side in (0, 1)]
         out_one = [rows_at(base + first[side] * 2 * unit, 2 * unit) for side in (0, 1)]
+        sides = (0, 1)
+
+        def mine(side):
+            return out.at[p.rank, self.out_two[side], lanes[side]]
+
+        def back(at, part_lanes, mate, sem):
+            part = out.at[:, at, part_lanes] if everywhere else out.at[at, part_lanes]
+            return remote(part, part, sem.take(), mate)
+
+        stages = [
+            ("core", 1, lambda sem: [remote(
+                src.at[:, rows_at((1 - p.core) * 4 * unit, 4 * unit)], got_core, sem.take(), p.core_mate)]),
+            ("one", 2, lambda sem: [remote(
+                buf.at[:, one(side, 1 - first[side]), lanes[side]], got_one.at[:, :, lanes[side]],
+                sem.take(), first_mate[side]) for side in sides]),
+            ("two", 2, lambda sem: [remote(
+                buf.at[:, two(side, 1 - second[side]), lanes[side]], got_two.at[:, :, lanes[side]],
+                sem.take(), second_mate[side]) for side in sides]),
+        ]
+        for bit in range(3, bits):
+            stages.append((bit - 3, 2, lambda sem, bit=bit: [remote(
+                buf.at[:, self.two_rows[side], lanes[side]], got_more.at[bit - 3, :, :, lanes[side]],
+                sem.take(), p.bit_mate(bit)) for side in sides]))
+        pairs = 2 * (RANKS - 1)
+        stages.append(("rank", pairs, lambda sem: [remote(
+            buf.at[p.ring(offset), self.two_rows[side], lanes[side]], got_rank.at[offset - 1, :, lanes[side]],
+            sem.take(), p.ring_device(offset)) for offset in range(1, RANKS) for side in sides]))
         if everywhere:
-            stages.append(("rank_back", [
-                remote(out.at[p.rank, self.out_two[side], lanes[side]], out.at[p.rank, self.out_two[side], lanes[side]],
-                       sems.take(), p.ring_device(offset))
-                for offset in range(1, RANKS) for side in (0, 1)]))
-
-        def back(at, part_lanes, mate):
-            part = out.at[:, at, part_lanes] if everywhere else out.at[at, part_lanes]
-            return remote(part, part, sems.take(), mate)
-
-        stages.append(("back_two", [back(self.out_two[side], lanes[side], second_mate[side]) for side in (0, 1)]))
-        stages.append(("back_one", [back(out_one[side], lanes[side], first_mate[side]) for side in (0, 1)]))
-        stages.append(("back_core", [back(self.own, slice(None), p.core_mate)]))
+            stages.append(("rank_back", pairs, lambda sem: [
+                remote(mine(side), mine(side), sem.take(), p.ring_device(offset))
+                for offset in range(1, RANKS) for side in sides]))
+        stages.append(("back_two", 2, lambda sem: [
+            back(self.out_two[side], lanes[side], second_mate[side], sem) for side in sides]))
+        stages.append(("back_one", 2, lambda sem: [
+            back(out_one[side], lanes[side], first_mate[side], sem) for side in sides]))
+        stages.append(("back_core", 1, lambda sem: [back(self.own, slice(None), p.core_mate, sem)]))
         self.stages = stages
+        self.sems, self.first_sem, at = sems, [], sems.next
+        for _, count, _ in stages:
+            self.first_sem.append(at)
+            at += count
+
+    def copies(self, index):
+        return self.stages[index][2](Sems(self.sems.send, self.sems.recv, self.first_sem[index]))
 
     def fetch(self, sem):
-        return pltpu.make_async_copy(self.src.at[:, self.own], self.buf, sem)
+        source = self.src if self.begin else self.src.at[:, self.own]
+        return pltpu.make_async_copy(source, self.buf, sem)
 
     def start(self, index):
-        for copy in self.stages[index][1]:
+        for copy in self.copies(index):
             copy.start()
 
-    def finish(self, index):
-        name, copies = self.stages[index]
-        for copy in copies:
+    def finish(self, index, staged=False):
+        name = self.stages[index][0]
+        for copy in self.copies(index):
             copy.wait()
         buf = self.buf
         if name == "core":
-            own = self.src if self.everywhere else None
             for quarter in range(RANKS):
-                mine = own[quarter, self.own, :] if self.everywhere else buf[quarter]
-                buf[quarter] = mine + self.got_core[quarter]
+                own = self.src[quarter, self.own, :] if staged or self.everywhere else buf[quarter]
+                buf[quarter] = own + self.got_core[quarter]
         elif name == "one":
             for at, lanes in zip(self.one_rows, self.lanes):
                 for quarter in range(RANKS):
@@ -299,19 +312,20 @@
                 for quarter in range(RANKS):
                     buf[quarter, at, lanes] += self.got_two[quarter, :, lanes]
         elif name == "rank":
+            target = self.out.at[self.p.rank] if self.everywhere else self.out
             for side in (0, 1):
                 at, lanes = self.two_rows[side], self.lanes[side]
                 total = buf[self.p.rank, at, lanes].astype(F32)
                 for k in range(RANKS - 1):
                     total = total + self.got_rank[k, :, lanes].astype(F32)
-                self.mine[self.out_two[side], lanes] = total.astype(BF)
+                target[self.out_two[side], lanes] = total.astype(BF)
         elif isinstance(name, int):
             for at, lanes in zip(self.two_rows, self.lanes):
                 for quarter in range(RANKS):
                     buf[quarter, at, lanes] += self.got_more[name, quarter, :, lanes]
 
     def step(self, index):
-        if index:
+        if index > self.begin:
             self.finish(index - 1)
         if index < len(self.stages):
             self.start(index)
@@ -322,12 +336,13 @@
     return 1 + 2 + 2 + 2 * (bits - 3) + pairs + (pairs if everywhere else 0) + 2 + 2 + 1
 
 
-def chain_scratch(bits, rows, lanes):
+def chain_scratch(bits, rows, lanes, begin=0):
     unit = rows // 8
+    early = 16 if begin else 4 * unit
     return [
         pltpu.VMEM((RANKS, 4 * unit, lanes), BF),
-        pltpu.VMEM((RANKS, 4 * unit, lanes), BF),
-        pltpu.VMEM((RANKS, 2 * unit, lanes), BF),
+        pltpu.VMEM((RANKS, early, lanes), BF),
+        pltpu.VMEM((RANKS, early // 2 if not begin else 16, lanes), BF),
         pltpu.VMEM((RANKS, unit, lanes), BF),
         pltpu.VMEM((max(bits - 3, 1), RANKS, unit, lanes), BF),
         pltpu.VMEM((RANKS - 1, unit, lanes), BF),
@@ -547,7 +562,8 @@
                 out_ref, gpl_ref, dproj_ref, dgain_ref, up_grad_out, down_grad_out, mix_grad_out,
                 n1_ref, q_ref, kv_ref, probs_ref, o_ref, act_ref, slope_ref, go_ref, gq_ref, gkv_ref,
                 back_ref, cot_own, cot_sem, part_ref, got_ref, table_ref, wqkv_ref, wout_ref, wup_ref, wdown_ref,
-                up_grad_ref, down_grad_ref, mix_grad_ref, io_sem, send_sem, recv_sem):
+                up_grad_ref, down_grad_ref, mix_grad_ref, up_buf, up_core, up_one, down_buf, down_core, down_one,
+                io_sem, send_sem, recv_sem):
     p = Place()
     words, wide = vec_ref.shape
     window = 3 * words
@@ -555,15 +571,19 @@
     loads = [pltpu.make_async_copy(source, target, io_sem.at[index]) for index, (source, target) in enumerate((
         (wqkv_in, wqkv_ref), (wout_in, wout_ref), (wup_in, wup_ref), (wdown_in, wdown_ref)))]
     stores = [pltpu.make_async_copy(source, target, io_sem.at[4 + index]) for index, (source, target) in enumerate((
-        (up_grad_ref, up_grad_out), (down_grad_ref, down_grad_out)))]
+        (up_buf, up_grad_out), (down_buf, down_grad_out)))]
 
     def store_mix(rank):
         return pltpu.make_async_copy(mix_grad_ref.at[rank], mix_grad_out.at[rank], io_sem.at[6 + rank])
 
+    up_chain = Chain(p, bits, up_grad_ref, (up_buf, up_core, up_one, None, None, None, None),
+                     Sems(send_sem, recv_sem, 2), False)
+    down_chain = Chain(p, bits, down_grad_ref, (down_buf, down_core, down_one, None, None, None, None),
+                       Sems(send_sem, recv_sem, 5), False)
     for copy in loads:
         copy.start()
     fetch.start()
-    meet([p.ring_device(offset) for offset in (1, 2, 3)])
+    meet(p.mates(3) + [p.ring_device(offset) for offset in (1, 2, 3)])
 
     table_ref[:, 0:2 * words] = jnp.full((1, 2 * words), -1, jnp.int32)
     table_ref[:, 2 * words:] = docs_ref[...]
@@ -610,25 +630,27 @@
         act_ref[rank] = active.astype(BF)
         slope_ref[rank] = slope.astype(BF)
         back_ref[...] += nn(act_ref[rank], wdown_ref[rank])
+        down_grad_ref[rank] = tn(act_ref[rank], cot_own[...]).astype(BF)
         return carry
 
     loads[2].wait()
     loads[3].wait()
+    fetch.wait()
     lax.fori_loop(0, RANKS, feed, 0)
     out_ref[...] = back_ref[...].astype(BF)
-    fetch.wait()
     back_ref[...] = jnp.zeros_like(back_ref)
 
     def feed_back(rank, carry):
         upstream = (nt(cot_own[...], wdown_ref[rank]) * slope_ref[rank].astype(F32)).astype(BF)
         back_ref[...] += nt(upstream, wup_ref[rank])
         up_grad_ref[rank] = tn(normed2, upstream).astype(BF)
-        down_grad_ref[rank] = tn(act_ref[rank], cot_own[...]).astype(BF)
         return carry
 
+    down_chain.start(0)
     lax.fori_loop(0, RANKS, feed_back, 0)
-    for copy in stores:
-        copy.start()
+    up_chain.start(0)
+    down_chain.finish(0, True)
+    down_chain.start(1)
     upstream2 = back_ref[...]
     dgain_ref[...] = jnp.zeros_like(dgain_ref)
     dgain_ref[1:2, :] = jnp.sum(upstream2 * unit2, axis=0, keepdims=True)
@@ -639,6 +661,11 @@
     part_ref[...] = jnp.zeros_like(part_ref)
 
     def attend_back(rank, carry):
+        @pl.when(rank == 2)
+        def _():
+            up_chain.finish(0, True)
+            up_chain.start(1)
+
         go_ref[...] = nt(middle_low, wout_ref[rank]).astype(BF)
         mix_grad_ref[rank, :, 3 * TILE:] = tn(middle_low, o_ref[rank]).astype(BF)
         go_pair = split_heads(go_ref[...])
@@ -670,11 +697,15 @@
         copy.start()
     for copy in sends:
         copy.wait()
+    down_chain.finish(1)
+    stores[1].start()
     upstream1 = back_ref[...] + got_ref[0, 0].astype(F32) + got_ref[1, 0].astype(F32)
     dgain_ref[0:1, :] = jnp.sum(upstream1 * unit1, axis=0, keepdims=True)
     grad_vec = (grad_middle + norm_back(upstream1, gain1_ref[...], unit1, rate1)).astype(BF)
     dproj_ref[...] = tn(pooled_ref[...], grad_vec).astype(BF)
     gpl_ref[...] = nt(grad_vec, wproj_ref[...])
+    up_chain.finish(1)
+    stores[0].start()
     for copy in stores + [store_mix(rank) for rank in range(RANKS)]:
         copy.wait()
 
@@ -695,7 +726,7 @@
             jax.ShapeDtypeStruct((width, wide), BF),
             jax.ShapeDtypeStruct((8, wide), F32),
         ] + [
-            jax.ShapeDtypeStruct((RANKS, wide, wide), BF) for _ in range(3)
+            jax.ShapeDtypeStruct((RANKS, rows, wide), BF) for rows in (wide // 2, wide // 2, wide)
         ],
         scratch_shapes=[
             pltpu.VMEM((window, wide), BF),
@@ -718,9 +749,10 @@
             pltpu.VMEM((RANKS, wide, wide), BF),
             pltpu.VMEM((RANKS, wide, wide), BF),
             pltpu.VMEM((RANKS, wide, wide), BF),
+        ] + [pltpu.VMEM((RANKS, rows, wide), BF) for rows in (wide // 2, wide // 2, wide // 4) * 2] + [
             pltpu.SemaphoreType.DMA((6 + RANKS,)),
-            pltpu.SemaphoreType.DMA((2,)),
-            pltpu.SemaphoreType.DMA((2,)),
+            pltpu.SemaphoreType.DMA((8,)),
+            pltpu.SemaphoreType.DMA((8,)),
         ],
         compiler_params=pltpu.CompilerParams(
             vmem_limit_bytes=62 << 20, collective_id=1, has_side_effects=True),
@@ -730,13 +762,14 @@
 
 
 CHAINS = 6
+BEGIN = (2, 2, 0, 0, 0, 0)
 PLAN = (
-    (0, 2, 7, 10, 14, 16, 20,),
-    (1, 5, 10, 13, 18, 22,),
-    (2, 11, 15, 19,),
-    (1, 4, 9, 12, 15, 19,),
-    (7, 9, 14, 16,),
-    (15, 17, 22,),
+    (0, 3, 8, 10, 12),
+    (0, 4, 10, 13, 15),
+    (0, 2, 7, 10, 14, 16, 20),
+    (0, 3, 7, 10, 15, 19, 22),
+    (7, 9, 12, 14, 18),
+    (15, 17, 21),
 )
 
 
@@ -763,7 +796,8 @@
     for index in range(CHAINS):
         everywhere = index >= word_chains
         refs = tuple(rest[6 * index:6 * index + 6]) + (outs[index],)
-        chains.append(Chain(p, bits, sources[index], refs, Sems(send_sem, recv_sem, first_sem), everywhere))
+        chains.append(Chain(p, bits, sources[index], refs, Sems(send_sem, recv_sem, first_sem), everywhere,
+                            BEGIN[index]))
         first_sem += chain_copies(bits, everywhere)
 
     @pl.when(step == 0)
@@ -865,18 +899,18 @@
         dx_ref[...] = low(spread_ref[here, :] + norm_back(upstream1, gain1_ref[...], unit1, rate1))
 
     for at in range(3 * half_steps):
-        todo = [(index, stages.index(at)) for index, stages in reversed(list(enumerate(PLAN))) if at in stages]
+        todo = [(index, stages.index(at) + BEGIN[index]) for index, stages in reversed(list(enumerate(PLAN))) if at in stages]
         if todo:
             @pl.when(step == at)
             def _(todo=todo):
                 for index, stage in todo:
-                    if stage == 1 and index < word_chains:
+                    if index < word_chains and stage == max(BEGIN[index], 1):
                         chains[index].fetch(own_sem.at[index]).wait()
                     chains[index].step(stage)
 
     @pl.when(step == steps - 1)
     def _():
-        done = [len(stages) for stages in PLAN]
+        done = [begin + len(stages) for begin, stages in zip(BEGIN, PLAN)]
         while any(done[index] <= len(chains[index].stages) for index in range(CHAINS)):
             for index in reversed(range(CHAINS)):
                 if done[index] <= len(chains[index].stages):
@@ -910,8 +944,8 @@
     sources = [(RANKS,) + shape if len(shape) == 2 else shape for shape in sum_shapes]
     copies = sum(chain_copies(bits, index >= 3) for index in range(CHAINS))
     scratch = []
-    for shape in sources:
-        scratch += chain_scratch(bits, shape[1], wide)
+    for begin, shape in zip(BEGIN, sources):
+        scratch += chain_scratch(bits, shape[1], wide, begin)
     return pl.pallas_call(
         functools.partial(char_backward_kernel, slots, bits),
         grid=(3 * CHAR_STEPS,),

time: 188 us -> 192 us (1.021)
  Pallas kernels: 187 us -> 191 us
    pallas_call x1, Pallas kernels: 43.3 us -> 47.1 us  [word_layer(): pl.pallas_call(functools.partial(word_kernel, bits), in_specs=[vm] * 3 +...]
where the time goes in v7:
time: 192 us
  Pallas kernels  191 us (99%)
    pallas_call x1, Pallas kernels, char_backward(): pl.pallas_call(functools.partial(char_backward_kernel, slots, bits), grid...  82.4 us
    pallas_call x1, Pallas kernels, char_forward(): pl.pallas_call(functools.partial(char_forward_kernel, slots), grid=(rows...  51.5 us
    pallas_call x1, Pallas kernels, word_layer(): pl.pallas_call(functools.partial(word_kernel, bits), in_specs=[vm] * 3 +...  47.1 us
    pallas_call x1, Pallas kernels, unpack(): pl.pallas_call(unpack_kernel, grid=(steps,), in_specs=[split(word_output....  9.68 us

profile of v7, /device:TPU:0, one launch (start us, length us, event | category | flops | bytes accessed | tf_op | source)
XLA Modules:
  0.0 191.6 jit_solution(7961408227187742594)
XLA Ops:
  0.7 51.5 %char_forward.1 = (bf16[256,512]{1,0:T(8,128)(2,1)}, bf16[256,256]{1,0:T(8,128)(2,1)}, bf16[4096,768]{1,0:T(8,128)(2,1)}, bf16[32,2,16,256]{3,2,1,0:T(8,128)(2,1...) custom-call(bf16[4096,256]{1,0:T(8,128)(2,1)} %x_ref.3, ...), custom_call_target="tpu_custom_call" | custom-call | tf_op jit(solution)/shard_map/char_forward/pallas_call | solution.py:498
  52.2 47.1 %word_layer.1 = (bf16[256,512]{1,0:T(8,128)(2,1)}, f32[256,256]{1,0:T(8,128)}, bf16[256,512]{1,0:T(8,128)(2,1)}, f32[8,512]{1,0:T(8,128)}, bf16[4,256,512]{2,1,0...) custom-call(bf16[256,512]{1,0:T(8,128)(2,1)} %get-tuple-element.65.vec_ref, ...), custom_call_target="tpu_custom_call" | custom-call | tf_op jit(solution)/shard_map/word_layer/pallas_call | solution.py:719
  99.3 82.4 %char_backward.1 = (bf16[4096,256]{1,0:T(8,128)(2,1)}, bf16[512,512]{1,0:T(8,128)(2,1)}, bf16[512,512]{1,0:T(8,128)(2,1)}, bf16[512,512]{1,0:T(8,128)(2,1)}, bf1...) custom-call(bf16[4096,256]{1,0:T(8,128)(2,1)} %x_ref.3, s32[1,256]{1,0:T(1,128)} %bitcast.15, ...), custom_call_target="tpu_custom_call" | custom-call | tf_op jit(solution)/shard_map/char_backward/pallas_call | solution.py:949
  181.8 9.7 %unpack.1 = (bf16[256,512]{1,0:T(8,128)(2,1)}, f32[4096,256]{1,0:T(8,128)}, f32[1,256]{1,0:T(1,128)}, f32[256,256]{1,0:T(8,128)}, f32[256,256]{1,0:T(8,128)}, /*...) custom-call(bf16[256,512]{1,0:T(8,128)(2,1)} %get-tuple-element.72.o, ...), custom_call_target="tpu_custom_call" | custom-call | tf_op jit(solution)/shard_map/unpack/pallas_call | solution.py:1069

commit v8 on v6

--- a/solution.py
+++ b/solution.py
@@ -348,7 +348,7 @@
                         gain2_ref, wup_ref, wdown_ref, wproj_ref,
                         lq_ref, lk_ref, lv_ref, lout_ref, lup_ref, ldown_ref,
                         vec_ref, pooled_ref, qkv_ref, probs_ref, mixed_ref, first_ref,
-                        slope_ref, act_pool_ref, near_ref, wqkv_all, wout_all, wup_all, wdown_all,
+                        slope_ref, act_pool_ref, normed_ref, near_ref, wqkv_all, wout_all, wup_all, wdown_all,
                         wqkv_ref, lqkv_ref, table_ref, own_sem, send_sem, recv_sem):
     rows = x_ref.shape[0]
     width = x_ref.shape[1]
@@ -402,6 +402,7 @@
     base = x_ref[...].astype(F32)
     unit, _ = norm_parts(base)
     normed = (unit * gain1_ref[...]).astype(BF)
+    normed_ref[...] = normed
     qkv_ref[...] = nn(normed, wqkv_ref[...]).astype(BF)
     mine = table_ref[pl.ds(step, 1), 0:words]
     word_at = lax.broadcasted_iota(jnp.int32, (words, rows), 0)
@@ -511,6 +512,7 @@
             row_block(width),
             row_block(hidden),
             word_block(hidden),
+            row_block(width),
         ] + [pl.BlockSpec(memory_space=pl.ANY)] * 5,
         out_shape=[
             jax.ShapeDtypeStruct((words, wide), BF),
@@ -521,6 +523,7 @@
             jax.ShapeDtypeStruct((rows, width), F32),
             jax.ShapeDtypeStruct((rows, hidden), BF),
             jax.ShapeDtypeStruct((words, hidden), BF),
+            jax.ShapeDtypeStruct((rows, width), BF),
             jax.ShapeDtypeStruct((2, words, wide), BF),
             jax.ShapeDtypeStruct((RANKS, wide, 3 * TILE), BF),
             jax.ShapeDtypeStruct((RANKS,) + lout.shape, BF),
@@ -741,7 +744,7 @@
 
 
 def char_backward_kernel(slots, bits, x_ref, counts_ref, gain1_ref, wq_ref, wk_ref, wv_ref, wout_ref, gain2_ref,
-                         wup_ref, wdown_ref, gpl_ref, act_pool_ref, dproj_ref, wgain_ref, qkv_ref, probs_ref,
+                         wup_ref, wdown_ref, gpl_ref, act_pool_ref, dproj_ref, wgain_ref, normed_ref, qkv_ref, probs_ref,
                          mixed_ref, first_ref, slope_ref, up_grad_ref, down_grad_ref, mix_grad_ref,
                          dx_ref, up_out, down_out, mix_out, early_out, mid_out, late_out,
                          down_ref, gq_ref, gmix_ref, gup_ref, spread_ref, dgain_ref, dqkv_ref, dout_ref, dup_ref,
@@ -846,8 +849,7 @@
                 all_ref[here, c0:c0 + TILE] = tn(stack_lanes(wide_scores), keys).astype(BF)
                 all_ref[here, width + c0:width + c0 + TILE] = nn(wide_scores, queries).astype(BF)
                 all_ref[here, 2 * width + c0:2 * width + c0 + TILE] = nn(wide_probs, grads).astype(BF)
-        unit1, _ = norm_parts(x_ref[...].astype(F32))
-        dqkv_ref[...] += tn((unit1 * gain1_ref[...]).astype(BF), all_ref[rows_at(base, rows), :])
+        dqkv_ref[...] += tn(normed_ref[...], all_ref[rows_at(base, rows), :])
 
     @pl.when(step == 2 * half_steps - 1)
     def _():
@@ -890,7 +892,7 @@
 
 def char_backward(bits, x, counts, gain1, weights, wout, gain2, wup, wdown, grad_pooled, saved, grad_proj,
                   word_gains, word_grads):
-    qkv, probs, mixed, first, slope, act_pool = saved
+    qkv, probs, mixed, first, slope, act_pool, normed = saved
     rows, width = x.shape
     words = counts.shape[0]
     slots = rows // words
@@ -900,7 +902,6 @@
     last = CHAR_STEPS - 1
     ahead = lambda i: i - ((i // CHAR_STEPS + 1) // 2) * (i - last)
     behind = lambda i: (i // CHAR_STEPS % 2) * (i - CHAR_STEPS) + (i // CHAR_STEPS // 2) * last
-    inputs = lambda i: (i % CHAR_STEPS) * ((i // CHAR_STEPS + 1) // 2)
     final = lambda i: (i // CHAR_STEPS // 2) * (i - 2 * CHAR_STEPS)
     ahead_block = lambda cols: pl.BlockSpec((step, cols), lambda i: (ahead(i), 0))
     behind_block = lambda cols: pl.BlockSpec((step, cols), lambda i: (behind(i), 0))
@@ -916,7 +917,7 @@
         functools.partial(char_backward_kernel, slots, bits),
         grid=(3 * CHAR_STEPS,),
         in_specs=[
-            pl.BlockSpec((step, width), lambda i: (inputs(i), 0)),
+            pl.BlockSpec((step, width), lambda i: (final(i), 0)),
             whole((1, words)),
             whole((1, width)),
             whole((width, width)),
@@ -930,6 +931,7 @@
             whole((words, hidden)),
             whole((width, wide)),
             whole((8, wide)),
+            behind_block(width),
             behind_block(3 * width),
             pl.BlockSpec((tiles, CHEADS // 2, slots, 2 * TILE), lambda i: (behind(i), 0, 0, 0)),
             ahead_block(width),
@@ -958,7 +960,7 @@
             vmem_limit_bytes=63 << 20, collective_id=2, has_side_effects=True),
         name="char_backward",
     )(x, counts[None, :], gain1[None, :], *weights, wout, gain2[None, :],
-      wup, wdown, grad_pooled, act_pool, grad_proj, word_gains, qkv, probs, mixed, first, slope, *word_grads)
+      wup, wdown, grad_pooled, act_pool, grad_proj, word_gains, normed, qkv, probs, mixed, first, slope, *word_grads)
 
 
 def unpack_kernel(out_in, dx_in, wq_in, wk_in, wv_in, gain1_in, up_in, down_in, mix_in, turn_in, early_in, mid_in, late_in,

time: 188 us -> 186 us (0.989)
  Pallas kernels: 187 us -> 185 us
where the time goes in v8:
time: 186 us
  Pallas kernels  185 us (99%)
    pallas_call x1, Pallas kernels, char_backward(): pl.pallas_call(functools.partial(char_backward_kernel, slots, bits), grid...  80.5 us
    pallas_call x1, Pallas kernels, char_forward(): pl.pallas_call(functools.partial(char_forward_kernel, slots), grid=(rows...  51.6 us
    pallas_call x1, Pallas kernels, word_layer(): pl.pallas_call(functools.partial(word_kernel, bits), in_specs=[vm] * 3 +...  43.2 us
    pallas_call x1, Pallas kernels, unpack(): pl.pallas_call(unpack_kernel, grid=(steps,), in_specs=[split(word_output....  9.68 us

profile of v8, /device:TPU:0, one launch (start us, length us, event | category | flops | bytes accessed | tf_op | source)
XLA Modules:
  0.0 185.8 jit_solution(3442571662906401860)
XLA Ops:
  0.7 51.6 %char_forward.1 = (bf16[256,512]{1,0:T(8,128)(2,1)}, bf16[256,256]{1,0:T(8,128)(2,1)}, bf16[4096,768]{1,0:T(8,128)(2,1)}, bf16[32,2,16,256]{3,2,1,0:T(8,128)(2,1...) custom-call(bf16[4096,256]{1,0:T(8,128)(2,1)} %x_ref.3, ...), custom_call_target="tpu_custom_call" | custom-call | tf_op jit(solution)/shard_map/char_forward/pallas_call | solution.py:484
  52.2 43.2 %word_layer.1 = (bf16[256,512]{1,0:T(8,128)(2,1)}, f32[256,256]{1,0:T(8,128)}, bf16[256,512]{1,0:T(8,128)(2,1)}, f32[8,512]{1,0:T(8,128)}, bf16[4,512,512]{2,1,0...) custom-call(bf16[256,512]{1,0:T(8,128)(2,1)} %get-tuple-element.66.vec_ref, ...), custom_call_target="tpu_custom_call" | custom-call | tf_op jit(solution)/shard_map/word_layer/pallas_call | solution.py:691
  95.4 80.5 %char_backward.1 = (bf16[4096,256]{1,0:T(8,128)(2,1)}, bf16[512,512]{1,0:T(8,128)(2,1)}, bf16[512,512]{1,0:T(8,128)(2,1)}, bf16[512,512]{1,0:T(8,128)(2,1)}, bf1...) custom-call(bf16[4096,256]{1,0:T(8,128)(2,1)} %x_ref.3, s32[1,256]{1,0:T(1,128)} %bitcast.15, ...), custom_call_target="tpu_custom_call" | custom-call | tf_op jit(solution)/shard_map/char_backward/pallas_call | solution.py:916
  175.9 9.7 %unpack.1 = (bf16[256,512]{1,0:T(8,128)(2,1)}, f32[4096,256]{1,0:T(8,128)}, f32[1,256]{1,0:T(1,128)}, f32[256,256]{1,0:T(8,128)}, f32[256,256]{1,0:T(8,128)}, /*...) custom-call(bf16[256,512]{1,0:T(8,128)(2,1)} %get-tuple-element.73.o, ...), custom_call_target="tpu_custom_call" | custom-call | tf_op jit(solution)/shard_map/unpack/pallas_call | solution.py:1037

commit v9 on v8

--- a/solution.py
+++ b/solution.py
@@ -853,11 +853,10 @@
 
     @pl.when(step == 2 * half_steps - 1)
     def _():
-        half = width // 2
-        for index in range(2):
-            late_ref[index] = low(dqkv_ref[index * half:(index + 1) * half, 0:2 * width])
-            late_ref[2, :, index * width:(index + 1) * width] = low(dqkv_ref[index * half:(index + 1) * half, 2 * width:])
-        late_ref[3] = jnp.zeros_like(late_ref[3])
+        rows_half, lanes_half = width // 2, 3 * width // 2
+        for index in range(RANKS):
+            rows_from, lanes_from = index % 2 * rows_half, index // 2 * lanes_half
+            late_ref[index] = low(dqkv_ref[rows_from:rows_from + rows_half, lanes_from:lanes_from + lanes_half])
 
     @pl.when(step >= 2 * half_steps)
     def _():
@@ -907,12 +906,12 @@
     behind_block = lambda cols: pl.BlockSpec((step, cols), lambda i: (behind(i), 0))
     whole = lambda shape: pl.BlockSpec(shape, lambda i: (0,) * len(shape))
     tiles = step // TILE
-    sum_shapes = [(wide, wide)] * 3 + [(RANKS, width // 2, wide), (RANKS, width, wide), (RANKS, width // 2, wide)]
+    sum_shapes = [(wide, wide)] * 3 + [(RANKS, width // 2, wide), (RANKS, width, wide), (RANKS, width // 2, 3 * width // 2)]
     sources = [(RANKS,) + shape if len(shape) == 2 else shape for shape in sum_shapes]
     copies = sum(chain_copies(bits, index >= 3) for index in range(CHAINS))
     scratch = []
     for shape in sources:
-        scratch += chain_scratch(bits, shape[1], wide)
+        scratch += chain_scratch(bits, shape[1], shape[2])
     return pl.pallas_call(
         functools.partial(char_backward_kernel, slots, bits),
         grid=(3 * CHAR_STEPS,),
@@ -1000,9 +999,8 @@
         parts = []
         for index in range(2):
             at = slice(index * half, (index + 1) * half)
-            cols = slice(index * width, (index + 1) * width)
-            grads = (late_in[index, :, 0:width].astype(F32), late_in[index, :, width:].astype(F32),
-                     late_in[2, :, cols].astype(F32))
+            joined = jnp.concatenate([late_in[index], late_in[2 + index]], axis=1).astype(F32)
+            grads = [joined[:, part * width:(part + 1) * width] for part in range(3)]
             total = 0.0
             for grad, weight, target in zip(grads, (wq_in, wk_in, wv_in), (dq_ref, dk_ref, dv_ref)):
                 target[at, :] = grad

time: 186 us -> 186 us (level)
  no operation moved by 1% of the time
where the time goes in v9:
time: 186 us; the launch traced here: 185 us
  Pallas kernels  185 us (99%)
    pallas_call x1, Pallas kernels, char_backward(): pl.pallas_call(functools.partial(char_backward_kernel, slots, bits), grid...  80.1 us
    pallas_call x1, Pallas kernels, char_forward(): pl.pallas_call(functools.partial(char_forward_kernel, slots), grid=(rows...  51.6 us
    pallas_call x1, Pallas kernels, word_layer(): pl.pallas_call(functools.partial(word_kernel, bits), in_specs=[vm] * 3 +...  43.2 us
    pallas_call x1, Pallas kernels, unpack(): pl.pallas_call(unpack_kernel, grid=(steps,), in_specs=[split(word_output....  9.61 us

profile of v9, /device:TPU:0, one launch (start us, length us, event | category | flops | bytes accessed | tf_op | source)
XLA Modules:
  0.0 185.4 jit_solution(12252697792601581353)
XLA Ops:
  0.7 51.6 %char_forward.1 = (bf16[256,512]{1,0:T(8,128)(2,1)}, bf16[256,256]{1,0:T(8,128)(2,1)}, bf16[4096,768]{1,0:T(8,128)(2,1)}, bf16[32,2,16,256]{3,2,1,0:T(8,128)(2,1...) custom-call(bf16[4096,256]{1,0:T(8,128)(2,1)} %x_ref.3, ...), custom_call_target="tpu_custom_call" | custom-call | tf_op jit(solution)/shard_map/char_forward/pallas_call | solution.py:484
  52.2 43.2 %word_layer.1 = (bf16[256,512]{1,0:T(8,128)(2,1)}, f32[256,256]{1,0:T(8,128)}, bf16[256,512]{1,0:T(8,128)(2,1)}, f32[8,512]{1,0:T(8,128)}, bf16[4,512,512]{2,1,0...) custom-call(bf16[256,512]{1,0:T(8,128)(2,1)} %get-tuple-element.66.vec_ref, ...), custom_call_target="tpu_custom_call" | custom-call | tf_op jit(solution)/shard_map/word_layer/pallas_call | solution.py:691
  95.4 80.1 %char_backward.1 = (bf16[4096,256]{1,0:T(8,128)(2,1)}, bf16[512,512]{1,0:T(8,128)(2,1)}, bf16[512,512]{1,0:T(8,128)(2,1)}, bf16[512,512]{1,0:T(8,128)(2,1)}, bf1...) custom-call(bf16[4096,256]{1,0:T(8,128)(2,1)} %x_ref.3, s32[1,256]{1,0:T(1,128)} %bitcast.15, ...), custom_call_target="tpu_custom_call" | custom-call | tf_op jit(solution)/shard_map/char_backward/pallas_call | solution.py:915
  175.6 9.6 %unpack.1 = (bf16[256,512]{1,0:T(8,128)(2,1)}, f32[4096,256]{1,0:T(8,128)}, f32[1,256]{1,0:T(1,128)}, f32[256,256]{1,0:T(8,128)}, f32[256,256]{1,0:T(8,128)}, /*...) custom-call(bf16[256,512]{1,0:T(8,128)(2,1)} %get-tuple-element.73.o, ...), custom_call_target="tpu_custom_call" | custom-call | tf_op jit(solution)/shard_map/unpack/pallas_call | solution.py:1035

commit v10 on v9

--- a/solution.py
+++ b/solution.py
@@ -650,16 +650,13 @@
         inner = jnp.sum(probs * grad_probs, axis=-1, keepdims=True)
         grad_scores = (probs * (grad_probs - inner) * (CHD ** -0.5)).astype(BF)
         q_pair = split_heads(q_ref[rank])
-        gkv_ref[:, 0:TILE] = tn(grad_scores, q_pair).astype(BF)
-        gkv_ref[:, TILE:] = tn(probs_ref[rank], go_pair).astype(BF)
+        gkv_ref[rank, :, 0:TILE] = tn(grad_scores, q_pair).astype(BF)
+        gkv_ref[rank, :, TILE:] = tn(probs_ref[rank], go_pair).astype(BF)
         pair = jnp.concatenate([grad_scores[0:words], grad_scores[words:]], axis=1)
-        gq_ref[...] = nn(pair, split_heads(kv_ref[rank, :, 0:TILE])).astype(BF)
-        part_ref[...] += nt(gkv_ref[0:2 * words, :], wqkv_ref[rank, :, TILE:])
-        back_ref[...] += nt(gkv_ref[2 * words:, :], wqkv_ref[rank, :, TILE:])
-        back_ref[...] += nt(gq_ref[...], wqkv_ref[rank, :, 0:TILE])
-        mix_grad_ref[rank, :, 0:TILE] = tn(n1_ref[2 * words:, :], gq_ref[...]).astype(BF)
-        mix_grad_ref[rank, :, TILE:3 * TILE] = tn(n1_ref[...], gkv_ref[...]).astype(BF)
-        store_mix(rank).start()
+        gq_ref[rank] = nn(pair, split_heads(kv_ref[rank, :, 0:TILE])).astype(BF)
+        part_ref[...] += nt(gkv_ref[rank, 0:2 * words, :], wqkv_ref[rank, :, TILE:])
+        back_ref[...] += nt(gkv_ref[rank, 2 * words:, :], wqkv_ref[rank, :, TILE:])
+        back_ref[...] += nt(gq_ref[rank], wqkv_ref[rank, :, 0:TILE])
         return carry
 
     lax.fori_loop(0, RANKS, attend_back, 0)
@@ -671,6 +668,14 @@
                             p.ring_device(offset)))
     for copy in sends:
         copy.start()
+
+    def weigh(rank, carry):
+        mix_grad_ref[rank, :, 0:TILE] = tn(n1_ref[2 * words:, :], gq_ref[rank]).astype(BF)
+        mix_grad_ref[rank, :, TILE:3 * TILE] = tn(n1_ref[...], gkv_ref[rank]).astype(BF)
+        store_mix(rank).start()
+        return carry
+
+    lax.fori_loop(0, RANKS, weigh, 0)
     for copy in sends:
         copy.wait()
     upstream1 = back_ref[...] + got_ref[0, 0].astype(F32) + got_ref[1, 0].astype(F32)
@@ -709,8 +714,8 @@
             pltpu.VMEM((RANKS, words, hidden), BF),
             pltpu.VMEM((RANKS, words, hidden), BF),
             pltpu.VMEM((words, TILE), BF),
-            pltpu.VMEM((words, TILE), BF),
-            pltpu.VMEM((window, 2 * TILE), BF),
+            pltpu.VMEM((RANKS, words, TILE), BF),
+            pltpu.VMEM((RANKS, window, 2 * TILE), BF),
             pltpu.VMEM((words, wide), F32),
             pltpu.VMEM((words, wide), BF),
             pltpu.SemaphoreType.DMA,

time: 186 us -> 184 us (0.989)
  Pallas kernels: 185 us -> 183 us
    pallas_call x1, Pallas kernels: 43.2 us -> 41.3 us  [word_layer(): pl.pallas_call(functools.partial(word_kernel, bits), in_specs=[vm] * 3 +...]
where the time goes in v10:
time: 184 us; the launch traced here: 183 us
  Pallas kernels  183 us (99%)
    pallas_call x1, Pallas kernels, char_backward(): pl.pallas_call(functools.partial(char_backward_kernel, slots, bits), grid...  80.2 us
    pallas_call x1, Pallas kernels, char_forward(): pl.pallas_call(functools.partial(char_forward_kernel, slots), grid=(rows...  51.6 us
    pallas_call x1, Pallas kernels, word_layer(): pl.pallas_call(functools.partial(word_kernel, bits), in_specs=[vm] * 3 +...  41.3 us
    pallas_call x1, Pallas kernels, unpack(): pl.pallas_call(unpack_kernel, grid=(steps,), in_specs=[split(word_output....  9.61 us

profile of v10, /device:TPU:0, one launch (start us, length us, event | category | flops | bytes accessed | tf_op | source)
XLA Modules:
  0.0 183.4 jit_solution(10243546655985413645)
XLA Ops:
  0.7 51.6 %char_forward.1 = (bf16[256,512]{1,0:T(8,128)(2,1)}, bf16[256,256]{1,0:T(8,128)(2,1)}, bf16[4096,768]{1,0:T(8,128)(2,1)}, bf16[32,2,16,256]{3,2,1,0:T(8,128)(2,1...) custom-call(bf16[4096,256]{1,0:T(8,128)(2,1)} %x_ref.3, ...), custom_call_target="tpu_custom_call" | custom-call | tf_op jit(solution)/shard_map/char_forward/pallas_call | solution.py:484
  52.2 41.3 %word_layer.1 = (bf16[256,512]{1,0:T(8,128)(2,1)}, f32[256,256]{1,0:T(8,128)}, bf16[256,512]{1,0:T(8,128)(2,1)}, f32[8,512]{1,0:T(8,128)}, bf16[4,512,512]{2,1,0...) custom-call(bf16[256,512]{1,0:T(8,128)(2,1)} %get-tuple-element.66.vec_ref, ...), custom_call_target="tpu_custom_call" | custom-call | tf_op jit(solution)/shard_map/word_layer/pallas_call | solution.py:696
  93.5 80.2 %char_backward.1 = (bf16[4096,256]{1,0:T(8,128)(2,1)}, bf16[512,512]{1,0:T(8,128)(2,1)}, bf16[512,512]{1,0:T(8,128)(2,1)}, bf16[512,512]{1,0:T(8,128)(2,1)}, bf1...) custom-call(bf16[4096,256]{1,0:T(8,128)(2,1)} %x_ref.3, s32[1,256]{1,0:T(1,128)} %bitcast.15, ...), custom_call_target="tpu_custom_call" | custom-call | tf_op jit(solution)/shard_map/char_backward/pallas_call | solution.py:920
  173.7 9.6 %unpack.1 = (bf16[256,512]{1,0:T(8,128)(2,1)}, f32[4096,256]{1,0:T(8,128)}, f32[1,256]{1,0:T(1,128)}, f32[256,256]{1,0:T(8,128)}, f32[256,256]{1,0:T(8,128)}, /*...) custom-call(bf16[256,512]{1,0:T(8,128)(2,1)} %get-tuple-element.73.o, ...), custom_call_target="tpu_custom_call" | custom-call | tf_op jit(solution)/shard_map/unpack/pallas_call | solution.py:1040
